TPU v7x, 512 devices: a whole 4x4x16 slice. The times are simulated.
512 devices in a mesh: ctx: 64 (over x_hi, z, core), head: 8 (over y, x_lo).
Axes of the slice: x: 4 (x_hi: 2, x_lo: 2; x = x_hi * 2 + x_lo), y: 4, z: 16, core: 2. Of those that a mesh axis runs over, the one named last changes fastest.
Arguments:
- queries: bfloat16 [12288, 4096], P('ctx', 'head'), may hold values from -96 to 96
- key_rows: bfloat16 [12288, 4096], P('ctx', 'head'), may hold values from -8 to 8
- value_rows: bfloat16 [12288, 4096], P('ctx', 'head'), may hold values from -6 to 6
- token_rates: float32 [12288, 8], P('ctx', 'head'), may hold values from 0.02 to 1
- fast_one: bfloat16 [8, 512, 512], P('head'), may hold values from -0.25 to 0.25
- fast_three: bfloat16 [8, 512, 512], P('head'), may hold values from -0.25 to 0.25
- fast_two: bfloat16 [8, 512, 512], P('head'), may hold values from -0.25 to 0.25
- head_gain: float32 [8], P('head'), may hold values from 0.5 to 1.5
Outputs:
- window_out: bfloat16 [12288, 4096], P('ctx', 'head')
- fast_out: bfloat16 [12288, 4096], P('ctx', 'head')
All inputs are finite; a program needn't handle non-finite values.
Results may differ from a plain program's by a relative error of at most 0.011.
Values may be sent and summed in bfloat16 or wider, within the bound.
No kernel may reach another device: no remote copies, remote signals or barrier semaphores. Data moves between devices by JAX's collectives and lax.ppermute only.
A program may use at most 64 MiB of HBM per device.

v0:
```python
import jax
import jax.numpy as jnp
from jax import lax
from jax.sharding import PartitionSpec as P

HEADS = 8
HD = 512
WINDOW = 1024
NS_STEPS = 2


COEF_A = 3.4445
COEF_B = -4.775
COEF_C = 2.0315
EPSILON = 1e-06


def passed_along(x, axis, by):
    peers = lax.axis_size(axis)
    pairs = [(i, i + by) for i in range(peers) if 0 <= i + by < peers]
    return lax.ppermute(x, axis, pairs)


def rms_heads(block):
    return block / jnp.sqrt(jnp.mean(block * block, axis=-1, keepdims=True) + EPSILON)


def window_attention(split_q, split_k, split_v):
    tokens_here = split_q.shape[0]
    span = (WINDOW + tokens_here - 2) // tokens_here
    paired = jnp.stack([split_k, split_v])
    earlier = []
    for distance in range(span, 0, -1):
        earlier.append(passed_along(paired, "ctx", distance))
    window_pairs = jnp.concatenate(earlier + [paired], axis=1)
    key_count = window_pairs.shape[1]
    scores = jnp.einsum(
        "qhd,khd->hqk", split_q, window_pairs[0], preferred_element_type=jnp.float32
    ) * split_q.shape[2] ** (-0.5)
    query_pos = lax.broadcasted_iota(jnp.int32, (tokens_here, key_count), 0) + span * tokens_here
    key_pos = lax.broadcasted_iota(jnp.int32, (tokens_here, key_count), 1)
    offset = query_pos - key_pos
    first_key = lax.axis_index("ctx") * tokens_here - span * tokens_here
    allowed = (offset >= 0) & (offset < WINDOW) & (key_pos + first_key >= 0)
    scores = jnp.where(allowed[None], scores, -1e30)
    row_top = jnp.max(scores, axis=-1, keepdims=True)
    exponent = jnp.exp(scores - row_top)
    weights = (exponent / jnp.sum(exponent, axis=-1, keepdims=True)).astype(jnp.bfloat16)
    return jnp.einsum("hqk,khd->qhd", weights, window_pairs[1], preferred_element_type=jnp.float32)


def start_iterate(gradient, squares):
    return lax.optimization_barrier(
        (gradient / (jnp.sqrt(squares)[:, None, None] + 1e-07)).astype(jnp.bfloat16)
    )


def mix_rows(piece_rows, gram_rows, gram_whole, whole_matrix):
    mixer = (
        COEF_B * gram_rows.astype(jnp.float32)
        + COEF_C
        * jnp.einsum("hrs,hst->hrt", gram_rows, gram_whole, preferred_element_type=jnp.float32)
    ).astype(jnp.bfloat16)
    return lax.optimization_barrier(
        (
            COEF_A * piece_rows.astype(jnp.float32)
            + jnp.einsum("hrs,hsc->hrc", mixer, whole_matrix, preferred_element_type=jnp.float32)
        ).astype(jnp.bfloat16)
    )


def gram_of(piece_rows, whole_matrix):
    return lax.optimization_barrier(
        jnp.einsum(
            "hrc,hsc->hrs", piece_rows, whole_matrix, preferred_element_type=jnp.float32
        ).astype(jnp.bfloat16)
    )


def orthogonalize(gradient_one, gradient_three, gradient_two):
    summed = lax.psum((gradient_one, gradient_three, gradient_two), "ctx")
    current = [start_iterate(matrix, jnp.sum(matrix * matrix, axis=(1, 2))) for matrix in summed]
    for sweep_index in range(NS_STEPS):
        updated = []
        for matrix in current:
            gram_full = gram_of(matrix, matrix)
            updated.append(mix_rows(matrix, gram_full, gram_full, matrix))
        current = updated
    return current


def fast_weights(split_q, split_k, split_v, token_rates, fast_one, fast_three, fast_two):
    key_normed = rms_heads(split_k.astype(jnp.float32)).astype(jnp.bfloat16)
    query_normed = rms_heads(split_q.astype(jnp.float32)).astype(jnp.bfloat16)
    hidden_one = jnp.einsum(
        "thd,hdf->thf", key_normed, fast_one, preferred_element_type=jnp.float32
    )
    hidden_three = jnp.einsum(
        "thd,hdf->thf", key_normed, fast_three, preferred_element_type=jnp.float32
    )
    sigmoid_one = jax.nn.sigmoid(hidden_one)
    active = hidden_one * sigmoid_one
    hidden = (active * hidden_three).astype(jnp.bfloat16)
    delta_out = (-token_rates[:, :, None] * split_v.astype(jnp.float32)).astype(jnp.bfloat16)
    delta_hidden = jnp.einsum(
        "thd,hfd->thf", delta_out, fast_two, preferred_element_type=jnp.float32
    )
    delta_three = (delta_hidden * active).astype(jnp.bfloat16)
    delta_one = (
        delta_hidden * hidden_three * sigmoid_one * (1.0 + hidden_one * (1.0 - sigmoid_one))
    ).astype(jnp.bfloat16)
    gradient_one = jnp.einsum(
        "thd,thf->hdf", key_normed, delta_one, preferred_element_type=jnp.float32
    )
    gradient_three = jnp.einsum(
        "thd,thf->hdf", key_normed, delta_three, preferred_element_type=jnp.float32
    )
    gradient_two = jnp.einsum("thf,thd->hfd", hidden, delta_out, preferred_element_type=jnp.float32)
    solved = orthogonalize(gradient_one, gradient_three, gradient_two)
    new_one = (fast_one.astype(jnp.float32) - solved[0].astype(jnp.float32)).astype(jnp.bfloat16)
    new_three = (fast_three.astype(jnp.float32) - solved[1].astype(jnp.float32)).astype(
        jnp.bfloat16
    )
    new_two = (fast_two.astype(jnp.float32) - solved[2].astype(jnp.float32)).astype(jnp.bfloat16)
    query_one = jnp.einsum(
        "thd,hdf->thf", query_normed, new_one, preferred_element_type=jnp.float32
    )
    query_three = jnp.einsum(
        "thd,hdf->thf", query_normed, new_three, preferred_element_type=jnp.float32
    )
    query_hidden = (jax.nn.silu(query_one) * query_three).astype(jnp.bfloat16)
    return jnp.einsum("thf,hfd->thd", query_hidden, new_two, preferred_element_type=jnp.float32)


def local(queries, key_rows, value_rows, token_rates, fast_one, fast_three, fast_two, head_gain):
    tokens_here = queries.shape[0]
    heads_here = fast_one.shape[0]
    width = fast_one.shape[1]
    split_q = queries.reshape(tokens_here, heads_here, width)
    split_k = key_rows.reshape(tokens_here, heads_here, width)
    split_v = value_rows.reshape(tokens_here, heads_here, width)
    attended = window_attention(split_q, split_k, split_v)
    fast = fast_weights(split_q, split_k, split_v, token_rates, fast_one, fast_three, fast_two)
    fast = fast * head_gain[None, :, None]
    totals = lax.psum(
        (jnp.sum(attended * attended, axis=(1, 2)), jnp.sum(fast * fast, axis=(1, 2))), "head"
    )
    full_width = HEADS * HD
    window_out = attended / jnp.sqrt(totals[0] / full_width + EPSILON)[:, None, None]
    fast_out = fast / jnp.sqrt(totals[1] / full_width + EPSILON)[:, None, None]
    return (
        window_out.reshape(tokens_here, heads_here * width).astype(jnp.bfloat16),
        fast_out.reshape(tokens_here, heads_here * width).astype(jnp.bfloat16),
    )


def solution(mesh):
    return jax.shard_map(
        local,
        mesh=mesh,
        in_specs=(
            P("ctx", "head"),
            P("ctx", "head"),
            P("ctx", "head"),
            P("ctx", "head"),
            P("head", None, None),
            P("head", None, None),
            P("head", None, None),
            P("head"),
        ),
        out_specs=(P("ctx", "head"), P("ctx", "head")),
        check_vma=False,
    )
```

profile of v0, /device:TPU:1, one launch (start us, length us, event | category | flops | bytes accessed | tf_op | source)
XLA Modules:
  0.0 606.2 jit_solution(5098626424853706436)
XLA Ops:
  8.4 1.5 convolution_bitcast_fusion.13
  11.3 1.4 convolution_bitcast_fusion
  12.8 1.5 convolution_bitcast_fusion.1
  14.3 1.4 convolution_bitcast_fusion.2
  15.7 7.2 %collective-permute-start = (bf16[2,192,1,512]{3,1,2,0:T(8,128)(2,1)S(1)}, bf16[2,192,1,512]{3,1,2,0:T(8,128)(2,1)S(1)}, u32[]{:S(2)}, u32[]{:S(2)}) collective-permute-start(bf16[2,192,1,512]{3,1,2,0:T(8,128)(2,1)S(1)} %pad_maximum_fusion), channel_id=1, source_target_pairs={{0,48},{8,56},{16,64},{24,72},{32,80},{40,88},{48,96},{56,104},{64... | collective-permute-start | bytes 1179656 | tf_op jit(solution)/shard_map/ppermute | solution.py:21
  23.0 8.3 %collective-permute-start.1 = (bf16[2,192,1,512]{3,1,2,0:T(8,128)(2,1)S(1)}, bf16[2,192,1,512]{3,1,2,0:T(8,128)(2,1)S(1)}, u32[]{:S(2)}, u32[]{:S(2)}) collective-permute-start(bf16[2,192,1,512]{3,1,2,0:T(8,128)(2,1)S(1)} %pad_maximum_fusion), channel_id=1, source_target_pairs={{0,40},{8,48},{16,56},{24,64},{32,72},{40,80},{48,88},{56,96},{64,... | collective-permute-start | bytes 1179656 | tf_op jit(solution)/shard_map/ppermute | solution.py:21
  31.3 6.1 %collective-permute-start.2 = (bf16[2,192,1,512]{3,1,2,0:T(8,128)(2,1)S(1)}, bf16[2,192,1,512]{3,1,2,0:T(8,128)(2,1)S(1)}, u32[]{:S(2)}, u32[]{:S(2)}) collective-permute-start(bf16[2,192,1,512]{3,1,2,0:T(8,128)(2,1)S(1)} %pad_maximum_fusion), channel_id=1, source_target_pairs={{0,32},{8,40},{16,48},{24,56},{32,64},{40,72},{48,80},{56,88},{64,... | collective-permute-start | bytes 1179656 | tf_op jit(solution)/shard_map/ppermute | solution.py:21
  37.4 2.4 collective-permute-start.3
  39.8 2.6 collective-permute-start.4
  43.3 12.9 %collective-permute-start.5 = (bf16[2,192,1,512]{3,1,2,0:T(8,128)(2,1)S(1)}, bf16[2,192,1,512]{3,1,2,0:T(8,128)(2,1)S(1)}, u32[]{:S(2)}, u32[]{:S(2)}) collective-permute-start(bf16[2,192,1,512]{3,1,2,0:T(8,128)(2,1)S(1)} %pad_maximum_fusion), channel_id=1, source_target_pairs={{0,8},{8,16},{16,24},{24,32},{32,40},{40,48},{48,56},{56,64},{64,7... | collective-permute-start | bytes 1179656 | tf_op jit(solution)/shard_map/ppermute | solution.py:21
  56.2 6.0 collective-permute-done.1
  62.3 21.1 %collective-permute-done.2 = bf16[2,192,1,512]{3,1,2,0:T(8,128)(2,1)S(1)} collective-permute-done((bf16[2,192,1,512]{3,1,2,0:T(8,128)(2,1)S(1)}, bf16[2,192,1,512]{3,1,2,0:T(8,128)(2,1)S(1)}, u32[]{:S(2)}, u32[]{:S(2)}) %collective-permute-start.2) | collective-permute-done | bytes 393248 | tf_op jit(solution)/shard_map/ppermute | solution.py:21
  83.5 16.3 %collective-permute-done.3 = bf16[2,192,1,512]{3,1,2,0:T(8,128)(2,1)S(1)} collective-permute-done((bf16[2,192,1,512]{3,1,2,0:T(8,128)(2,1)S(1)}, bf16[2,192,1,512]{3,1,2,0:T(8,128)(2,1)S(1)}, u32[]{:S(2)}, u32[]{:S(2)}) %collective-permute-start.3) | collective-permute-done | bytes 393248 | tf_op jit(solution)/shard_map/ppermute | solution.py:21
  99.8 11.7 %collective-permute-done.4 = bf16[2,192,1,512]{3,1,2,0:T(8,128)(2,1)S(1)} collective-permute-done((bf16[2,192,1,512]{3,1,2,0:T(8,128)(2,1)S(1)}, bf16[2,192,1,512]{3,1,2,0:T(8,128)(2,1)S(1)}, u32[]{:S(2)}, u32[]{:S(2)}) %collective-permute-start.4) | collective-permute-done | bytes 393248 | tf_op jit(solution)/shard_map/ppermute | solution.py:21
  111.5 5.9 collective-permute-done.5
  118.6 1.3 multiply_reduce_fusion.4
  119.9 441.6 %all-reduce.4.cloned.1.call-done = (f32[1,512,512]{2,1,0:T(8,128)}, f32[1,512,512]{2,1,0:T(8,128)}, f32[1,512,512]{2,1,0:T(8,128)}) async-done(((f32[1,512,512]{2,1,0:T(8,128)}, f32[1,512,512]{2,1,0:T(8,128)}, f32[1,512,512]{2,1,0:T(8,128)}), (f32[1,512,512]{2,1,0:T(8,128)}, f32[1,512,512]{2,1,0:T(8,128)}, f32[1,512,512]{2,1,0:T(8,128)})) %all-reduce.4.cloned.1.call-update) | async-done | bytes 3145744 | tf_op jit(solution)/shard_map/psum | solution.py:81
  561.5 2.2 multiply_reduce_fusion.1
  567.6 2.0 fusion.30
  570.0 1.6 fusion.29
  573.3 1.6 fusion.27
  578.3 1.5 fusion.31
  580.9 1.9 multiply_reduce_fusion.3
  582.8 15.0 %all-reduce.1 = (f32[192]{0:T(256)S(1)}, f32[192]{0:T(256)S(1)}) all-reduce(f32[192]{0:T(256)S(1)} %get-tuple-element.9, f32[192]{0:T(256)S(1)} %get-tuple-element.11), channel_id=1, replica_groups=mesh['ctx'=64,'head'=8] {'head'}, use_global_device_ids=true, to_apply=%region_3.4 | all-reduce | flops 384 | bytes 3072 | tf_op jit(solution)/shard_map/psum | solution.py:145
  (67 shorter events, 14.0 us)
Async XLA Ops:
  7.2 2.7 copy-start.4
  7.2 2.7 copy-start.11
  7.2 554.3 %all-reduce.4.cloned.1.call-start = ((), (), s32[]{:S(2)}) async-start(), calls=%async_computation | async-start | bytes 6291456 | tf_op jit(solution)/shard_map/psum | solution.py:81
  9.8 0.7 copy-start.9
  9.9 0.9 copy-start.3
  9.9 1.1 copy-start.5
  15.7 26.8 %copy-start.8 = (bf16[192,512]{1,0:T(8,128)(2,1)S(1)}, bf16[192,512]{1,0:T(8,128)(2,1)}, u32[]{:S(2)}) copy-start(bf16[192,512]{1,0:T(8,128)(2,1)} %param.8) | copy-start | bytes 589828
  15.7 27.5 %collective-permute-start = (bf16[2,192,1,512]{3,1,2,0:T(8,128)(2,1)S(1)}, bf16[2,192,1,512]{3,1,2,0:T(8,128)(2,1)S(1)}, u32[]{:S(2)}, u32[]{:S(2)}) collective-permute-start(bf16[2,192,1,512]{3,1,2,0:T(8,128)(2,1)S(1)} %pad_maximum_fusion), channel_id=1, source_target_pairs={{0,48},{8,56},{16,64},{24,72},{32,80},{40,88},{48,96},{56,104},{64... | collective-permute-start | bytes 1179656 | tf_op jit(solution)/shard_map/ppermute | solution.py:21
  23.0 39.3 %collective-permute-start.1 = (bf16[2,192,1,512]{3,1,2,0:T(8,128)(2,1)S(1)}, bf16[2,192,1,512]{3,1,2,0:T(8,128)(2,1)S(1)}, u32[]{:S(2)}, u32[]{:S(2)}) collective-permute-start(bf16[2,192,1,512]{3,1,2,0:T(8,128)(2,1)S(1)} %pad_maximum_fusion), channel_id=1, source_target_pairs={{0,40},{8,48},{16,56},{24,64},{32,72},{40,80},{48,88},{56,96},{64,... | collective-permute-start | bytes 1179656 | tf_op jit(solution)/shard_map/ppermute | solution.py:21
  31.3 52.1 %collective-permute-start.2 = (bf16[2,192,1,512]{3,1,2,0:T(8,128)(2,1)S(1)}, bf16[2,192,1,512]{3,1,2,0:T(8,128)(2,1)S(1)}, u32[]{:S(2)}, u32[]{:S(2)}) collective-permute-start(bf16[2,192,1,512]{3,1,2,0:T(8,128)(2,1)S(1)} %pad_maximum_fusion), channel_id=1, source_target_pairs={{0,32},{8,40},{16,48},{24,56},{32,64},{40,72},{48,80},{56,88},{64,... | collective-permute-start | bytes 1179656 | tf_op jit(solution)/shard_map/ppermute | solution.py:21
  37.4 62.4 %collective-permute-start.3 = (bf16[2,192,1,512]{3,1,2,0:T(8,128)(2,1)S(1)}, bf16[2,192,1,512]{3,1,2,0:T(8,128)(2,1)S(1)}, u32[]{:S(2)}, u32[]{:S(2)}) collective-permute-start(bf16[2,192,1,512]{3,1,2,0:T(8,128)(2,1)S(1)} %pad_maximum_fusion), channel_id=1, source_target_pairs={{0,24},{8,32},{16,40},{24,48},{32,56},{40,64},{48,72},{56,80},{64,... | collective-permute-start | bytes 1179656 | tf_op jit(solution)/shard_map/ppermute | solution.py:21
  39.8 71.7 %collective-permute-start.4 = (bf16[2,192,1,512]{3,1,2,0:T(8,128)(2,1)S(1)}, bf16[2,192,1,512]{3,1,2,0:T(8,128)(2,1)S(1)}, u32[]{:S(2)}, u32[]{:S(2)}) collective-permute-start(bf16[2,192,1,512]{3,1,2,0:T(8,128)(2,1)S(1)} %pad_maximum_fusion), channel_id=1, source_target_pairs={{0,16},{8,24},{16,32},{24,40},{32,48},{40,56},{48,64},{56,72},{64,... | collective-permute-start | bytes 1179656 | tf_op jit(solution)/shard_map/ppermute | solution.py:21
  43.3 74.2 %collective-permute-start.5 = (bf16[2,192,1,512]{3,1,2,0:T(8,128)(2,1)S(1)}, bf16[2,192,1,512]{3,1,2,0:T(8,128)(2,1)S(1)}, u32[]{:S(2)}, u32[]{:S(2)}) collective-permute-start(bf16[2,192,1,512]{3,1,2,0:T(8,128)(2,1)S(1)} %pad_maximum_fusion), channel_id=1, source_target_pairs={{0,8},{8,16},{16,24},{24,32},{32,40},{40,48},{48,56},{56,64},{64,7... | collective-permute-start | bytes 1179656 | tf_op jit(solution)/shard_map/ppermute | solution.py:21
  561.5 2.9 copy-start.1
  561.5 4.5 copy-start.2
  566.3 0.8 copy-start.6
  573.3 1.6 copy-start
  578.2 1.6 copy-start.10
  578.3 1.6 copy-start.13
  579.8 1.0 copy-start.12
  580.9 17.7 %copy-start.7 = (f32[1,512,192]{1,2,0:T(8,128)S(1)}, f32[1,512,192]{1,2,0:T(8,128)}, u32[]{:S(2)}) copy-start(f32[1,512,192]{1,2,0:T(8,128)} %get-tuple-element.10) | copy-start | bytes 1179652
Sparse Core Ops, SparseCore 0:
  15.8 545.6 all-reduce.3
where the time goes:
time: 609 us; the launch traced here: 606 us
  waiting for transfers between devices  503 us (83%)
  starting transfers between devices  39.6 us (7%)
  matrix products  21.6 us (4%)
  between operations  17.1 us (3%)
  blocking collectives  15 us (2%)
  other arithmetic  7.6 us (1%)
    psum x1, waiting for transfers between devices, orthogonalize(): summed = lax.psum((gradient_one, gradient_three, gradient_two), 'ctx')  442 us
    ppermute x6, waiting for transfers between devices, passed_along(): return lax.ppermute(x, axis, pairs)  61.1 us
    ppermute x6, starting transfers between devices, passed_along(): return lax.ppermute(x, axis, pairs)  39.6 us
    psum x1, blocking collectives, local(): lax.psum((jnp.sum(attended * attended, axis=(1, 2)), jnp.sum(fast * fast,...  15 us
  transfers between devices with their start and end apart: 7, of which 6 were waited for; matrix products, arithmetic and copies ran while one was open for 0% of the time, Pallas kernels for 0%

commit v1 on v0

v1 whole, which is shorter than its diff:
```python
import functools

import jax
import jax.numpy as jnp
from jax import lax
from jax.experimental import pallas as pl
from jax.experimental.pallas import tpu as pltpu
from jax.sharding import Mesh
from jax.sharding import PartitionSpec as P

HEADS = 8
HD = 512
FH = 512
WINDOW = 1024
NS_STEPS = 2
TOK = 192
PART = 128
ROWS = 3 * PART

COEF_A = 3.4445
COEF_B = -4.775
COEF_C = 2.0315
EPSILON = 1e-06

CHIPS = ("xh", "zh", "zl")
RING = ("zh", "zl")
SAME = ("xh", "zh")

NT = (((1,), (1,)), ((), ()))
TN = (((0,), (0,)), ((), ()))


def shifted(x, axes, by):
    count = lax.axis_size(axes)
    return lax.ppermute(x, axes, [(i, (i + by) % count) for i in range(count)])


def nt(a, b):
    return lax.dot_general(a, b, NT, preferred_element_type=jnp.float32)


def nn(a, b):
    return jnp.dot(a, b, preferred_element_type=jnp.float32)


def sigmoid(x):
    return 1.0 / (1.0 + jnp.exp(-x))


def grad_kernel(first, ids_ref, pa_ref, pb_ref, w1_ref, w3_ref, w2_ref, *rest):
    if first:
        (out_ref,) = rest
    else:
        sofar_ref, out_ref = rest
    w13 = jnp.concatenate([w1_ref[...], w3_ref[...]], axis=0)
    w2 = w2_ref[...]
    ones = jnp.ones((8, HD), jnp.bfloat16)
    g13 = None
    g2 = None
    for ref in (pa_ref, pb_ref):
        k = ref[0:TOK, :]
        v = ref[TOK : 2 * TOK, :]
        extra = ref[2 * TOK : 2 * TOK + 16, :].astype(jnp.float32)
        rate = -(extra[0:1, 0:TOK] + extra[1:2, 0:TOK])
        kf = k.astype(jnp.float32)
        squares = nt(ones, (kf * kf).astype(jnp.bfloat16))
        scale = lax.rsqrt(squares[0:1, :] * (1.0 / HD) + EPSILON)
        both = nt(w13, k) * scale
        a = both[:PART]
        b = both[PART:]
        s = sigmoid(a)
        u = a * s
        dh = nt(w2, v) * rate
        hid = (u * b * rate).astype(jnp.bfloat16)
        d1 = (dh * b * s * (1.0 + a * (1.0 - s)) * scale).astype(jnp.bfloat16)
        d3 = (dh * u * scale).astype(jnp.bfloat16)
        p13 = nn(jnp.concatenate([d1, d3], axis=0), k)
        p2 = nn(hid, v)
        g13 = p13 if g13 is None else g13 + p13
        g2 = p2 if g2 is None else g2 + p2
    if first:
        out_ref[0 : 2 * PART, :] = g13
        out_ref[2 * PART : ROWS, :] = g2
    else:
        out_ref[0 : 2 * PART, :] = (g13 + sofar_ref[0 : 2 * PART, :]).astype(jnp.bfloat16)
        out_ref[2 * PART : ROWS, :] = (g2 + sofar_ref[2 * PART : ROWS, :]).astype(jnp.bfloat16)


def gradients(first, ids, pa, pb, w1t, w3t, w2, sofar=None):
    whole = lambda a: pl.BlockSpec(a.shape, lambda i, ids: (0,) * a.ndim)
    mine = pl.BlockSpec((PART, HD), lambda i, ids: (ids[0], 0))
    args = [pa, pb, w1t, w3t, w2]
    specs = [whole(pa), whole(pb), mine, mine, mine]
    if not first:
        args.append(sofar)
        specs.append(whole(sofar))
    return pl.pallas_call(
        functools.partial(grad_kernel, first),
        out_shape=jax.ShapeDtypeStruct((ROWS, HD), jnp.float32 if first else jnp.bfloat16),
        grid_spec=pltpu.PrefetchScalarGridSpec(
            num_scalar_prefetch=1,
            grid=(1,),
            in_specs=specs,
            out_specs=pl.BlockSpec((ROWS, HD), lambda i, ids: (0, 0)),
        ),
        name="grad_first" if first else "grad_second",
    )(ids, *args)


def solve_kernel(ids_ref, gain_ref, q_ref, w1_ref, w3_ref, w2_ref, ga, gb, gc, gd, o_ref, sq_ref):
    slots = (ga, gb, gc, gd)
    fresh = []
    for m, w_ref in enumerate((w1_ref, w3_ref, w2_ref)):
        g = jnp.concatenate([r[m * PART : (m + 1) * PART, :] for r in slots], axis=0).astype(
            jnp.float32
        )
        norm = jnp.sqrt(jnp.sum(g * g, keepdims=True)) + 1e-07
        x = (g / norm).astype(jnp.bfloat16)
        for _ in range(NS_STEPS):
            gram = nt(x, x).astype(jnp.bfloat16)
            mixer = (COEF_B * gram.astype(jnp.float32) + COEF_C * nn(gram, gram)).astype(
                jnp.bfloat16
            )
            x = (COEF_A * x.astype(jnp.float32) + nn(mixer, x)).astype(jnp.bfloat16)
        w = jnp.concatenate(
            [w_ref[pl.ds(pl.multiple_of(ids_ref[i] * PART, PART), PART), :] for i in range(4)],
            axis=0,
        )
        fresh.append((w.astype(jnp.float32) - x.astype(jnp.float32)).astype(jnp.bfloat16))
    q = q_ref[...].astype(jnp.float32)
    qn = (q * lax.rsqrt(jnp.mean(q * q, axis=-1, keepdims=True) + EPSILON)).astype(jnp.bfloat16)
    h1 = nt(qn, fresh[0])
    h3 = nt(qn, fresh[1])
    hidden = (h1 * sigmoid(h1) * h3).astype(jnp.bfloat16)
    o = nn(hidden, fresh[2]) * gain_ref[0]
    o_ref[...] = o
    sq_ref[...] = lax.dot_general(
        jnp.ones((8, HD), jnp.float32), o * o, NT,
        precision=lax.Precision.HIGHEST, preferred_element_type=jnp.float32,
    )


def solve(ids, gain, q, w1t, w3t, w2, slots):
    vmem = pl.BlockSpec(memory_space=pltpu.VMEM)
    smem = pl.BlockSpec(memory_space=pltpu.SMEM)
    return pl.pallas_call(
        solve_kernel,
        out_shape=(
            jax.ShapeDtypeStruct((TOK, HD), jnp.float32),
            jax.ShapeDtypeStruct((8, TOK), jnp.float32),
        ),
        in_specs=[smem, smem] + [vmem] * 8,
        out_specs=(vmem, vmem),
        name="solve",
    )(ids, gain, q, w1t, w3t, w2, *slots)


def window_kernel(info_ref, q_ref, *refs):
    blocks = refs[:8]
    o_ref, sq_ref = refs[8:]
    core = info_ref[0]
    start = info_ref[1]
    places = (
        0, 1 - 2 * core, -2, -1 - 2 * core, -4, -3 - 2 * core, -6, -5 - 2 * core
    )
    q = q_ref[...]
    row = lax.broadcasted_iota(jnp.int32, (TOK, TOK), 0)
    col = lax.broadcasted_iota(jnp.int32, (TOK, TOK), 1)
    scores = []
    for ref, place in zip(blocks, places):
        s = nt(q, ref[0:TOK, :]) * HD ** (-0.5)
        offset = row - col - place * TOK
        allowed = (offset >= 0) & (offset < WINDOW) & (col + (start + place) * TOK >= 0)
        scores.append(jnp.where(allowed, s, -1e30))
    top = functools.reduce(jnp.maximum, scores)
    top = jnp.max(top, axis=-1, keepdims=True)
    weights = [jnp.exp(s - top) for s in scores]
    total = jnp.sum(functools.reduce(jnp.add, weights), axis=-1, keepdims=True)
    inverse = 1.0 / total
    o = None
    for ref, w in zip(blocks, weights):
        part = nn((w * inverse).astype(jnp.bfloat16), ref[TOK : 2 * TOK, :])
        o = part if o is None else o + part
    o_ref[...] = o
    sq_ref[...] = lax.dot_general(
        jnp.ones((8, HD), jnp.float32), o * o, NT,
        precision=lax.Precision.HIGHEST, preferred_element_type=jnp.float32,
    )


def window_attention(info, q, blocks):
    vmem = pl.BlockSpec(memory_space=pltpu.VMEM)
    smem = pl.BlockSpec(memory_space=pltpu.SMEM)
    return pl.pallas_call(
        window_kernel,
        out_shape=(
            jax.ShapeDtypeStruct((TOK, HD), jnp.float32),
            jax.ShapeDtypeStruct((8, TOK), jnp.float32),
        ),
        in_specs=[smem] + [vmem] * 9,
        out_specs=(vmem, vmem),
        name="window",
    )(info, q, *blocks)


def finish_kernel(sums_ref, a_ref, o_ref, wo_ref, fo_ref):
    ones = jnp.ones((HEADS, 128), jnp.float32)
    for which, (src, dst) in enumerate(((a_ref, wo_ref), (o_ref, fo_ref))):
        total = lax.dot_general(
            sums_ref[:, which, :], ones, TN,
            precision=lax.Precision.HIGHEST, preferred_element_type=jnp.float32,
        )[:, 0:1]
        dst[...] = (src[...] * lax.rsqrt(total * (1.0 / (HEADS * HD)) + EPSILON)).astype(
            jnp.bfloat16
        )


def finish(sums, attended, fast):
    vmem = pl.BlockSpec(memory_space=pltpu.VMEM)
    return pl.pallas_call(
        finish_kernel,
        out_shape=(
            jax.ShapeDtypeStruct((TOK, HD), jnp.bfloat16),
            jax.ShapeDtypeStruct((TOK, HD), jnp.bfloat16),
        ),
        in_specs=[vmem] * 3,
        out_specs=(vmem, vmem),
        name="finish",
    )(sums, attended, fast)


def local(queries, key_rows, value_rows, token_rates, fast_one, fast_three, fast_two, head_gain):
    zl = lax.axis_index("zl")
    core = lax.axis_index("core")
    chip = lax.axis_index(CHIPS)
    ids = jnp.stack(
        [zl * 2 + core, zl * 2 + 1 - core, (1 - zl) * 2 + core, (1 - zl) * 2 + 1 - core]
    ).astype(jnp.int32)
    info = jnp.stack([core, chip * 2 + core]).astype(jnp.int32)

    rate = token_rates[:, 0]
    high = lax.reduce_precision(rate, 8, 7)
    extra = jnp.stack([high, rate - high]).astype(jnp.bfloat16)
    extra = jnp.pad(extra, ((0, 14), (0, HD - TOK)))
    own = jnp.concatenate([key_rows, value_rows, extra], axis=0)

    back1 = shifted(own, CHIPS, 1)
    own_x = shifted(own, "core", 1)
    w1t = fast_one[0].T
    w3t = fast_three[0].T
    w2 = fast_two[0]
    sofar = gradients(True, ids, own, own_x, w1t, w3t, w2)
    back1_x = shifted(back1, "core", 1)
    back2 = shifted(back1[: 2 * TOK], CHIPS, 1)
    partial = gradients(False, ids, back1, back1_x, w1t, w3t, w2, sofar)

    pieces = lax.all_to_all(partial.reshape(16, ROWS // 16, HD), SAME, 0, 0)
    piece = jnp.sum(pieces.astype(jnp.float32), axis=0).astype(jnp.bfloat16)

    back2_x = shifted(back2, "core", 1)
    back3 = shifted(back2, CHIPS, 1)
    back3_x = shifted(back3, "core", 1)
    attended, attended_sq = window_attention(
        info, queries, (own, own_x, back1, back1_x, back2, back2_x, back3, back3_x)
    )

    spread = jnp.broadcast_to(piece[None], (16,) + piece.shape)
    mine = lax.all_to_all(spread, SAME, 0, 0).reshape(ROWS, HD)
    mine_x = shifted(mine, "core", 1)
    upper = shifted(mine[ROWS // 2 :], RING, 1)
    lower = shifted(mine[: ROWS // 2], RING, -1)
    other = jnp.concatenate([lower, upper], axis=0)
    other_x = shifted(other, "core", 1)

    fast, fast_sq = solve(
        ids, head_gain, queries, w1t, w3t, w2, (mine, mine_x, other, other_x)
    )
    sums = jnp.concatenate([attended_sq[0:1], fast_sq[0:1]], axis=0)
    sums = lax.all_to_all(jnp.broadcast_to(sums[None], (HEADS,) + sums.shape), "head", 0, 0)
    return finish(sums, attended, fast)


def solution(mesh):
    fine = Mesh(mesh.devices.reshape(2, 8, 2, 2, 8), ("xh", "zh", "zl", "core", "head"))
    ctx = ("xh", "zh", "zl", "core")
    return jax.shard_map(
        local,
        mesh=fine,
        in_specs=(
            P(ctx, "head"),
            P(ctx, "head"),
            P(ctx, "head"),
            P(ctx, "head"),
            P("head", None, None),
            P("head", None, None),
            P("head", None, None),
            P("head"),
        ),
        out_specs=(P(ctx, "head"), P(ctx, "head")),
        check_vma=False,
    )
```

time: 609 us -> 169 us (0.28)
  waiting for transfers between devices: 503 us -> 40.7 us
  blocking collectives: 15 us -> 42.6 us
  Pallas kernels: 0 us -> 24.8 us
  matrix products: 21.6 us -> 0 us
  between operations: 17.1 us -> 1.57 us
  starting transfers between devices: 39.6 us -> 46.1 us
  local copies, waits for them, and re-layouts: 2.56 us -> 8.91 us
    psum x1 -> x0, waiting for transfers between devices: 442 us -> none  [orthogonalize(): summed = lax.psum((gradient_one, gradient_three, gradient_two), 'ctx')]
    all_to_all x0 -> x2, blocking collectives: none -> 42.6 us  [the longest x1 33.4 us: local(): pieces = lax.all_to_all(partial.reshape(16, ROWS // 16, HD), SAME, 0, 0)]
    pallas_call x0 -> x5, Pallas kernels: none -> 24.8 us  [the longest x1 9.95 us: solve(): pl.pallas_call(solve_kernel, out_shape=(jax.ShapeDtypeStruct((TOK, HD), j...]
    dot_general x22 -> x0, matrix products: 21.6 us -> none  [the longest x6 8.12 us: mix_rows(): jnp.einsum('hrs,hsc->hrc', mixer, whole_matrix, preferred_element_type=jn...]
    ppermute x6 -> x11, waiting for transfers between devices: 61.1 us -> 40.7 us  [shifted(): return lax.ppermute(x, axes, [(i, (i + by) % count) for i in range(count)])]
    psum x1 -> x0, blocking collectives: 15 us -> none  [local(): lax.psum((jnp.sum(attended * attended, axis=(1, 2)), jnp.sum(fast * fast,...]
    all_to_all x0 -> x1, starting transfers between devices: none -> 6.75 us  [local(): mine = lax.all_to_all(spread, SAME, 0, 0).reshape(ROWS, HD)]
    ppermute x6 -> x11, starting transfers between devices: 39.6 us -> 39.4 us  [shifted(): return lax.ppermute(x, axes, [(i, (i + by) % count) for i in range(count)])]
  transfers between devices with their start and end apart: 7 -> 12, of which waited for: 6 -> 3; matrix products, arithmetic and copies ran while one was open for 0% -> 2% of each run, Pallas kernels for 0% -> 5%
where the time goes in v1:
time: 169 us; the launch traced here: 168 us
  starting transfers between devices  46.1 us (27%)
  blocking collectives  42.6 us (25%)
  waiting for transfers between devices  40.7 us (24%)
  Pallas kernels  24.8 us (15%)
  local copies, waits for them, and re-layouts  8.91 us (5%)
  other arithmetic  3.08 us (2%)
    ppermute x11, waiting for transfers between devices, shifted(): return lax.ppermute(x, axes, [(i, (i + by) % count) for i in range(count)])  40.7 us
    ppermute x11, starting transfers between devices, shifted(): return lax.ppermute(x, axes, [(i, (i + by) % count) for i in range(count)])  39.4 us
    all_to_all x1, blocking collectives, local(): pieces = lax.all_to_all(partial.reshape(16, ROWS // 16, HD), SAME, 0, 0)  33.4 us
    pallas_call x1, Pallas kernels, solve(): pl.pallas_call(solve_kernel, out_shape=(jax.ShapeDtypeStruct((TOK, HD), j...  9.95 us
    all_to_all x1, blocking collectives, local(): lax.all_to_all(jnp.broadcast_to(sums[None], (HEADS,) + sums.shape), 'head...  9.2 us
    pallas_call x2, Pallas kernels, gradients(): pl.pallas_call(functools.partial(grad_kernel, first), out_shape=jax.Shape...  7.51 us
    all_to_all x1, starting transfers between devices, local(): mine = lax.all_to_all(spread, SAME, 0, 0).reshape(ROWS, HD)  6.75 us
    unnamed x33, local copies, waits for them, and re-layouts  6.66 us
  transfers between devices with their start and end apart: 12, of which 3 were waited for; matrix products, arithmetic and copies ran while one was open for 2% of the time, Pallas kernels for 5%

profile of v1, /device:TPU:1, one launch (start us, length us, event | category | flops | bytes accessed | tf_op | source)
XLA Modules:
  0.0 167.8 jit_solution(17414477515526839869)
XLA Ops:
  1.4 1.1 pad_maximum_fusion.refs_0_.pa_ref
  2.5 4.4 %collective-permute-start.1 = (bf16[400,512]{1,0:T(8,128)(2,1)S(1)}, bf16[400,512]{1,0:T(8,128)(2,1)S(1)}, u32[]{:S(2)}, u32[]{:S(2)}) collective-permute-start(bf16[400,512]{1,0:T(8,128)(2,1)S(1)} %pad_maximum_fusion.refs_0_.pa_ref), channel_id=1, source_target_pairs={{0,16},{16,32},{32,48},{48,64},{64,80},{80,96},{96,112},{112,128},... | collective-permute-start | bytes 1228808 | tf_op jit(solution)/shard_map/ppermute | solution.py:35
  6.8 6.3 %collective-permute-start = (bf16[400,512]{1,0:T(8,128)(2,1)S(1)}, bf16[400,512]{1,0:T(8,128)(2,1)S(1)}, u32[]{:S(2)}, u32[]{:S(2)}) collective-permute-start(bf16[400,512]{1,0:T(8,128)(2,1)S(1)} %pad_maximum_fusion.refs_0_.pa_ref), channel_id=1, source_target_pairs={{0,8},{8,0},{1,9},{9,1},{2,10},{10,2},{3,11},{11,3},{4,12},{12,4},... | collective-permute-start | bytes 1228808 | tf_op jit(solution)/shard_map/ppermute | solution.py:35
  13.1 12.9 %collective-permute-done.1.refs_2_.pa_ref = bf16[400,512]{1,0:T(8,128)(2,1)S(1)} collective-permute-done((bf16[400,512]{1,0:T(8,128)(2,1)S(1)}, bf16[400,512]{1,0:T(8,128)(2,1)S(1)}, u32[]{:S(2)}, u32[]{:S(2)}) %collective-permute-start.1) | collective-permute-done | bytes 409632 | tf_op jit(solution)/shard_map/ppermute | solution.py:35
  26.0 3.1 %collective-permute-start.2 = (bf16[400,512]{1,0:T(8,128)(2,1)S(1)}, bf16[400,512]{1,0:T(8,128)(2,1)S(1)}, u32[]{:S(2)}, u32[]{:S(2)}) collective-permute-start(bf16[400,512]{1,0:T(8,128)(2,1)S(1)} %collective-permute-done.1.refs_2_.pa_ref), channel_id=1, source_target_pairs={{0,8},{8,0},{1,9},{9,1},{2,10},{10,2},{3,11},{11,3},{4,12},{12,4},... | collective-permute-start | bytes 1228808 | tf_op jit(solution)/shard_map/ppermute | solution.py:35
  29.2 1.0 copy.10
  32.6 3.7 %grad_first.1.rest_0_ = f32[384,512]{1,0:T(8,128)} custom-call(s32[4]{0:T(128)} %pad_add_fusion.1.ids_ref, bf16[400,512]{1,0:T(8,128)(2,1)} %copy-done, bf16[400,512]{1,0:T(8,128)(2,1)} %copy-done.4, bf16[512,512]{1,0:T(8,128)(2,1)} %bitcast.20, bf16[512,512]{1,0:T(8,128)(2,1)} %bitcast.23, bf16[512,512]{1,0:T(8,128)(2,1)} %bitcast.26), custom_call_target="tpu_custom_call" | custom-call | tf_op jit(solution)/shard_map/grad_first/pallas_call | solution.py:97
  37.1 3.8 %grad_second.1 = bf16[384,512]{1,0:T(8,128)(2,1)} custom-call(s32[4]{0:T(128)} %pad_add_fusion.1.ids_ref, bf16[400,512]{1,0:T(8,128)(2,1)} %copy-done.1, bf16[400,512]{1,0:T(8,128)(2,1)} %copy-done.5, bf16[512,512]{1,0:T(8,128)(2,1)} %bitcast.21, bf16[512,512]{1,0:T(8,128)(2,1)} %bitcast.24, bf16[512,512]{1,0:T(8,128)(2,1)} %bitcast.27, ...), custom_call_target="tpu_custom_call" | custom-call | tf_op jit(solution)/shard_map/grad_second/pallas_call | solution.py:97
  40.9 33.4 %all_to_all.15 = bf16[16,24,512]{2,1,0:T(8,128)(2,1)S(1)} all-to-all(bf16[16,24,512]{2,1,0:T(8,128)(2,1)} %bitcast.31), channel_id=1, replica_groups=mesh['xh'=2,'zh'=8,'zl'=2,'core'=2,'head'=8] {'xh','zh'}, dimensions={0} | all-to-all | bytes 786432 | tf_op jit(solution)/shard_map/all_to_all | solution.py:257
  75.1 6.8 %all-to-all-start.1 = ((bf16[16,24,512]{2,1,0:T(8,128)(2,1)}), bf16[16,24,512]{2,1,0:T(8,128)(2,1)S(1)}, u32[]{:S(2)}, u32[]{:S(2)}) async-start(bf16[16,24,512]{2,1,0:T(8,128)(2,1)} %broadcast_in_dim.4), calls=%async_computation.1 | async-start | bytes 786432 | tf_op jit(solution)/shard_map/all_to_all | solution.py:268
  81.9 1.9 %collective-permute-start.3 = (bf16[384,512]{1,0:T(8,128)(2,1)S(1)}, bf16[384,512]{1,0:T(8,128)(2,1)S(1)}, u32[]{:S(2)}, u32[]{:S(2)}) collective-permute-start(bf16[384,512]{1,0:T(8,128)(2,1)S(1)} %slice.28), channel_id=1, source_target_pairs={{0,16},{16,32},{32,48},{48,64},{64,80},{80,96},{96,112},{112,128},... | collective-permute-start | bytes 1179656 | tf_op jit(solution)/shard_map/ppermute | solution.py:35
  83.8 26.5 %collective-permute-done.3.refs_4_ = bf16[384,512]{1,0:T(8,128)(2,1)S(1)} collective-permute-done((bf16[384,512]{1,0:T(8,128)(2,1)S(1)}, bf16[384,512]{1,0:T(8,128)(2,1)S(1)}, u32[]{:S(2)}, u32[]{:S(2)}) %collective-permute-start.3) | collective-permute-done | bytes 393248 | tf_op jit(solution)/shard_map/ppermute | solution.py:35
  110.3 1.9 %collective-permute-start.5 = (bf16[384,512]{1,0:T(8,128)(2,1)S(1)}, bf16[384,512]{1,0:T(8,128)(2,1)S(1)}, u32[]{:S(2)}, u32[]{:S(2)}) collective-permute-start(bf16[384,512]{1,0:T(8,128)(2,1)S(1)} %collective-permute-done.3.refs_4_), channel_id=1, source_target_pairs={{0,16},{16,32},{32,48},{48,64},{64,80},{80,96},{96,112},{112,128},... | collective-permute-start | bytes 1179656 | tf_op jit(solution)/shard_map/ppermute | solution.py:35
  112.3 5.1 %collective-permute-start.8 = (bf16[192,512]{1,0:T(8,128)(2,1)S(1)}, bf16[192,512]{1,0:T(8,128)(2,1)S(1)}, u32[]{:S(2)}, u32[]{:S(2)}) collective-permute-start(bf16[192,512]{1,0:T(8,128)(2,1)S(1)} %bitcast.33), channel_id=1, source_target_pairs={{0,240},{16,0},{32,16},{48,32},{64,48},{80,64},{96,80},{112,96},{1... | collective-permute-start | bytes 589832 | tf_op jit(solution)/shard_map/ppermute | solution.py:35
  117.4 1.9 %collective-permute-start.9 = (bf16[192,512]{1,0:T(8,128)(2,1)S(1)}, bf16[192,512]{1,0:T(8,128)(2,1)S(1)}, u32[]{:S(2)}, u32[]{:S(2)}) collective-permute-start(bf16[192,512]{1,0:T(8,128)(2,1)S(1)} %bitcast.32), channel_id=1, source_target_pairs={{0,16},{16,32},{32,48},{48,64},{64,80},{80,96},{96,112},{112,128},... | collective-permute-start | bytes 589832 | tf_op jit(solution)/shard_map/ppermute | solution.py:35
  119.4 3.8 %collective-permute-start.4 = (bf16[384,512]{1,0:T(8,128)(2,1)S(1)}, bf16[384,512]{1,0:T(8,128)(2,1)S(1)}, u32[]{:S(2)}, u32[]{:S(2)}) collective-permute-start(bf16[384,512]{1,0:T(8,128)(2,1)S(1)} %collective-permute-done.3.refs_4_), channel_id=1, source_target_pairs={{0,8},{8,0},{1,9},{9,1},{2,10},{10,2},{3,11},{11,3},{4,12},{12,4},... | collective-permute-start | bytes 1179656 | tf_op jit(solution)/shard_map/ppermute | solution.py:35
  123.2 1.4 collective-permute-done.5.refs_6_
  124.6 6.5 %collective-permute-start.6 = (bf16[384,512]{1,0:T(8,128)(2,1)S(1)}, bf16[384,512]{1,0:T(8,128)(2,1)S(1)}, u32[]{:S(2)}, u32[]{:S(2)}) collective-permute-start(bf16[384,512]{1,0:T(8,128)(2,1)S(1)} %collective-permute-done.5.refs_6_), channel_id=1, source_target_pairs={{0,8},{8,0},{1,9},{9,1},{2,10},{10,2},{3,11},{11,3},{4,12},{12,4},... | collective-permute-start | bytes 1179656 | tf_op jit(solution)/shard_map/ppermute | solution.py:35
  131.1 1.9 %collective-permute-start.7 = (bf16[384,512]{1,0:T(8,128)(2,1)S(1)}, bf16[384,512]{1,0:T(8,128)(2,1)S(1)}, u32[]{:S(2)}, u32[]{:S(2)}) collective-permute-start(bf16[384,512]{1,0:T(8,128)(2,1)S(1)} %bitcast.29), channel_id=1, source_target_pairs={{0,8},{8,0},{1,9},{9,1},{2,10},{10,2},{3,11},{11,3},{4,12},{12,4},... | collective-permute-start | bytes 1179656 | tf_op jit(solution)/shard_map/ppermute | solution.py:35
  133.1 2.4 %collective-permute-start.10 = (bf16[384,512]{1,0:T(8,128)(2,1)S(1)}, bf16[384,512]{1,0:T(8,128)(2,1)S(1)}, u32[]{:S(2)}, u32[]{:S(2)}) collective-permute-start(bf16[384,512]{1,0:T(8,128)(2,1)S(1)} %constant_dynamic-update-slice_fusion.gc), channel_id=1, source_target_pairs={{0,8},{8,0},{1,9},{9,1},{2,10},{10,2},{3,11},{11,3},{4,12},{12,4},... | collective-permute-start | bytes 1179656 | tf_op jit(solution)/shard_map/ppermute | solution.py:35
  138.4 4.9 %window.1 = (f32[192,512]{1,0:T(8,128)}, f32[8,192]{1,0:T(8,128)}) custom-call(s32[2]{0:T(128)} %pad_add_fusion.info_ref, bf16[192,512]{1,0:T(8,128)(2,1)} %q_ref.3, bf16[400,512]{1,0:T(8,128)(2,1)} %copy-done, bf16[400,512]{1,0:T(8,128)(2,1)} %copy-done.4, bf16[400,512]{1,0:T(8,128)(2,1)} %copy-done.1, bf16[400,512]{1,0:T(8,128)(2,1)} %copy-done.5, ...), custom_call_target="tpu_custom_call" | custom-call | tf_op jit(solution)/shard_map/window/pallas_call | solution.py:194
  145.5 9.9 %solve.1 = (f32[192,512]{1,0:T(8,128)}, f32[8,192]{1,0:T(8,128)}) custom-call(s32[4]{0:T(128)} %pad_add_fusion.1.ids_ref, f32[1]{0:T(128)S(6)} %copy.13.gain_ref, bf16[192,512]{1,0:T(8,128)(2,1)} %q_ref.3, bf16[512,512]{1,0:T(8,128)(2,1)} %bitcast.22, bf16[512,512]{1,0:T(8,128)(2,1)} %bitcast.25, bf16[512,512]{1,0:T(8,128)(2,1)} %bitcast.28, ...), custom_call_target="tpu_custom_call" | custom-call | tf_op jit(solution)/shard_map/solve/pallas_call | solution.py:146
  156.2 9.2 %all_to_all.16.sums_ref = f32[8,2,192]{2,1,0:T(2,128)} all-to-all(f32[8,2,192]{2,1,0:T(2,128)S(1)} %broadcast_in_dim.5), channel_id=1, replica_groups=mesh['xh'=2,'zh'=8,'zl'=2,'core'=2,'head'=8] {'head'}, dimensions={0} | all-to-all | bytes 24576 | tf_op jit(solution)/shard_map/all_to_all | solution.py:279
  165.4 2.4 %finish.1 = (bf16[192,512]{1,0:T(8,128)(2,1)}, bf16[192,512]{1,0:T(8,128)(2,1)}) custom-call(f32[8,2,192]{2,1,0:T(2,128)} %all_to_all.16.sums_ref, f32[192,512]{1,0:T(8,128)} %get-tuple-element.8.a_ref, f32[192,512]{1,0:T(8,128)} %get-tuple-element.9.o_ref), custom_call_target="tpu_custom_call" | custom-call | tf_op jit(solution)/shard_map/finish/pallas_call | solution.py:220
  (54 shorter events, 9.9 us)
Async XLA Ops:
  0.6 28.6 %copy-start.7 = (bf16[1,512,512]{2,1,0:T(8,128)(2,1)S(1)}, bf16[1,512,512]{2,1,0:T(8,128)(2,1)}, u32[]{:S(2)}) copy-start(bf16[1,512,512]{2,1,0:T(8,128)(2,1)} %param.12) | copy-start | bytes 1572868
  2.4 27.8 %copy-start = (bf16[400,512]{1,0:T(8,128)(2,1)}, bf16[400,512]{1,0:T(8,128)(2,1)S(1)}, u32[]{:S(2)}) copy-start(bf16[400,512]{1,0:T(8,128)(2,1)S(1)} %pad_maximum_fusion.refs_0_.pa_ref) | copy-start | bytes 1228804
  2.5 23.6 %collective-permute-start.1 = (bf16[400,512]{1,0:T(8,128)(2,1)S(1)}, bf16[400,512]{1,0:T(8,128)(2,1)S(1)}, u32[]{:S(2)}, u32[]{:S(2)}) collective-permute-start(bf16[400,512]{1,0:T(8,128)(2,1)S(1)} %pad_maximum_fusion.refs_0_.pa_ref), channel_id=1, source_target_pairs={{0,16},{16,32},{32,48},{48,64},{64,80},{80,96},{96,112},{112,128},... | collective-permute-start | bytes 1228808 | tf_op jit(solution)/shard_map/ppermute | solution.py:35
  6.8 25.0 %collective-permute-start = (bf16[400,512]{1,0:T(8,128)(2,1)S(1)}, bf16[400,512]{1,0:T(8,128)(2,1)S(1)}, u32[]{:S(2)}, u32[]{:S(2)}) collective-permute-start(bf16[400,512]{1,0:T(8,128)(2,1)S(1)} %pad_maximum_fusion.refs_0_.pa_ref), channel_id=1, source_target_pairs={{0,8},{8,0},{1,9},{9,1},{2,10},{10,2},{3,11},{11,3},{4,12},{12,4},... | collective-permute-start | bytes 1228808 | tf_op jit(solution)/shard_map/ppermute | solution.py:35
  26.0 4.2 %copy-start.1 = (bf16[400,512]{1,0:T(8,128)(2,1)}, bf16[400,512]{1,0:T(8,128)(2,1)S(1)}, u32[]{:S(2)}) copy-start(bf16[400,512]{1,0:T(8,128)(2,1)S(1)} %collective-permute-done.1.refs_2_.pa_ref) | copy-start | bytes 1228804
  26.0 10.3 %collective-permute-start.2 = (bf16[400,512]{1,0:T(8,128)(2,1)S(1)}, bf16[400,512]{1,0:T(8,128)(2,1)S(1)}, u32[]{:S(2)}, u32[]{:S(2)}) collective-permute-start(bf16[400,512]{1,0:T(8,128)(2,1)S(1)} %collective-permute-done.1.refs_2_.pa_ref), channel_id=1, source_target_pairs={{0,8},{8,0},{1,9},{9,1},{2,10},{10,2},{3,11},{11,3},{4,12},{12,4},... | collective-permute-start | bytes 1228808 | tf_op jit(solution)/shard_map/ppermute | solution.py:35
  29.2 1.1 copy-start.8
  31.9 0.8 copy-start.4
  75.1 6.8 %copy-start.2 = (bf16[400,512]{1,0:T(8,128)(2,1)S(1)}, bf16[400,512]{1,0:T(8,128)(2,1)}, u32[]{:S(2)}) copy-start(bf16[400,512]{1,0:T(8,128)(2,1)} %copy-done.1) | copy-start | bytes 1228804
  75.1 37.1 %all-to-all-start.1 = ((bf16[16,24,512]{2,1,0:T(8,128)(2,1)}), bf16[16,24,512]{2,1,0:T(8,128)(2,1)S(1)}, u32[]{:S(2)}, u32[]{:S(2)}) async-start(bf16[16,24,512]{2,1,0:T(8,128)(2,1)} %broadcast_in_dim.4), calls=%async_computation.1 | async-start | bytes 786432 | tf_op jit(solution)/shard_map/all_to_all | solution.py:268
  81.9 28.4 %collective-permute-start.3 = (bf16[384,512]{1,0:T(8,128)(2,1)S(1)}, bf16[384,512]{1,0:T(8,128)(2,1)S(1)}, u32[]{:S(2)}, u32[]{:S(2)}) collective-permute-start(bf16[384,512]{1,0:T(8,128)(2,1)S(1)} %slice.28), channel_id=1, source_target_pairs={{0,16},{16,32},{32,48},{48,64},{64,80},{80,96},{96,112},{112,128},... | collective-permute-start | bytes 1179656 | tf_op jit(solution)/shard_map/ppermute | solution.py:35
  110.3 9.0 %copy-start.11 = (bf16[384,512]{1,0:T(8,128)(2,1)}, bf16[384,512]{1,0:T(8,128)(2,1)S(1)}, u32[]{:S(2)}) copy-start(bf16[384,512]{1,0:T(8,128)(2,1)S(1)} %collective-permute-done.3.refs_4_) | copy-start | bytes 1179652
  110.3 14.2 %collective-permute-start.5 = (bf16[384,512]{1,0:T(8,128)(2,1)S(1)}, bf16[384,512]{1,0:T(8,128)(2,1)S(1)}, u32[]{:S(2)}, u32[]{:S(2)}) collective-permute-start(bf16[384,512]{1,0:T(8,128)(2,1)S(1)} %collective-permute-done.3.refs_4_), channel_id=1, source_target_pairs={{0,16},{16,32},{32,48},{48,64},{64,80},{80,96},{96,112},{112,128},... | collective-permute-start | bytes 1179656 | tf_op jit(solution)/shard_map/ppermute | solution.py:35
  112.2 18.9 %copy-start.3 = (bf16[16,24,512]{2,1,0:T(8,128)(2,1)}, bf16[16,24,512]{2,1,0:T(8,128)(2,1)S(1)}, u32[]{:S(2)}) copy-start(bf16[16,24,512]{2,1,0:T(8,128)(2,1)S(1)} %all-to-all-done.1) | copy-start | bytes 1179652
  112.3 20.8 %collective-permute-start.8 = (bf16[192,512]{1,0:T(8,128)(2,1)S(1)}, bf16[192,512]{1,0:T(8,128)(2,1)S(1)}, u32[]{:S(2)}, u32[]{:S(2)}) collective-permute-start(bf16[192,512]{1,0:T(8,128)(2,1)S(1)} %bitcast.33), channel_id=1, source_target_pairs={{0,240},{16,0},{32,16},{48,32},{64,48},{80,64},{96,80},{112,96},{1... | collective-permute-start | bytes 589832 | tf_op jit(solution)/shard_map/ppermute | solution.py:35
  117.4 15.7 %collective-permute-start.9 = (bf16[192,512]{1,0:T(8,128)(2,1)S(1)}, bf16[192,512]{1,0:T(8,128)(2,1)S(1)}, u32[]{:S(2)}, u32[]{:S(2)}) collective-permute-start(bf16[192,512]{1,0:T(8,128)(2,1)S(1)} %bitcast.32), channel_id=1, source_target_pairs={{0,16},{16,32},{32,48},{48,64},{64,80},{80,96},{96,112},{112,128},... | collective-permute-start | bytes 589832 | tf_op jit(solution)/shard_map/ppermute | solution.py:35
  119.4 17.5 %collective-permute-start.4 = (bf16[384,512]{1,0:T(8,128)(2,1)S(1)}, bf16[384,512]{1,0:T(8,128)(2,1)S(1)}, u32[]{:S(2)}, u32[]{:S(2)}) collective-permute-start(bf16[384,512]{1,0:T(8,128)(2,1)S(1)} %collective-permute-done.3.refs_4_), channel_id=1, source_target_pairs={{0,8},{8,0},{1,9},{9,1},{2,10},{10,2},{3,11},{11,3},{4,12},{12,4},... | collective-permute-start | bytes 1179656 | tf_op jit(solution)/shard_map/ppermute | solution.py:35
  124.6 8.6 %copy-start.12 = (bf16[384,512]{1,0:T(8,128)(2,1)}, bf16[384,512]{1,0:T(8,128)(2,1)S(1)}, u32[]{:S(2)}) copy-start(bf16[384,512]{1,0:T(8,128)(2,1)S(1)} %collective-permute-done.5.refs_6_) | copy-start | bytes 1179652
  124.6 12.3 %collective-permute-start.6 = (bf16[384,512]{1,0:T(8,128)(2,1)S(1)}, bf16[384,512]{1,0:T(8,128)(2,1)S(1)}, u32[]{:S(2)}, u32[]{:S(2)}) collective-permute-start(bf16[384,512]{1,0:T(8,128)(2,1)S(1)} %collective-permute-done.5.refs_6_), channel_id=1, source_target_pairs={{0,8},{8,0},{1,9},{9,1},{2,10},{10,2},{3,11},{11,3},{4,12},{12,4},... | collective-permute-start | bytes 1179656 | tf_op jit(solution)/shard_map/ppermute | solution.py:35
  131.1 12.9 %collective-permute-start.7 = (bf16[384,512]{1,0:T(8,128)(2,1)S(1)}, bf16[384,512]{1,0:T(8,128)(2,1)S(1)}, u32[]{:S(2)}, u32[]{:S(2)}) collective-permute-start(bf16[384,512]{1,0:T(8,128)(2,1)S(1)} %bitcast.29), channel_id=1, source_target_pairs={{0,8},{8,0},{1,9},{9,1},{2,10},{10,2},{3,11},{11,3},{4,12},{12,4},... | collective-permute-start | bytes 1179656 | tf_op jit(solution)/shard_map/ppermute | solution.py:35
  133.1 10.2 %copy-start.6 = (bf16[384,512]{1,0:T(8,128)(2,1)}, bf16[384,512]{1,0:T(8,128)(2,1)S(1)}, u32[]{:S(2)}) copy-start(bf16[384,512]{1,0:T(8,128)(2,1)S(1)} %constant_dynamic-update-slice_fusion.gc) | copy-start | bytes 1179652
  133.1 10.9 %collective-permute-start.10 = (bf16[384,512]{1,0:T(8,128)(2,1)S(1)}, bf16[384,512]{1,0:T(8,128)(2,1)S(1)}, u32[]{:S(2)}, u32[]{:S(2)}) collective-permute-start(bf16[384,512]{1,0:T(8,128)(2,1)S(1)} %constant_dynamic-update-slice_fusion.gc), channel_id=1, source_target_pairs={{0,8},{8,0},{1,9},{9,1},{2,10},{10,2},{3,11},{11,3},{4,12},{12,4},... | collective-permute-start | bytes 1179656 | tf_op jit(solution)/shard_map/ppermute | solution.py:35
  136.8 0.8 copy-start.13
  137.6 0.8 copy-start.14
  (3 other events, 2.3 us)

commit v2 on v1

v2 whole, which is shorter than its diff:
```python
import functools

import jax
import jax.numpy as jnp
from jax import lax
from jax.experimental import pallas as pl
from jax.experimental.pallas import tpu as pltpu
from jax.sharding import Mesh
from jax.sharding import PartitionSpec as P

HEADS = 8
HD = 512
WINDOW = 1024
NS_STEPS = 2
TOK = 192
PART = 128
ROWS = 3 * PART

COEF_A = 3.4445
COEF_B = -4.775
COEF_C = 2.0315
EPSILON = 1e-06

HALF = ROWS // 2
FAR = 128

CHIPS = ("xh", "zq", "zm", "zl")
RING = ("zq", "zm", "zl")
SAME = ("zm", "xh", "zq")
KIN = ("xh", "zq")

NT = (((1,), (1,)), ((), ()))
TN = (((0,), (0,)), ((), ()))


def shifted(x, axes, by):
    count = lax.axis_size(axes)
    return lax.ppermute(x, axes, [(i, (i + by) % count) for i in range(count)])


def exchanged(x, axes):
    return lax.all_to_all(x, axes, 0, 0)


def nt(a, b):
    return lax.dot_general(a, b, NT, preferred_element_type=jnp.float32)


def nn(a, b):
    return jnp.dot(a, b, preferred_element_type=jnp.float32)


def near(x):
    return pltpu.with_memory_space_constraint(x, pltpu.MemorySpace.VMEM)


def near_out(shape, dtype):
    return pltpu.MemorySpace.VMEM(shape, dtype)


def sigmoid(x):
    return 1.0 / (1.0 + jnp.exp(-x))


def grad_kernel(first, ids_ref, pa_ref, pb_ref, w1_ref, w3_ref, w2_ref, *rest):
    if first:
        (out_ref,) = rest
    else:
        sofar_ref, out_ref = rest
    mine = pl.ds(pl.multiple_of(ids_ref[0] * PART, PART), PART)
    w13 = jnp.concatenate([w1_ref[mine, :], w3_ref[mine, :]], axis=0)
    w2 = w2_ref[mine, :]
    ones = jnp.ones((8, HD), jnp.bfloat16)
    g13 = None
    g2 = None
    for ref in (pa_ref, pb_ref):
        k = ref[0:TOK, :]
        v = ref[TOK : 2 * TOK, :]
        extra = ref[2 * TOK : 2 * TOK + 16, :].astype(jnp.float32)
        rate = -(extra[0:1, 0:TOK] + extra[1:2, 0:TOK])
        kf = k.astype(jnp.float32)
        squares = nt(ones, (kf * kf).astype(jnp.bfloat16))
        scale = lax.rsqrt(squares[0:1, :] * (1.0 / HD) + EPSILON)
        both = nt(w13, k) * scale
        a = both[:PART]
        b = both[PART:]
        s = sigmoid(a)
        u = a * s
        dh = nt(w2, v) * rate
        hid = (u * b * rate).astype(jnp.bfloat16)
        d1 = (dh * b * s * (1.0 + a * (1.0 - s)) * scale).astype(jnp.bfloat16)
        d3 = (dh * u * scale).astype(jnp.bfloat16)
        p13 = nn(jnp.concatenate([d1, d3], axis=0), k)
        p2 = nn(hid, v)
        g13 = p13 if g13 is None else g13 + p13
        g2 = p2 if g2 is None else g2 + p2
    if first:
        out_ref[0 : 2 * PART, :] = g13
        out_ref[2 * PART : ROWS, :] = g2
    else:
        out_ref[0 : 2 * PART, :] = (g13 + sofar_ref[0 : 2 * PART, :]).astype(jnp.bfloat16)
        out_ref[2 * PART : ROWS, :] = (g2 + sofar_ref[2 * PART : ROWS, :]).astype(jnp.bfloat16)


VMEM = pl.BlockSpec(memory_space=pltpu.VMEM)
SMEM = pl.BlockSpec(memory_space=pltpu.SMEM)


def gradients(first, ids, *arrays):
    return pl.pallas_call(
        functools.partial(grad_kernel, first),
        out_shape=near_out((ROWS, HD), jnp.float32)
        if first
        else jax.ShapeDtypeStruct((ROWS, HD), jnp.bfloat16),
        in_specs=[SMEM] + [VMEM] * len(arrays),
        out_specs=VMEM,
        compiler_params=pltpu.CompilerParams(vmem_limit_bytes=16 << 20),
        name="grad_first" if first else "grad_second",
    )(ids, *[near(x) for x in arrays])


def solve_kernel(ids_ref, gain_ref, q_ref, w1_ref, w3_ref, w2_ref, g_ref, gx_ref, o_ref, sq_ref):
    low = ids_ref[4] == 0
    near_low = ids_ref[4] == ids_ref[5]
    slots = []
    for first, second, when in ((0, HALF, low), (3 * HALF, 2 * HALF, near_low)):
        for ref in (g_ref, gx_ref):
            a = ref[first : first + HALF, :]
            b = ref[second : second + HALF, :]
            slots.append(
                jnp.concatenate([jnp.where(when, a, b), jnp.where(when, b, a)], axis=0)
            )
    fresh = []
    for m, w_ref in enumerate((w1_ref, w3_ref, w2_ref)):
        g = jnp.concatenate([r[m * PART : (m + 1) * PART, :] for r in slots], axis=0).astype(
            jnp.float32
        )
        norm = jnp.sqrt(jnp.sum(g * g, keepdims=True)) + 1e-07
        x = (g / norm).astype(jnp.bfloat16)
        for _ in range(NS_STEPS):
            gram = nt(x, x).astype(jnp.bfloat16)
            mixer = (COEF_B * gram.astype(jnp.float32) + COEF_C * nn(gram, gram)).astype(
                jnp.bfloat16
            )
            x = (COEF_A * x.astype(jnp.float32) + nn(mixer, x)).astype(jnp.bfloat16)
        w = jnp.concatenate(
            [w_ref[pl.ds(pl.multiple_of(ids_ref[i] * PART, PART), PART), :] for i in range(4)],
            axis=0,
        )
        fresh.append((w.astype(jnp.float32) - x.astype(jnp.float32)).astype(jnp.bfloat16))
    q = q_ref[...].astype(jnp.float32)
    qn = (q * lax.rsqrt(jnp.mean(q * q, axis=-1, keepdims=True) + EPSILON)).astype(jnp.bfloat16)
    h1 = nt(qn, fresh[0])
    h3 = nt(qn, fresh[1])
    hidden = (h1 * sigmoid(h1) * h3).astype(jnp.bfloat16)
    o = nn(hidden, fresh[2]) * gain_ref[0]
    o_ref[...] = o
    sq_ref[...] = lax.dot_general(
        jnp.ones((8, HD), jnp.float32), o * o, NT,
        precision=lax.Precision.HIGHEST, preferred_element_type=jnp.float32,
    )


def solve(ids, gain, *arrays):
    return pl.pallas_call(
        solve_kernel,
        out_shape=(near_out((TOK, HD), jnp.float32), near_out((8, TOK), jnp.float32)),
        in_specs=[SMEM, SMEM] + [VMEM] * len(arrays),
        out_specs=(VMEM, VMEM),
        compiler_params=pltpu.CompilerParams(vmem_limit_bytes=28 << 20),
        name="solve",
    )(ids, gain, *[near(x) for x in arrays])


def window_kernel(info_ref, q_ref, *refs):
    blocks = refs[:8]
    o_ref, sq_ref = refs[8:]
    core = info_ref[0]
    start = info_ref[1]
    places = (
        (TOK, 0),
        (TOK, TOK * (1 - 2 * core)),
        (TOK, -2 * TOK),
        (TOK, -TOK * (1 + 2 * core)),
        (TOK, -4 * TOK),
        (TOK, -TOK * (3 + 2 * core)),
        (FAR, -WINDOW + (FAR - TOK) * core),
        (FAR, -WINDOW + FAR - (FAR + TOK) * core),
    )
    q = q_ref[...]
    scores = []
    top = None
    for ref, (count, place) in zip(blocks, places):
        row = lax.broadcasted_iota(jnp.int32, (TOK, count), 0)
        col = lax.broadcasted_iota(jnp.int32, (TOK, count), 1)
        s = nt(q, ref[0:count, :]) * HD ** (-0.5)
        offset = row - col - place
        allowed = (offset >= 0) & (offset < WINDOW) & (col + (start * TOK + place) >= 0)
        s = jnp.where(allowed, s, -1e30)
        scores.append(s)
        here = jnp.max(s, axis=-1, keepdims=True)
        top = here if top is None else jnp.maximum(top, here)
    weights = [jnp.exp(s - top) for s in scores]
    total = functools.reduce(jnp.add, [jnp.sum(w, axis=-1, keepdims=True) for w in weights])
    inverse = 1.0 / total
    o = None
    for ref, w, (count, _) in zip(blocks, weights, places):
        part = nn((w * inverse).astype(jnp.bfloat16), ref[count : 2 * count, :])
        o = part if o is None else o + part
    o_ref[...] = o
    sq_ref[...] = lax.dot_general(
        jnp.ones((8, HD), jnp.float32), o * o, NT,
        precision=lax.Precision.HIGHEST, preferred_element_type=jnp.float32,
    )


def window_attention(info, *arrays):
    return pl.pallas_call(
        window_kernel,
        out_shape=(near_out((TOK, HD), jnp.float32), near_out((8, TOK), jnp.float32)),
        in_specs=[SMEM] + [VMEM] * len(arrays),
        out_specs=(VMEM, VMEM),
        compiler_params=pltpu.CompilerParams(vmem_limit_bytes=24 << 20),
        name="window",
    )(info, *[near(x) for x in arrays])


def finish_kernel(sums_ref, a_ref, o_ref, wo_ref, fo_ref):
    ones = jnp.ones((HEADS, 128), jnp.float32)
    for which, (src, dst) in enumerate(((a_ref, wo_ref), (o_ref, fo_ref))):
        total = lax.dot_general(
            sums_ref[:, which, :], ones, TN,
            precision=lax.Precision.HIGHEST, preferred_element_type=jnp.float32,
        )[:, 0:1]
        dst[...] = (src[...] * lax.rsqrt(total * (1.0 / (HEADS * HD)) + EPSILON)).astype(
            jnp.bfloat16
        )


def finish(*arrays):
    return pl.pallas_call(
        finish_kernel,
        out_shape=(
            jax.ShapeDtypeStruct((TOK, HD), jnp.bfloat16),
            jax.ShapeDtypeStruct((TOK, HD), jnp.bfloat16),
        ),
        in_specs=[VMEM] * 3,
        out_specs=(VMEM, VMEM),
        compiler_params=pltpu.CompilerParams(vmem_limit_bytes=8 << 20),
        name="finish",
    )(*[near(x) for x in arrays])


def local(queries, key_rows, value_rows, token_rates, fast_one, fast_three, fast_two, head_gain):
    zl = lax.axis_index("zl")
    zm = lax.axis_index("zm")
    core = lax.axis_index("core")
    chip = lax.axis_index(CHIPS)
    ids = jnp.stack(
        [zl * 2 + core, zl * 2 + 1 - core, 2 - 2 * zl + core, 3 - 2 * zl - core, zm, zl]
    ).astype(jnp.int32)
    info = jnp.stack([core, chip * 2 + core]).astype(jnp.int32)

    rate = token_rates[:, 0]
    high = lax.reduce_precision(rate, 8, 7)
    extra = jnp.stack([high, rate - high]).astype(jnp.bfloat16)
    extra = jnp.pad(extra, ((0, 14), (0, HD - TOK)))
    own = jnp.concatenate([key_rows, value_rows, extra], axis=0)

    back1 = shifted(own, CHIPS, 1)
    own_x = shifted(own, "core", 1)
    w1t = fast_one[0].T
    w3t = fast_three[0].T
    w2 = fast_two[0]
    sofar = gradients(True, ids, own, own_x, w1t, w3t, w2)
    back1, sofar = lax.optimization_barrier((back1, sofar))

    back1_x = shifted(back1, "core", 1)
    back2 = shifted(back1, CHIPS, 1)
    partial = gradients(False, ids, back1, back1_x, w1t, w3t, w2, sofar)
    pieces = exchanged(partial.reshape(16, ROWS // 16, HD), SAME)
    back2_x = shifted(back2, "core", 1)
    cut = TOK - FAR
    far = jnp.where(
        core == 0,
        jnp.concatenate(
            [back2[FAR:TOK], back2_x[:cut], back2[TOK + FAR : 2 * TOK], back2_x[TOK : TOK + cut]]
        ),
        jnp.concatenate([back2[cut:TOK], back2[TOK + cut : 2 * TOK]]),
    )
    back3 = shifted(far, CHIPS, 1)
    back3_x = shifted(back3, "core", 1)
    piece = jnp.sum(pieces.astype(jnp.float32), axis=0).astype(jnp.bfloat16)
    spread = jnp.broadcast_to(piece[None], (8,) + piece.shape)
    mine = exchanged(spread, KIN).reshape(HALF, HD)
    attended, attended_sq = window_attention(
        info, queries, own, own_x, back1, back1_x, back2, back2_x, back3, back3_x
    )
    mine, attended, attended_sq = lax.optimization_barrier((mine, attended, attended_sq))

    up = shifted(mine, RING, 1)
    down = shifted(mine, RING, -1)
    far_up = shifted(mine[HALF // 2 :], RING, 2)
    far_down = shifted(mine[: HALF // 2], RING, -2)
    held = jnp.concatenate([mine, far_down, far_up, up, down], axis=0)
    held_x = shifted(held, "core", 1)

    fast, fast_sq = solve(ids, head_gain, queries, w1t, w3t, w2, held, held_x)
    sums = jnp.concatenate([attended_sq[0:1], fast_sq[0:1]], axis=0)
    sums = exchanged(jnp.broadcast_to(sums[None], (HEADS,) + sums.shape), "head")
    return finish(sums, attended, fast)


def solution(mesh):
    fine = Mesh(mesh.devices.reshape(2, 4, 2, 2, 2, 8), CHIPS + ("core", "head"))
    ctx = CHIPS + ("core",)
    return jax.shard_map(
        local,
        mesh=fine,
        in_specs=(
            P(ctx, "head"),
            P(ctx, "head"),
            P(ctx, "head"),
            P(ctx, "head"),
            P("head", None, None),
            P("head", None, None),
            P("head", None, None),
            P("head"),
        ),
        out_specs=(P(ctx, "head"), P(ctx, "head")),
        check_vma=False,
    )
```

time: 169 us -> 166 us (0.982)
  blocking collectives: 42.6 us -> 9.08 us
  waiting for transfers between devices: 40.7 us -> 68.2 us
  starting transfers between devices: 46.1 us -> 56 us
  Pallas kernels: 24.8 us -> 15.6 us
    all_to_all x2 -> x1, blocking collectives: 42.6 us -> 9.08 us  [exchanged(): return lax.all_to_all(x, axes, 0, 0)]
    ppermute x11 -> x12, waiting for transfers between devices: 40.7 us -> 68.1 us  [shifted(): return lax.ppermute(x, axes, [(i, (i + by) % count) for i in range(count)])]
    all_to_all x1 -> x2, starting transfers between devices: 6.75 us -> 16.5 us  [exchanged(): return lax.all_to_all(x, axes, 0, 0)]
    pallas_call x4, Pallas kernels: 22.4 us -> 14.4 us  [the longest x1 7.95 us: solve(): pl.pallas_call(solve_kernel, out_shape=(near_out((TOK, HD), jnp.float32),...]
    slice x2 -> x4, local copies, waits for them, and re-layouts: 0.06 us -> 5.07 us  [the longest x1 1.64 us: local(): back2[cut:TOK]]
    unnamed x33 -> x26, local copies, waits for them, and re-layouts: 6.66 us -> 4.52 us
    ppermute x11 -> x12, starting transfers between devices: 39.4 us -> 39.5 us  [shifted(): return lax.ppermute(x, axes, [(i, (i + by) % count) for i in range(count)])]
  transfers between devices with their start and end apart: 12 -> 14, of which waited for: 3 -> 8; matrix products, arithmetic and copies ran while one was open for 2% -> 5% of each run, Pallas kernels for 5% -> 3%
where the time goes in v2:
time: 166 us; the launch traced here: 164 us
  waiting for transfers between devices  68.2 us (41%)
  starting transfers between devices  56 us (34%)
  Pallas kernels  15.6 us (9%)
  local copies, waits for them, and re-layouts  10.4 us (6%)
  blocking collectives  9.08 us (5%)
  other arithmetic  3.04 us (2%)
    ppermute x12, waiting for transfers between devices, shifted(): return lax.ppermute(x, axes, [(i, (i + by) % count) for i in range(count)])  68.1 us
    ppermute x12, starting transfers between devices, shifted(): return lax.ppermute(x, axes, [(i, (i + by) % count) for i in range(count)])  39.5 us
    all_to_all x2, starting transfers between devices, exchanged(): return lax.all_to_all(x, axes, 0, 0)  16.5 us
    all_to_all x1, blocking collectives, exchanged(): return lax.all_to_all(x, axes, 0, 0)  9.08 us
    pallas_call x1, Pallas kernels, solve(): pl.pallas_call(solve_kernel, out_shape=(near_out((TOK, HD), jnp.float32),...  7.95 us
    unnamed x26, local copies, waits for them, and re-layouts  4.52 us
    pallas_call x1, Pallas kernels, window_attention(): pl.pallas_call(window_kernel, out_shape=(near_out((TOK, HD), jnp.float32)...  3.59 us
  transfers between devices with their start and end apart: 14, of which 8 were waited for; matrix products, arithmetic and copies ran while one was open for 5% of the time, Pallas kernels for 3%

profile of v2, /device:TPU:1, one launch (start us, length us, event | category | flops | bytes accessed | tf_op | source)
XLA Modules:
  0.0 164.0 jit_solution(15569933272522958815)
XLA Ops:
  2.4 8.7 %collective-permute-start.1 = (bf16[400,512]{1,0:T(8,128)(2,1)S(1)}, bf16[400,512]{1,0:T(8,128)(2,1)S(1)}, u32[]{:S(2)}, u32[]{:S(2)}) collective-permute-start(bf16[400,512]{1,0:T(8,128)(2,1)S(1)} %pad_maximum_fusion.pa_ref.refs_0_), channel_id=1, source_target_pairs={{0,8},{8,0},{1,9},{9,1},{2,10},{10,2},{3,11},{11,3},{4,12},{12,4},... | collective-permute-start | bytes 1228808 | tf_op jit(solution)/shard_map/ppermute | solution.py:38
  11.2 1.9 %collective-permute-start = (bf16[400,512]{1,0:T(8,128)(2,1)S(1)}, bf16[400,512]{1,0:T(8,128)(2,1)S(1)}, u32[]{:S(2)}, u32[]{:S(2)}) collective-permute-start(bf16[400,512]{1,0:T(8,128)(2,1)S(1)} %pad_maximum_fusion.pa_ref.refs_0_), channel_id=1, source_target_pairs={{0,16},{16,32},{32,48},{48,64},{64,80},{80,96},{96,112},{112,128},... | collective-permute-start | bytes 1228808 | tf_op jit(solution)/shard_map/ppermute | solution.py:38
  16.7 12.6 %collective-permute-done.pa_ref.refs_2_ = bf16[400,512]{1,0:T(8,128)(2,1)S(1)} collective-permute-done((bf16[400,512]{1,0:T(8,128)(2,1)S(1)}, bf16[400,512]{1,0:T(8,128)(2,1)S(1)}, u32[]{:S(2)}, u32[]{:S(2)}) %collective-permute-start) | collective-permute-done | bytes 409632 | tf_op jit(solution)/shard_map/ppermute | solution.py:38
  29.3 2.5 %collective-permute-start.2 = (bf16[400,512]{1,0:T(8,128)(2,1)S(1)}, bf16[400,512]{1,0:T(8,128)(2,1)S(1)}, u32[]{:S(2)}, u32[]{:S(2)}) collective-permute-start(bf16[400,512]{1,0:T(8,128)(2,1)S(1)} %collective-permute-done.pa_ref.refs_2_), channel_id=1, source_target_pairs={{0,8},{8,0},{1,9},{9,1},{2,10},{10,2},{3,11},{11,3},{4,12},{12,4},... | collective-permute-start | bytes 1228808 | tf_op jit(solution)/shard_map/ppermute | solution.py:38
  33.1 1.4 grad_second.1
  35.3 8.4 %all-to-all-start = ((bf16[16,24,512]{2,1,0:T(8,128)(2,1)}), bf16[16,24,512]{2,1,0:T(8,128)(2,1)}, u32[]{:S(2)}, u32[]{:S(2)}) async-start(bf16[16,24,512]{2,1,0:T(8,128)(2,1)} %bitcast.29), calls=%async_computation | async-start | bytes 786432 | tf_op jit(solution)/shard_map/all_to_all | solution.py:42
  43.7 1.9 %collective-permute-start.3 = (bf16[400,512]{1,0:T(8,128)(2,1)S(1)}, bf16[400,512]{1,0:T(8,128)(2,1)}, u32[]{:S(2)}, u32[]{:S(2)}) collective-permute-start(bf16[400,512]{1,0:T(8,128)(2,1)S(1)} %collective-permute-done.pa_ref.refs_2_), channel_id=1, source_target_pairs={{0,16},{16,32},{32,48},{48,64},{64,80},{80,96},{96,112},{112,128},... | collective-permute-start | bytes 1228808 | tf_op jit(solution)/shard_map/ppermute | solution.py:38
  45.6 28.5 %collective-permute-done.3.refs_4_ = bf16[400,512]{1,0:T(8,128)(2,1)} collective-permute-done((bf16[400,512]{1,0:T(8,128)(2,1)S(1)}, bf16[400,512]{1,0:T(8,128)(2,1)}, u32[]{:S(2)}, u32[]{:S(2)}) %collective-permute-start.3) | collective-permute-done | bytes 409632 | tf_op jit(solution)/shard_map/ppermute | solution.py:38
  74.1 3.3 %collective-permute-start.4 = (bf16[400,512]{1,0:T(8,128)(2,1)}, bf16[400,512]{1,0:T(8,128)(2,1)}, u32[]{:S(2)}, u32[]{:S(2)}) collective-permute-start(bf16[400,512]{1,0:T(8,128)(2,1)} %collective-permute-done.3.refs_4_), channel_id=1, source_target_pairs={{0,8},{8,0},{1,9},{9,1},{2,10},{10,2},{3,11},{11,3},{4,12},{12,4},... | collective-permute-start | bytes 1228808 | tf_op jit(solution)/shard_map/ppermute | solution.py:38
  77.4 1.5 fusion.8
  79.0 1.6 fusion.7
  82.4 8.1 %all-to-all-start.1 = ((bf16[8,24,512]{2,1,0:T(8,128)(2,1)}), bf16[8,24,512]{2,1,0:T(8,128)(2,1)}, u32[]{:S(2)}, u32[]{:S(2)}) async-start(bf16[8,24,512]{2,1,0:T(8,128)(2,1)} %broadcast_in_dim.4), calls=%async_computation.1 | async-start | bytes 393216 | tf_op jit(solution)/shard_map/all_to_all | solution.py:42
  91.6 3.1 %collective-permute-start.5 = (bf16[256,512]{1,0:T(8,128)(2,1)S(1)}, bf16[256,512]{1,0:T(8,128)(2,1)}, u32[]{:S(2)}, u32[]{:S(2)}) collective-permute-start(bf16[256,512]{1,0:T(8,128)(2,1)S(1)} %maximum_select_fusion), channel_id=1, source_target_pairs={{0,16},{16,32},{32,48},{48,64},{64,80},{80,96},{96,112},{112,128},... | collective-permute-start | bytes 786440 | tf_op jit(solution)/shard_map/ppermute | solution.py:38
  94.7 18.8 %collective-permute-done.5.refs_6_ = bf16[256,512]{1,0:T(8,128)(2,1)} collective-permute-done((bf16[256,512]{1,0:T(8,128)(2,1)S(1)}, bf16[256,512]{1,0:T(8,128)(2,1)}, u32[]{:S(2)}, u32[]{:S(2)}) %collective-permute-start.5) | collective-permute-done | bytes 262176 | tf_op jit(solution)/shard_map/ppermute | solution.py:38
  113.5 2.5 %collective-permute-start.6 = (bf16[256,512]{1,0:T(8,128)(2,1)}, bf16[256,512]{1,0:T(8,128)(2,1)}, u32[]{:S(2)}, u32[]{:S(2)}) collective-permute-start(bf16[256,512]{1,0:T(8,128)(2,1)} %collective-permute-done.5.refs_6_), channel_id=1, source_target_pairs={{0,8},{8,0},{1,9},{9,1},{2,10},{10,2},{3,11},{11,3},{4,12},{12,4},... | collective-permute-start | bytes 786440 | tf_op jit(solution)/shard_map/ppermute | solution.py:38
  117.6 3.6 %window.1 = (f32[192,512]{1,0:T(8,128)S(1)}, f32[8,192]{1,0:T(8,128)S(1)}) custom-call(s32[2]{0:T(128)S(1)} %pad_add_fusion.info_ref, bf16[192,512]{1,0:T(8,128)(2,1)S(1)} %copy-done.2, bf16[400,512]{1,0:T(8,128)(2,1)S(1)} %pad_maximum_fusion.pa_ref.refs_0_, bf16[400,512]{1,0:T(8,128)(2,1)S(1)} %collective-permute-done.1.pb_ref.refs_1_, ...), custom_call_target="tpu_custom_call" | custom-call | tf_op jit(solution)/shard_map/window/pallas_call | solution.py:218
  122.9 1.9 %collective-permute-start.9 = (bf16[192,512]{1,0:T(8,128)(2,1)}, bf16[192,512]{1,0:T(8,128)(2,1)S(1)}, u32[]{:S(2)}, u32[]{:S(2)}) collective-permute-start(bf16[192,512]{1,0:T(8,128)(2,1)} %bitcast.13), channel_id=1, source_target_pairs={{0,16},{16,32},{32,48},{48,64},{64,80},{80,96},{96,112},{112,128},... | collective-permute-start | bytes 589832 | tf_op jit(solution)/shard_map/ppermute | solution.py:38
  124.8 4.6 %collective-permute-start.10 = (bf16[192,512]{1,0:T(8,128)(2,1)}, bf16[192,512]{1,0:T(8,128)(2,1)S(1)}, u32[]{:S(2)}, u32[]{:S(2)}) collective-permute-start(bf16[192,512]{1,0:T(8,128)(2,1)} %bitcast.13), channel_id=1, source_target_pairs={{0,240},{16,0},{32,16},{48,32},{64,48},{80,64},{96,80},{112,96},{1... | collective-permute-start | bytes 589832 | tf_op jit(solution)/shard_map/ppermute | solution.py:38
  129.4 1.9 %collective-permute-start.7 = (bf16[96,512]{1,0:T(8,128)(2,1)S(1)}, bf16[96,512]{1,0:T(8,128)(2,1)S(1)}, u32[]{:S(2)}, u32[]{:S(2)}) collective-permute-start(bf16[96,512]{1,0:T(8,128)(2,1)S(1)} %get-tuple-element.27), channel_id=1, source_target_pairs={{0,224},{16,240},{32,0},{48,16},{64,32},{80,48},{96,64},{112,80},{... | collective-permute-start | bytes 294920 | tf_op jit(solution)/shard_map/ppermute | solution.py:38
  131.3 4.3 %collective-permute-start.8 = (bf16[96,512]{1,0:T(8,128)(2,1)S(1)}, bf16[96,512]{1,0:T(8,128)(2,1)S(1)}, u32[]{:S(2)}, u32[]{:S(2)}) collective-permute-start(bf16[96,512]{1,0:T(8,128)(2,1)S(1)} %get-tuple-element.26), channel_id=1, source_target_pairs={{0,32},{16,48},{32,64},{48,80},{64,96},{80,112},{96,128},{112,144}... | collective-permute-start | bytes 294920 | tf_op jit(solution)/shard_map/ppermute | solution.py:38
  137.5 3.5 %collective-permute-done.8 = bf16[96,512]{1,0:T(8,128)(2,1)S(1)} collective-permute-done((bf16[96,512]{1,0:T(8,128)(2,1)S(1)}, bf16[96,512]{1,0:T(8,128)(2,1)S(1)}, u32[]{:S(2)}, u32[]{:S(2)}) %collective-permute-start.8) | collective-permute-done | bytes 98336 | tf_op jit(solution)/shard_map/ppermute | solution.py:38
  141.1 2.8 %collective-permute-start.11 = (bf16[768,512]{1,0:T(8,128)(2,1)S(1)}, bf16[768,512]{1,0:T(8,128)(2,1)S(1)}, u32[]{:S(2)}, u32[]{:S(2)}) collective-permute-start(bf16[768,512]{1,0:T(8,128)(2,1)S(1)} %constant_dynamic-update-slice_fusion.g_ref), channel_id=1, source_target_pairs={{0,8},{8,0},{1,9},{9,1},{2,10},{10,2},{3,11},{11,3},{4,12},{12,4},... | collective-permute-start | bytes 2359304 | tf_op jit(solution)/shard_map/ppermute | solution.py:38
  145.6 7.9 %solve.1 = (f32[192,512]{1,0:T(8,128)S(1)}, f32[8,192]{1,0:T(8,128)S(1)}) custom-call(s32[6]{0:T(128)S(1)} %stack.42.ids_ref, f32[1]{0:T(128)S(6)} %copy.16.gain_ref, bf16[192,512]{1,0:T(8,128)(2,1)S(1)} %copy-done.2, bf16[512,512]{1,0:T(8,128)(2,1)S(1)} %bitcast.22, bf16[512,512]{1,0:T(8,128)(2,1)S(1)} %bitcast.25, bf16[512,512]{1,0:T(8,128)(2,1)S(1)} %bitcast.28, ...), custom_call_target="tpu_custom_call" | custom-call | tf_op jit(solution)/shard_map/solve/pallas_call | solution.py:165
  153.6 9.1 %all_to_all.15.sums_ref = f32[8,2,192]{2,1,0:T(2,128)S(1)} all-to-all(f32[8,2,192]{2,1,0:T(2,128)S(1)} %broadcast_in_dim.5), channel_id=1, replica_groups=mesh['xh'=2,'zq'=4,'zm'=2,'zl'=2,'core'=2,'head'=8] {'head'}, dimensions={0} | all-to-all | bytes 24576 | tf_op jit(solution)/shard_map/all_to_all | solution.py:42
  (53 shorter events, 17.7 us)
Async XLA Ops:
  0.6 12.5 %copy-start.5 = (bf16[1,512,512]{2,1,0:T(8,128)(2,1)S(1)}, bf16[1,512,512]{2,1,0:T(8,128)(2,1)}, u32[]{:S(2)}) copy-start(bf16[1,512,512]{2,1,0:T(8,128)(2,1)} %param.12) | copy-start | bytes 1572868
  2.4 12.1 %collective-permute-start.1 = (bf16[400,512]{1,0:T(8,128)(2,1)S(1)}, bf16[400,512]{1,0:T(8,128)(2,1)S(1)}, u32[]{:S(2)}, u32[]{:S(2)}) collective-permute-start(bf16[400,512]{1,0:T(8,128)(2,1)S(1)} %pad_maximum_fusion.pa_ref.refs_0_), channel_id=1, source_target_pairs={{0,8},{8,0},{1,9},{9,1},{2,10},{10,2},{3,11},{11,3},{4,12},{12,4},... | collective-permute-start | bytes 1228808 | tf_op jit(solution)/shard_map/ppermute | solution.py:38
  11.2 18.1 %collective-permute-start = (bf16[400,512]{1,0:T(8,128)(2,1)S(1)}, bf16[400,512]{1,0:T(8,128)(2,1)S(1)}, u32[]{:S(2)}, u32[]{:S(2)}) collective-permute-start(bf16[400,512]{1,0:T(8,128)(2,1)S(1)} %pad_maximum_fusion.pa_ref.refs_0_), channel_id=1, source_target_pairs={{0,16},{16,32},{32,48},{48,64},{64,80},{80,96},{96,112},{112,128},... | collective-permute-start | bytes 1228808 | tf_op jit(solution)/shard_map/ppermute | solution.py:38
  13.2 1.0 copy-start.6
  14.2 1.0 copy-start
  29.3 3.8 %collective-permute-start.2 = (bf16[400,512]{1,0:T(8,128)(2,1)S(1)}, bf16[400,512]{1,0:T(8,128)(2,1)S(1)}, u32[]{:S(2)}, u32[]{:S(2)}) collective-permute-start(bf16[400,512]{1,0:T(8,128)(2,1)S(1)} %collective-permute-done.pa_ref.refs_2_), channel_id=1, source_target_pairs={{0,8},{8,0},{1,9},{9,1},{2,10},{10,2},{3,11},{11,3},{4,12},{12,4},... | collective-permute-start | bytes 1228808 | tf_op jit(solution)/shard_map/ppermute | solution.py:38
  34.5 0.8 copy-start.1
  35.3 45.3 %all-to-all-start = ((bf16[16,24,512]{2,1,0:T(8,128)(2,1)}), bf16[16,24,512]{2,1,0:T(8,128)(2,1)}, u32[]{:S(2)}, u32[]{:S(2)}) async-start(bf16[16,24,512]{2,1,0:T(8,128)(2,1)} %bitcast.29), calls=%async_computation | async-start | bytes 786432 | tf_op jit(solution)/shard_map/all_to_all | solution.py:42
  43.7 30.4 %collective-permute-start.3 = (bf16[400,512]{1,0:T(8,128)(2,1)S(1)}, bf16[400,512]{1,0:T(8,128)(2,1)}, u32[]{:S(2)}, u32[]{:S(2)}) collective-permute-start(bf16[400,512]{1,0:T(8,128)(2,1)S(1)} %collective-permute-done.pa_ref.refs_2_), channel_id=1, source_target_pairs={{0,16},{16,32},{32,48},{48,64},{64,80},{80,96},{96,112},{112,128},... | collective-permute-start | bytes 1228808 | tf_op jit(solution)/shard_map/ppermute | solution.py:38
  74.1 16.4 %collective-permute-start.4 = (bf16[400,512]{1,0:T(8,128)(2,1)}, bf16[400,512]{1,0:T(8,128)(2,1)}, u32[]{:S(2)}, u32[]{:S(2)}) collective-permute-start(bf16[400,512]{1,0:T(8,128)(2,1)} %collective-permute-done.3.refs_4_), channel_id=1, source_target_pairs={{0,8},{8,0},{1,9},{9,1},{2,10},{10,2},{3,11},{11,3},{4,12},{12,4},... | collective-permute-start | bytes 1228808 | tf_op jit(solution)/shard_map/ppermute | solution.py:38
  82.4 39.6 %all-to-all-start.1 = ((bf16[8,24,512]{2,1,0:T(8,128)(2,1)}), bf16[8,24,512]{2,1,0:T(8,128)(2,1)}, u32[]{:S(2)}, u32[]{:S(2)}) async-start(bf16[8,24,512]{2,1,0:T(8,128)(2,1)} %broadcast_in_dim.4), calls=%async_computation.1 | async-start | bytes 393216 | tf_op jit(solution)/shard_map/all_to_all | solution.py:42
  90.5 1.0 copy-start.7
  90.5 1.0 copy-start.8
  90.5 1.0 copy-start.9
  91.5 26.1 %copy-start.2 = (bf16[192,512]{1,0:T(8,128)(2,1)S(1)}, bf16[192,512]{1,0:T(8,128)(2,1)}, u32[]{:S(2)}) copy-start(bf16[192,512]{1,0:T(8,128)(2,1)} %q_ref.3) | copy-start | bytes 589828
  91.6 21.9 %collective-permute-start.5 = (bf16[256,512]{1,0:T(8,128)(2,1)S(1)}, bf16[256,512]{1,0:T(8,128)(2,1)}, u32[]{:S(2)}, u32[]{:S(2)}) collective-permute-start(bf16[256,512]{1,0:T(8,128)(2,1)S(1)} %maximum_select_fusion), channel_id=1, source_target_pairs={{0,16},{16,32},{32,48},{48,64},{64,80},{80,96},{96,112},{112,128},... | collective-permute-start | bytes 786440 | tf_op jit(solution)/shard_map/ppermute | solution.py:38
  113.5 4.0 %collective-permute-start.6 = (bf16[256,512]{1,0:T(8,128)(2,1)}, bf16[256,512]{1,0:T(8,128)(2,1)}, u32[]{:S(2)}, u32[]{:S(2)}) collective-permute-start(bf16[256,512]{1,0:T(8,128)(2,1)} %collective-permute-done.5.refs_6_), channel_id=1, source_target_pairs={{0,8},{8,0},{1,9},{9,1},{2,10},{10,2},{3,11},{11,3},{4,12},{12,4},... | collective-permute-start | bytes 786440 | tf_op jit(solution)/shard_map/ppermute | solution.py:38
  121.1 0.8 copy-start.3
  122.9 18.2 %collective-permute-start.9 = (bf16[192,512]{1,0:T(8,128)(2,1)}, bf16[192,512]{1,0:T(8,128)(2,1)S(1)}, u32[]{:S(2)}, u32[]{:S(2)}) collective-permute-start(bf16[192,512]{1,0:T(8,128)(2,1)} %bitcast.13), channel_id=1, source_target_pairs={{0,16},{16,32},{32,48},{48,64},{64,80},{80,96},{96,112},{112,128},... | collective-permute-start | bytes 589832 | tf_op jit(solution)/shard_map/ppermute | solution.py:38
  124.8 16.3 %collective-permute-start.10 = (bf16[192,512]{1,0:T(8,128)(2,1)}, bf16[192,512]{1,0:T(8,128)(2,1)S(1)}, u32[]{:S(2)}, u32[]{:S(2)}) collective-permute-start(bf16[192,512]{1,0:T(8,128)(2,1)} %bitcast.13), channel_id=1, source_target_pairs={{0,240},{16,0},{32,16},{48,32},{64,48},{80,64},{96,80},{112,96},{1... | collective-permute-start | bytes 589832 | tf_op jit(solution)/shard_map/ppermute | solution.py:38
  129.4 8.1 %collective-permute-start.7 = (bf16[96,512]{1,0:T(8,128)(2,1)S(1)}, bf16[96,512]{1,0:T(8,128)(2,1)S(1)}, u32[]{:S(2)}, u32[]{:S(2)}) collective-permute-start(bf16[96,512]{1,0:T(8,128)(2,1)S(1)} %get-tuple-element.27), channel_id=1, source_target_pairs={{0,224},{16,240},{32,0},{48,16},{64,32},{80,48},{96,64},{112,80},{... | collective-permute-start | bytes 294920 | tf_op jit(solution)/shard_map/ppermute | solution.py:38
  131.3 9.7 %collective-permute-start.8 = (bf16[96,512]{1,0:T(8,128)(2,1)S(1)}, bf16[96,512]{1,0:T(8,128)(2,1)S(1)}, u32[]{:S(2)}, u32[]{:S(2)}) collective-permute-start(bf16[96,512]{1,0:T(8,128)(2,1)S(1)} %get-tuple-element.26), channel_id=1, source_target_pairs={{0,32},{16,48},{32,64},{48,80},{64,96},{80,112},{96,128},{112,144}... | collective-permute-start | bytes 294920 | tf_op jit(solution)/shard_map/ppermute | solution.py:38
  141.1 4.5 %collective-permute-start.11 = (bf16[768,512]{1,0:T(8,128)(2,1)S(1)}, bf16[768,512]{1,0:T(8,128)(2,1)S(1)}, u32[]{:S(2)}, u32[]{:S(2)}) collective-permute-start(bf16[768,512]{1,0:T(8,128)(2,1)S(1)} %constant_dynamic-update-slice_fusion.g_ref), channel_id=1, source_target_pairs={{0,8},{8,0},{1,9},{9,1},{2,10},{10,2},{3,11},{11,3},{4,12},{12,4},... | collective-permute-start | bytes 2359304 | tf_op jit(solution)/shard_map/ppermute | solution.py:38
  144.6 18.2 %copy-start.4 = (f32[192,512]{1,0:T(8,128)S(1)}, f32[192,512]{1,0:T(8,128)}, u32[]{:S(2)}) copy-start(f32[192,512]{1,0:T(8,128)} %copy-done.3) | copy-start | bytes 1179652

commit v3 on v2

--- a/solution.py
+++ b/solution.py
@@ -21,21 +21,35 @@
 COEF_C = 2.0315
 EPSILON = 1e-06
 
-HALF = ROWS // 2
+BIT = ROWS // 4
 FAR = 128
+SPAN = 3
 
 CHIPS = ("xh", "zq", "zm", "zl")
 RING = ("zq", "zm", "zl")
-SAME = ("zm", "xh", "zq")
+SAME = ("zm", "zl", "zq")
 KIN = ("xh", "zq")
 
 NT = (((1,), (1,)), ((), ()))
 TN = (((0,), (0,)), ((), ()))
 
 
-def shifted(x, axes, by):
-    count = lax.axis_size(axes)
-    return lax.ppermute(x, axes, [(i, (i + by) % count) for i in range(count)])
+def swapped(x, axis):
+    return lax.ppermute(x, axis, [(0, 1), (1, 0)])
+
+
+def forwarded(x):
+    count = lax.axis_size(RING)
+    return lax.ppermute(x, RING, [(i, (i + 1) % count) for i in range(count)])
+
+
+def around(x, by):
+    count = lax.axis_size(RING)
+    pairs = []
+    for i in range(count):
+        pairs.append((2 * i, 2 * ((i - by) % count)))
+        pairs.append((2 * i + 1, 2 * ((i + by) % count) + 1))
+    return lax.ppermute(x, RING + ("core",), pairs)
 
 
 def exchanged(x, axes):
@@ -60,6 +74,35 @@
 
 def sigmoid(x):
     return 1.0 / (1.0 + jnp.exp(-x))
+
+
+VMEM = pl.BlockSpec(memory_space=pltpu.VMEM)
+SMEM = pl.BlockSpec(memory_space=pltpu.SMEM)
+
+
+def in_lanes(dtype, *columns):
+    lane = lax.broadcasted_iota(jnp.int32, (TOK, 128), 1)
+    out = jnp.zeros((TOK, 128), jnp.float32)
+    for i, column in enumerate(columns):
+        out = jnp.where(lane == i, column, out)
+    return out.astype(dtype)
+
+
+def tally_kernel(pieces_ref, out_ref):
+    total = jnp.sum(pieces_ref[...].astype(jnp.float32), axis=0).astype(jnp.bfloat16)
+    for i in range(out_ref.shape[0]):
+        out_ref[i] = total
+
+
+def tally(pieces, copies):
+    return pl.pallas_call(
+        tally_kernel,
+        out_shape=jax.ShapeDtypeStruct((copies,) + pieces.shape[1:], jnp.bfloat16),
+        in_specs=[VMEM],
+        out_specs=VMEM,
+        compiler_params=pltpu.CompilerParams(vmem_limit_bytes=8 << 20),
+        name="tally",
+    )(pieces)
 
 
 def grad_kernel(first, ids_ref, pa_ref, pb_ref, w1_ref, w3_ref, w2_ref, *rest):
@@ -102,10 +145,6 @@
         out_ref[2 * PART : ROWS, :] = (g2 + sofar_ref[2 * PART : ROWS, :]).astype(jnp.bfloat16)
 
 
-VMEM = pl.BlockSpec(memory_space=pltpu.VMEM)
-SMEM = pl.BlockSpec(memory_space=pltpu.SMEM)
-
-
 def gradients(first, ids, *arrays):
     return pl.pallas_call(
         functools.partial(grad_kernel, first),
@@ -119,22 +158,32 @@
     )(ids, *[near(x) for x in arrays])
 
 
-def solve_kernel(ids_ref, gain_ref, q_ref, w1_ref, w3_ref, w2_ref, g_ref, gx_ref, o_ref, sq_ref):
-    low = ids_ref[4] == 0
-    near_low = ids_ref[4] == ids_ref[5]
-    slots = []
-    for first, second, when in ((0, HALF, low), (3 * HALF, 2 * HALF, near_low)):
-        for ref in (g_ref, gx_ref):
-            a = ref[first : first + HALF, :]
-            b = ref[second : second + HALF, :]
-            slots.append(
-                jnp.concatenate([jnp.where(when, a, b), jnp.where(when, b, a)], axis=0)
-            )
+def solve_kernel(
+    ids_ref, gain_ref, q_ref, w1_ref, w3_ref, w2_ref, h_ref, hx_ref, a_ref, ax_ref, o_ref, sq_ref, all_ref
+):
+    core = ids_ref[1]
+    place = ids_ref[2]
+
+    def put(ref, row, which, plane, turn):
+        start = (plane * 2 + which) * ROWS + lax.rem(place + turn, 4) * BIT
+        all_ref[pl.ds(pl.multiple_of(start, 32), BIT), :] = ref[row : row + BIT, :]
+
+    for plane in range(2):
+        put(h_ref, plane * BIT, core, plane, 0)
+        put(hx_ref, plane * BIT, 1 - core, plane, 0)
+        put(a_ref, plane * BIT, core, plane, 1 + 2 * core)
+        put(a_ref, (2 + plane) * BIT, 1 - core, plane, 1 + 2 * core)
+        put(ax_ref, plane * BIT, 1 - core, plane, 3 + 2 * core)
+        put(ax_ref, (2 + plane) * BIT, core, plane, 3 + 2 * core)
+    put(a_ref, 4 * BIT, core, core, 2)
+    put(a_ref, 5 * BIT, 1 - core, core, 2)
+    put(ax_ref, 4 * BIT, 1 - core, 1 - core, 2)
+    put(ax_ref, 5 * BIT, core, 1 - core, 2)
     fresh = []
     for m, w_ref in enumerate((w1_ref, w3_ref, w2_ref)):
-        g = jnp.concatenate([r[m * PART : (m + 1) * PART, :] for r in slots], axis=0).astype(
-            jnp.float32
-        )
+        g = jnp.concatenate(
+            [all_ref[i * ROWS + m * PART : i * ROWS + (m + 1) * PART, :] for i in range(4)], axis=0
+        ).astype(jnp.float32)
         norm = jnp.sqrt(jnp.sum(g * g, keepdims=True)) + 1e-07
         x = (g / norm).astype(jnp.bfloat16)
         for _ in range(NS_STEPS):
@@ -143,11 +192,7 @@
                 jnp.bfloat16
             )
             x = (COEF_A * x.astype(jnp.float32) + nn(mixer, x)).astype(jnp.bfloat16)
-        w = jnp.concatenate(
-            [w_ref[pl.ds(pl.multiple_of(ids_ref[i] * PART, PART), PART), :] for i in range(4)],
-            axis=0,
-        )
-        fresh.append((w.astype(jnp.float32) - x.astype(jnp.float32)).astype(jnp.bfloat16))
+        fresh.append((w_ref[...].astype(jnp.float32) - x.astype(jnp.float32)).astype(jnp.bfloat16))
     q = q_ref[...].astype(jnp.float32)
     qn = (q * lax.rsqrt(jnp.mean(q * q, axis=-1, keepdims=True) + EPSILON)).astype(jnp.bfloat16)
     h1 = nt(qn, fresh[0])
@@ -167,16 +212,13 @@
         out_shape=(near_out((TOK, HD), jnp.float32), near_out((8, TOK), jnp.float32)),
         in_specs=[SMEM, SMEM] + [VMEM] * len(arrays),
         out_specs=(VMEM, VMEM),
+        scratch_shapes=[pltpu.VMEM((4 * ROWS, HD), jnp.bfloat16)],
         compiler_params=pltpu.CompilerParams(vmem_limit_bytes=28 << 20),
         name="solve",
     )(ids, gain, *[near(x) for x in arrays])
 
 
-def window_kernel(info_ref, q_ref, *refs):
-    blocks = refs[:8]
-    o_ref, sq_ref = refs[8:]
-    core = info_ref[0]
-    start = info_ref[1]
+def attend(q, blocks, core, start, foreign):
     places = (
         (TOK, 0),
         (TOK, TOK * (1 - 2 * core)),
@@ -187,41 +229,99 @@
         (FAR, -WINDOW + (FAR - TOK) * core),
         (FAR, -WINDOW + FAR - (FAR + TOK) * core),
     )
-    q = q_ref[...]
+    pairs = list(zip(blocks, places))[2 if foreign else 0 :]
     scores = []
     top = None
-    for ref, (count, place) in zip(blocks, places):
+    for ref, (count, place) in pairs:
         row = lax.broadcasted_iota(jnp.int32, (TOK, count), 0)
         col = lax.broadcasted_iota(jnp.int32, (TOK, count), 1)
         s = nt(q, ref[0:count, :]) * HD ** (-0.5)
         offset = row - col - place
-        allowed = (offset >= 0) & (offset < WINDOW) & (col + (start * TOK + place) >= 0)
+        before = col + (start * TOK + place) < 0
+        allowed = (offset >= 0) & (offset < WINDOW)
+        allowed = allowed & before if foreign else allowed & jnp.logical_not(before)
         s = jnp.where(allowed, s, -1e30)
         scores.append(s)
         here = jnp.max(s, axis=-1, keepdims=True)
         top = here if top is None else jnp.maximum(top, here)
-    weights = [jnp.exp(s - top) for s in scores]
+    if foreign:
+        top = top.astype(jnp.bfloat16).astype(jnp.float32)
+        weights = [jnp.where(s > -1e29, jnp.exp(s - top), 0.0) for s in scores]
+    else:
+        weights = [jnp.exp(s - top) for s in scores]
     total = functools.reduce(jnp.add, [jnp.sum(w, axis=-1, keepdims=True) for w in weights])
-    inverse = 1.0 / total
+    inverse = 1.0 / (jnp.maximum(total, 1e-30) if foreign else total)
     o = None
-    for ref, w, (count, _) in zip(blocks, weights, places):
+    for w, (ref, (count, _)) in zip(weights, pairs):
         part = nn((w * inverse).astype(jnp.bfloat16), ref[count : 2 * count, :])
         o = part if o is None else o + part
+    return o, top, total
+
+
+def window_kernel(info_ref, q_ref, visitor_ref, *refs):
+    blocks = refs[:8]
+    o_ref, stat_ref, reply_ref = refs[8:]
+    core = info_ref[0]
+    start = info_ref[1]
+    hosts = info_ref[2] == 1
+    o, top, total = attend(q_ref[...], blocks, core, start, False)
     o_ref[...] = o
+    stat_ref[...] = in_lanes(jnp.float32, top, total)
+
+    @pl.when(hosts)
+    def _():
+        o, top, total = attend(visitor_ref[...], blocks, core, start, True)
+        high = total.astype(jnp.bfloat16).astype(jnp.float32)
+        reply_ref[:, 0:HD] = o.astype(jnp.bfloat16)
+        reply_ref[:, HD : HD + 128] = in_lanes(jnp.bfloat16, top, high, total - high)
+
+    @pl.when(jnp.logical_not(hosts))
+    def _():
+        reply_ref[...] = jnp.zeros_like(reply_ref)
+
+
+def window_attention(info, *arrays):
+    return pl.pallas_call(
+        window_kernel,
+        out_shape=(
+            near_out((TOK, HD), jnp.float32),
+            near_out((TOK, 128), jnp.float32),
+            near_out((TOK, HD + 128), jnp.bfloat16),
+        ),
+        in_specs=[SMEM] + [VMEM] * len(arrays),
+        out_specs=(VMEM, VMEM, VMEM),
+        compiler_params=pltpu.CompilerParams(vmem_limit_bytes=24 << 20),
+        name="window",
+    )(info, *[near(x) for x in arrays])
+
+
+def merge_kernel(info_ref, o_ref, stat_ref, reply_ref, out_ref, sq_ref):
+    guest = info_ref[3] == 1
+    top = stat_ref[:, 0:1]
+    total = stat_ref[:, 1:2]
+    far_stat = reply_ref[:, HD : HD + 128].astype(jnp.float32)
+    far_top = jnp.where(guest, far_stat[:, 0:1], top)
+    far_total = jnp.where(guest, far_stat[:, 1:2] + far_stat[:, 2:3], 0.0)
+    both = jnp.maximum(top, far_top)
+    e1 = total * jnp.exp(top - both)
+    e2 = far_total * jnp.exp(far_top - both)
+    inverse = 1.0 / (e1 + e2)
+    o = o_ref[...] * (e1 * inverse) + reply_ref[:, 0:HD].astype(jnp.float32) * (e2 * inverse)
+    out_ref[...] = o
     sq_ref[...] = lax.dot_general(
         jnp.ones((8, HD), jnp.float32), o * o, NT,
         precision=lax.Precision.HIGHEST, preferred_element_type=jnp.float32,
     )
 
 
-def window_attention(info, *arrays):
-    return pl.pallas_call(
-        window_kernel,
+def merge(info, *arrays):
+    return pl.pallas_call(
+        merge_kernel,
         out_shape=(near_out((TOK, HD), jnp.float32), near_out((8, TOK), jnp.float32)),
         in_specs=[SMEM] + [VMEM] * len(arrays),
         out_specs=(VMEM, VMEM),
-        compiler_params=pltpu.CompilerParams(vmem_limit_bytes=24 << 20),
-        name="window",
+        compiler_params=pltpu.CompilerParams(vmem_limit_bytes=8 << 20),
+        name="merge",
     )(info, *[near(x) for x in arrays])
 
 
@@ -252,14 +352,12 @@
 
 
 def local(queries, key_rows, value_rows, token_rates, fast_one, fast_three, fast_two, head_gain):
-    zl = lax.axis_index("zl")
-    zm = lax.axis_index("zm")
+    xh = lax.axis_index("xh")
+    z = lax.axis_index(RING)
     core = lax.axis_index("core")
-    chip = lax.axis_index(CHIPS)
-    ids = jnp.stack(
-        [zl * 2 + core, zl * 2 + 1 - core, 2 - 2 * zl + core, 3 - 2 * zl - core, zm, zl]
-    ).astype(jnp.int32)
-    info = jnp.stack([core, chip * 2 + core]).astype(jnp.int32)
+    ids = jnp.stack([xh * 2 + core, core, lax.rem(z, 4)]).astype(jnp.int32)
+    edge = (z < SPAN).astype(jnp.int32)
+    info = jnp.stack([core, z * 2 + core, (1 - xh) * edge, xh * edge]).astype(jnp.int32)
 
     rate = token_rates[:, 0]
     high = lax.reduce_precision(rate, 8, 7)
@@ -267,19 +365,23 @@
     extra = jnp.pad(extra, ((0, 14), (0, HD - TOK)))
     own = jnp.concatenate([key_rows, value_rows, extra], axis=0)
 
-    back1 = shifted(own, CHIPS, 1)
-    own_x = shifted(own, "core", 1)
+    deep = lax.axis_size(RING)
+    own_x = swapped(own, "core")
+    across = swapped(own, "xh")
+    back1 = forwarded(own)
     w1t = fast_one[0].T
     w3t = fast_three[0].T
     w2 = fast_two[0]
     sofar = gradients(True, ids, own, own_x, w1t, w3t, w2)
-    back1, sofar = lax.optimization_barrier((back1, sofar))
-
-    back1_x = shifted(back1, "core", 1)
-    back2 = shifted(back1, CHIPS, 1)
-    partial = gradients(False, ids, back1, back1_x, w1t, w3t, w2, sofar)
+    across, sofar = lax.optimization_barrier((across, sofar))
+    across_x = swapped(across, "core")
+    partial = gradients(False, ids, across, across_x, w1t, w3t, w2, sofar)
     pieces = exchanged(partial.reshape(16, ROWS // 16, HD), SAME)
-    back2_x = shifted(back2, "core", 1)
+
+    visitor = lax.ppermute(queries, CHIPS, [(deep + i, i) for i in range(SPAN)])
+    back1_x = swapped(back1, "core")
+    back2 = forwarded(back1)
+    back2_x = swapped(back2, "core")
     cut = TOK - FAR
     far = jnp.where(
         core == 0,
@@ -288,24 +390,32 @@
         ),
         jnp.concatenate([back2[cut:TOK], back2[TOK + cut : 2 * TOK]]),
     )
-    back3 = shifted(far, CHIPS, 1)
-    back3_x = shifted(back3, "core", 1)
-    piece = jnp.sum(pieces.astype(jnp.float32), axis=0).astype(jnp.bfloat16)
-    spread = jnp.broadcast_to(piece[None], (8,) + piece.shape)
-    mine = exchanged(spread, KIN).reshape(HALF, HD)
-    attended, attended_sq = window_attention(
-        info, queries, own, own_x, back1, back1_x, back2, back2_x, back3, back3_x
-    )
-    mine, attended, attended_sq = lax.optimization_barrier((mine, attended, attended_sq))
-
-    up = shifted(mine, RING, 1)
-    down = shifted(mine, RING, -1)
-    far_up = shifted(mine[HALF // 2 :], RING, 2)
-    far_down = shifted(mine[: HALF // 2], RING, -2)
-    held = jnp.concatenate([mine, far_down, far_up, up, down], axis=0)
-    held_x = shifted(held, "core", 1)
-
-    fast, fast_sq = solve(ids, head_gain, queries, w1t, w3t, w2, held, held_x)
+    back3 = forwarded(far)
+    back3_x = swapped(back3, "core")
+    spread = tally(pieces, 8)
+    mine = exchanged(spread, KIN).reshape(2 * BIT, HD)
+    seen, stats, answer = window_attention(
+        info, queries, visitor, own, own_x, back1, back1_x, back2, back2_x, back3, back3_x
+    )
+    reply = lax.ppermute(answer, CHIPS, [(i, deep + i) for i in range(SPAN)])
+    attended, attended_sq = merge(info, seen, stats, reply)
+
+    mine_x = swapped(mine, "core")
+    beside = around(jnp.concatenate([mine, mine_x]), 1)
+    beyond = around(
+        jnp.where(
+            core == 0,
+            jnp.concatenate([mine[:BIT], mine_x[:BIT]]),
+            jnp.concatenate([mine[BIT:], mine_x[BIT:]]),
+        ),
+        2,
+    )
+    held = jnp.concatenate([beside, beyond])
+    held_x = swapped(held, "core")
+
+    fast, fast_sq = solve(
+        ids, head_gain, queries, w1t, w3t, w2, mine, mine_x, held, held_x
+    )
     sums = jnp.concatenate([attended_sq[0:1], fast_sq[0:1]], axis=0)
     sums = exchanged(jnp.broadcast_to(sums[None], (HEADS,) + sums.shape), "head")
     return finish(sums, attended, fast)

time: 166 us -> 190 us (1.14)
  the two profiles are of different devices: /device:TPU:1 before, /device:TPU:4 now
where the time goes in v3:
time: 190 us; the launch traced here: 189 us
  waiting for transfers between devices  79.4 us (42%)
  starting transfers between devices  70.9 us (37%)
  Pallas kernels  19.6 us (10%)
  blocking collectives  11.1 us (6%)
  local copies, waits for them, and re-layouts  3.99 us (2%)
  other arithmetic  2.14 us (1%)
    ppermute x3, waiting for transfers between devices, forwarded(): return lax.ppermute(x, RING, [(i, (i + 1) % count) for i in range(count)])  37.1 us
    all_to_all x2, starting transfers between devices, exchanged(): return lax.all_to_all(x, axes, 0, 0)  25.7 us
    ppermute x8, starting transfers between devices, swapped(): return lax.ppermute(x, axis, [(0, 1), (1, 0)])  23.4 us
    all_to_all x2, waiting for transfers between devices, exchanged(): return lax.all_to_all(x, axes, 0, 0)  14.3 us
    all_to_all x1, blocking collectives, exchanged(): return lax.all_to_all(x, axes, 0, 0)  11.1 us
    ppermute x8, waiting for transfers between devices, swapped(): return lax.ppermute(x, axis, [(0, 1), (1, 0)])  9.69 us
    ppermute x1, waiting for transfers between devices, local(): reply = lax.ppermute(answer, CHIPS, [(i, deep + i) for i in range(SPAN)])  9.61 us
    ppermute x3, starting transfers between devices, forwarded(): return lax.ppermute(x, RING, [(i, (i + 1) % count) for i in range(count)])  9.61 us
  transfers between devices with their start and end apart: 17, of which 11 were waited for; matrix products, arithmetic and copies ran while one was open for 1% of the time, Pallas kernels for 4%

profile of v3, /device:TPU:4, one launch (start us, length us, event | category | flops | bytes accessed | tf_op | source)
XLA Modules:
  0.0 188.7 jit_solution(8563600193370609718)
XLA Ops:
  2.4 1.9 %collective-permute-start.1 = (bf16[400,512]{1,0:T(8,128)(2,1)S(1)}, bf16[400,512]{1,0:T(8,128)(2,1)S(1)}, u32[]{:S(2)}, u32[]{:S(2)}) collective-permute-start(bf16[400,512]{1,0:T(8,128)(2,1)S(1)} %pad_maximum_fusion.refs_0_.pa_ref), channel_id=1, source_target_pairs={{0,8},{8,0},{1,9},{9,1},{2,10},{10,2},{3,11},{11,3},{4,12},{12,4},... | collective-permute-start | bytes 1228808 | tf_op jit(solution)/shard_map/ppermute | solution.py:38
  4.4 7.8 %collective-permute-start.9 = (bf16[400,512]{1,0:T(8,128)(2,1)S(1)}, bf16[400,512]{1,0:T(8,128)(2,1)S(1)}, u32[]{:S(2)}, u32[]{:S(2)}) collective-permute-start(bf16[400,512]{1,0:T(8,128)(2,1)S(1)} %pad_maximum_fusion.refs_0_.pa_ref), channel_id=1, source_target_pairs={{0,256},{256,0},{1,257},{257,1},{2,258},{258,2},{3,259},{259,3},{4... | collective-permute-start | bytes 1228808 | tf_op jit(solution)/shard_map/ppermute | solution.py:38
  15.7 6.6 %collective-permute-done.9.pa_ref = bf16[400,512]{1,0:T(8,128)(2,1)S(1)} collective-permute-done((bf16[400,512]{1,0:T(8,128)(2,1)S(1)}, bf16[400,512]{1,0:T(8,128)(2,1)S(1)}, u32[]{:S(2)}, u32[]{:S(2)}) %collective-permute-start.9) | collective-permute-done | bytes 409632 | tf_op jit(solution)/shard_map/ppermute | solution.py:38
  25.9 2.2 %grad_second.1 = bf16[384,512]{1,0:T(8,128)(2,1)} custom-call(s32[3]{0:T(128)S(1)} %pad_add_fusion.1.ids_ref, bf16[400,512]{1,0:T(8,128)(2,1)S(1)} %collective-permute-done.9.pa_ref, bf16[400,512]{1,0:T(8,128)(2,1)S(1)} %collective-permute-done.10.pb_ref, bf16[512,512]{1,0:T(8,128)(2,1)S(1)} %bitcast.24, bf16[512,512]{1,0:T(8,128)(2,1)S(1)} %bitcast.21, ...), custom_call_target="tpu_custom_call" | custom-call | tf_op jit(solution)/shard_map/grad_second/pallas_call | solution.py:149
  28.1 12.6 %all-to-all-start = ((bf16[16,24,512]{2,1,0:T(8,128)(2,1)}), bf16[16,24,512]{2,1,0:T(8,128)(2,1)}, u32[]{:S(2)}, u32[]{:S(2)}) async-start(bf16[16,24,512]{2,1,0:T(8,128)(2,1)} %bitcast.14), calls=%async_computation | async-start | bytes 786432 | tf_op jit(solution)/shard_map/all_to_all | solution.py:56
  40.7 3.8 %collective-permute-start.2 = (bf16[400,512]{1,0:T(8,128)(2,1)S(1)}, bf16[400,512]{1,0:T(8,128)(2,1)}, u32[]{:S(2)}, u32[]{:S(2)}) collective-permute-start(bf16[400,512]{1,0:T(8,128)(2,1)S(1)} %pad_maximum_fusion.refs_0_.pa_ref), channel_id=1, source_target_pairs={{0,16},{16,32},{32,48},{48,64},{64,80},{80,96},{96,112},{112,128},... | collective-permute-start | bytes 1228808 | tf_op jit(solution)/shard_map/ppermute | solution.py:43
  44.5 25.7 %collective-permute-done.2.refs_2_ = bf16[400,512]{1,0:T(8,128)(2,1)} collective-permute-done((bf16[400,512]{1,0:T(8,128)(2,1)S(1)}, bf16[400,512]{1,0:T(8,128)(2,1)}, u32[]{:S(2)}, u32[]{:S(2)}) %collective-permute-start.2) | collective-permute-done | bytes 409632 | tf_op jit(solution)/shard_map/ppermute | solution.py:43
  72.1 1.9 %collective-permute-start.3 = (bf16[400,512]{1,0:T(8,128)(2,1)}, bf16[400,512]{1,0:T(8,128)(2,1)}, u32[]{:S(2)}, u32[]{:S(2)}) collective-permute-start(bf16[400,512]{1,0:T(8,128)(2,1)} %collective-permute-done.2.refs_2_), channel_id=1, source_target_pairs={{0,8},{8,0},{1,9},{9,1},{2,10},{10,2},{3,11},{11,3},{4,12},{12,4},... | collective-permute-start | bytes 1228808 | tf_op jit(solution)/shard_map/ppermute | solution.py:38
  74.0 9.8 %collective-permute-done.4.refs_4_ = bf16[400,512]{1,0:T(8,128)(2,1)S(1)} collective-permute-done((bf16[400,512]{1,0:T(8,128)(2,1)}, bf16[400,512]{1,0:T(8,128)(2,1)S(1)}, u32[]{:S(2)}, u32[]{:S(2)}) %collective-permute-start.4) | collective-permute-done | bytes 409632 | tf_op jit(solution)/shard_map/ppermute | solution.py:43
  83.9 1.9 %collective-permute-start.5 = (bf16[400,512]{1,0:T(8,128)(2,1)S(1)}, bf16[400,512]{1,0:T(8,128)(2,1)}, u32[]{:S(2)}, u32[]{:S(2)}) collective-permute-start(bf16[400,512]{1,0:T(8,128)(2,1)S(1)} %collective-permute-done.4.refs_4_), channel_id=1, source_target_pairs={{0,8},{8,0},{1,9},{9,1},{2,10},{10,2},{3,11},{11,3},{4,12},{12,4},... | collective-permute-start | bytes 1228808 | tf_op jit(solution)/shard_map/ppermute | solution.py:38
  87.5 13.1 %all-to-all-start.1 = ((bf16[8,24,512]{2,1,0:T(8,128)(2,1)}), bf16[8,24,512]{2,1,0:T(8,128)(2,1)S(1)}, u32[]{:S(2)}, u32[]{:S(2)}) async-start(bf16[8,24,512]{2,1,0:T(8,128)(2,1)} %tally.1), calls=%async_computation.1 | async-start | bytes 393216 | tf_op jit(solution)/shard_map/all_to_all | solution.py:56
  101.6 14.3 %all-to-all-done.1 = bf16[8,24,512]{2,1,0:T(8,128)(2,1)S(1)} async-done(((bf16[8,24,512]{2,1,0:T(8,128)(2,1)}), bf16[8,24,512]{2,1,0:T(8,128)(2,1)S(1)}, u32[]{:S(2)}, u32[]{:S(2)}) %all-to-all-start.1) | async-done | bytes 196640 | tf_op jit(solution)/shard_map/all_to_all | solution.py:56
  119.2 1.9 %collective-permute-start.12 = (bf16[384,512]{1,0:T(8,128)(2,1)S(1)}, bf16[384,512]{1,0:T(8,128)(2,1)S(1)}, u32[]{:S(2)}, u32[]{:S(2)}) collective-permute-start(bf16[384,512]{1,0:T(8,128)(2,1)S(1)} %pad_maximum_fusion.1), channel_id=1, source_target_pairs={{0,240},{8,24},{16,0},{24,40},{32,16},{40,56},{48,32},{56,72},{64,... | collective-permute-start | bytes 1179656 | tf_op jit(solution)/shard_map/ppermute | solution.py:52
  121.2 3.1 %collective-permute-start.13 = (bf16[192,512]{1,0:T(8,128)(2,1)S(1)}, bf16[192,512]{1,0:T(8,128)(2,1)S(1)}, u32[]{:S(2)}, u32[]{:S(2)}) collective-permute-start(bf16[192,512]{1,0:T(8,128)(2,1)S(1)} %maximum_select_fusion.1), channel_id=1, source_target_pairs={{0,224},{8,40},{16,240},{24,56},{32,0},{40,72},{48,16},{56,88},{64... | collective-permute-start | bytes 589832 | tf_op jit(solution)/shard_map/ppermute | solution.py:52
  124.4 3.9 %collective-permute-start.6 = (bf16[256,512]{1,0:T(8,128)(2,1)S(1)}, bf16[256,512]{1,0:T(8,128)(2,1)}, u32[]{:S(2)}, u32[]{:S(2)}) collective-permute-start(bf16[256,512]{1,0:T(8,128)(2,1)S(1)} %maximum_select_fusion), channel_id=1, source_target_pairs={{0,16},{16,32},{32,48},{48,64},{64,80},{80,96},{96,112},{112,128},... | collective-permute-start | bytes 786440 | tf_op jit(solution)/shard_map/ppermute | solution.py:43
  128.9 4.3 %collective-permute-done.13 = bf16[192,512]{1,0:T(8,128)(2,1)S(1)} collective-permute-done((bf16[192,512]{1,0:T(8,128)(2,1)S(1)}, bf16[192,512]{1,0:T(8,128)(2,1)S(1)}, u32[]{:S(2)}, u32[]{:S(2)}) %collective-permute-start.13) | collective-permute-done | bytes 196640 | tf_op jit(solution)/shard_map/ppermute | solution.py:52
  133.2 1.9 %collective-permute-start.14 = (bf16[576,512]{1,0:T(8,128)(2,1)S(1)}, bf16[576,512]{1,0:T(8,128)(2,1)}, u32[]{:S(2)}, u32[]{:S(2)}) collective-permute-start(bf16[576,512]{1,0:T(8,128)(2,1)S(1)} %constant_dynamic-update-slice_fusion.a_ref), channel_id=1, source_target_pairs={{0,8},{8,0},{1,9},{9,1},{2,10},{10,2},{3,11},{11,3},{4,12},{12,4},... | collective-permute-start | bytes 1769480 | tf_op jit(solution)/shard_map/ppermute | solution.py:38
  136.8 4.2 %collective-permute-start.7 = (bf16[256,512]{1,0:T(8,128)(2,1)}, bf16[256,512]{1,0:T(8,128)(2,1)}, u32[]{:S(2)}, u32[]{:S(2)}) collective-permute-start(bf16[256,512]{1,0:T(8,128)(2,1)} %collective-permute-done.6.refs_6_), channel_id=1, source_target_pairs={{0,8},{8,0},{1,9},{9,1},{2,10},{10,2},{3,11},{11,3},{4,12},{12,4},... | collective-permute-start | bytes 786440 | tf_op jit(solution)/shard_map/ppermute | solution.py:38
  140.9 5.6 %collective-permute-start = (bf16[192,512]{1,0:T(8,128)(2,1)}, bf16[192,512]{1,0:T(8,128)(2,1)}, u32[]{:S(2)}, u32[]{:S(2)}) collective-permute-start(bf16[192,512]{1,0:T(8,128)(2,1)} %q_ref.3), channel_id=1, source_target_pairs={{256,0},{272,16},{288,32},{257,1},{273,17},{289,33},{258,2},{274,1... | collective-permute-start | bytes 589832 | tf_op jit(solution)/shard_map/ppermute | solution.py:381
  146.6 3.9 %collective-permute-done.visitor_ref = bf16[192,512]{1,0:T(8,128)(2,1)} collective-permute-done((bf16[192,512]{1,0:T(8,128)(2,1)}, bf16[192,512]{1,0:T(8,128)(2,1)}, u32[]{:S(2)}, u32[]{:S(2)}) %collective-permute-start) | collective-permute-done | bytes 196640 | tf_op jit(solution)/shard_map/ppermute | solution.py:381
  151.5 3.1 %window.1 = (f32[192,512]{1,0:T(8,128)S(1)}, f32[192,128]{1,0:T(8,128)S(1)}, bf16[192,640]{1,0:T(8,128)(2,1)S(1)}) custom-call(s32[4]{0:T(128)S(1)} %pad_add_fusion.info_ref, bf16[192,512]{1,0:T(8,128)(2,1)} %q_ref.3, bf16[192,512]{1,0:T(8,128)(2,1)} %collective-permute-done.visitor_ref, bf16[400,512]{1,0:T(8,128)(2,1)S(1)} %pad_maximum_fusion.refs_0_.pa_ref, ...), custom_call_target="tpu_custom_call" | custom-call | tf_op jit(solution)/shard_map/window/pallas_call | solution.py:284
  156.7 9.6 %collective-permute-done.8.reply_ref = bf16[192,640]{1,0:T(8,128)(2,1)S(1)} collective-permute-done((bf16[192,640]{1,0:T(8,128)(2,1)S(1)}, bf16[192,640]{1,0:T(8,128)(2,1)S(1)}, u32[]{:S(2)}, u32[]{:S(2)}) %collective-permute-start.8) | collective-permute-done | bytes 245792 | tf_op jit(solution)/shard_map/ppermute | solution.py:400
  167.5 8.7 %solve.1 = (f32[192,512]{1,0:T(8,128)S(1)}, f32[8,192]{1,0:T(8,128)S(1)}) custom-call(s32[3]{0:T(128)S(1)} %pad_add_fusion.1.ids_ref, f32[1]{0:T(128)S(6)} %copy.13.gain_ref, bf16[192,512]{1,0:T(8,128)(2,1)} %q_ref.3, bf16[512,512]{1,0:T(8,128)(2,1)S(1)} %bitcast.25, bf16[512,512]{1,0:T(8,128)(2,1)S(1)} %bitcast.22, bf16[512,512]{1,0:T(8,128)(2,1)S(1)} %bitcast.28, ...), custom_call_target="tpu_custom_call" | custom-call | tf_op jit(solution)/shard_map/solve/pallas_call | solution.py:210
  176.3 11.1 %all_to_all.15.sums_ref = f32[8,2,192]{2,1,0:T(2,128)S(1)} all-to-all(f32[8,2,192]{2,1,0:T(2,128)S(1)} %broadcast_in_dim.2), channel_id=1, replica_groups=mesh['xh'=2,'zq'=4,'zm'=2,'zl'=2,'core'=2,'head'=8] {'head'}, dimensions={0} | all-to-all | bytes 24576 | tf_op jit(solution)/shard_map/all_to_all | solution.py:56
  (49 shorter events, 24.2 us)
Async XLA Ops:
  0.6 11.5 %copy-start.3 = (bf16[1,512,512]{2,1,0:T(8,128)(2,1)S(1)}, bf16[1,512,512]{2,1,0:T(8,128)(2,1)}, u32[]{:S(2)}) copy-start(bf16[1,512,512]{2,1,0:T(8,128)(2,1)} %param.13) | copy-start | bytes 1572868
  2.4 11.1 %collective-permute-start.1 = (bf16[400,512]{1,0:T(8,128)(2,1)S(1)}, bf16[400,512]{1,0:T(8,128)(2,1)S(1)}, u32[]{:S(2)}, u32[]{:S(2)}) collective-permute-start(bf16[400,512]{1,0:T(8,128)(2,1)S(1)} %pad_maximum_fusion.refs_0_.pa_ref), channel_id=1, source_target_pairs={{0,8},{8,0},{1,9},{9,1},{2,10},{10,2},{3,11},{11,3},{4,12},{12,4},... | collective-permute-start | bytes 1228808 | tf_op jit(solution)/shard_map/ppermute | solution.py:38
  4.4 17.9 %collective-permute-start.9 = (bf16[400,512]{1,0:T(8,128)(2,1)S(1)}, bf16[400,512]{1,0:T(8,128)(2,1)S(1)}, u32[]{:S(2)}, u32[]{:S(2)}) collective-permute-start(bf16[400,512]{1,0:T(8,128)(2,1)S(1)} %pad_maximum_fusion.refs_0_.pa_ref), channel_id=1, source_target_pairs={{0,256},{256,0},{1,257},{257,1},{2,258},{258,2},{3,259},{259,3},{4... | collective-permute-start | bytes 1228808 | tf_op jit(solution)/shard_map/ppermute | solution.py:38
  12.2 1.0 copy-start.4
  13.2 1.0 copy-start
  22.3 3.6 %collective-permute-start.10 = (bf16[400,512]{1,0:T(8,128)(2,1)S(1)}, bf16[400,512]{1,0:T(8,128)(2,1)S(1)}, u32[]{:S(2)}, u32[]{:S(2)}) collective-permute-start(bf16[400,512]{1,0:T(8,128)(2,1)S(1)} %collective-permute-done.9.pa_ref), channel_id=1, source_target_pairs={{0,8},{8,0},{1,9},{9,1},{2,10},{10,2},{3,11},{11,3},{4,12},{12,4},... | collective-permute-start | bytes 1228808 | tf_op jit(solution)/shard_map/ppermute | solution.py:38
  28.1 57.7 %all-to-all-start = ((bf16[16,24,512]{2,1,0:T(8,128)(2,1)}), bf16[16,24,512]{2,1,0:T(8,128)(2,1)}, u32[]{:S(2)}, u32[]{:S(2)}) async-start(bf16[16,24,512]{2,1,0:T(8,128)(2,1)} %bitcast.14), calls=%async_computation | async-start | bytes 786432 | tf_op jit(solution)/shard_map/all_to_all | solution.py:56
  40.7 29.5 %collective-permute-start.2 = (bf16[400,512]{1,0:T(8,128)(2,1)S(1)}, bf16[400,512]{1,0:T(8,128)(2,1)}, u32[]{:S(2)}, u32[]{:S(2)}) collective-permute-start(bf16[400,512]{1,0:T(8,128)(2,1)S(1)} %pad_maximum_fusion.refs_0_.pa_ref), channel_id=1, source_target_pairs={{0,16},{16,32},{32,48},{48,64},{64,80},{80,96},{96,112},{112,128},... | collective-permute-start | bytes 1228808 | tf_op jit(solution)/shard_map/ppermute | solution.py:43
  70.2 13.7 %collective-permute-start.4 = (bf16[400,512]{1,0:T(8,128)(2,1)}, bf16[400,512]{1,0:T(8,128)(2,1)S(1)}, u32[]{:S(2)}, u32[]{:S(2)}) collective-permute-start(bf16[400,512]{1,0:T(8,128)(2,1)} %collective-permute-done.2.refs_2_), channel_id=1, source_target_pairs={{0,16},{16,32},{32,48},{48,64},{64,80},{80,96},{96,112},{112,128},... | collective-permute-start | bytes 1228808 | tf_op jit(solution)/shard_map/ppermute | solution.py:43
  72.1 78.4 %collective-permute-start.3 = (bf16[400,512]{1,0:T(8,128)(2,1)}, bf16[400,512]{1,0:T(8,128)(2,1)}, u32[]{:S(2)}, u32[]{:S(2)}) collective-permute-start(bf16[400,512]{1,0:T(8,128)(2,1)} %collective-permute-done.2.refs_2_), channel_id=1, source_target_pairs={{0,8},{8,0},{1,9},{9,1},{2,10},{10,2},{3,11},{11,3},{4,12},{12,4},... | collective-permute-start | bytes 1228808 | tf_op jit(solution)/shard_map/ppermute | solution.py:38
  83.9 16.8 %copy-start.1 = (bf16[400,512]{1,0:T(8,128)(2,1)}, bf16[400,512]{1,0:T(8,128)(2,1)S(1)}, u32[]{:S(2)}) copy-start(bf16[400,512]{1,0:T(8,128)(2,1)S(1)} %collective-permute-done.4.refs_4_) | copy-start | bytes 1228804
  83.9 16.8 %collective-permute-start.5 = (bf16[400,512]{1,0:T(8,128)(2,1)S(1)}, bf16[400,512]{1,0:T(8,128)(2,1)}, u32[]{:S(2)}, u32[]{:S(2)}) collective-permute-start(bf16[400,512]{1,0:T(8,128)(2,1)S(1)} %collective-permute-done.4.refs_4_), channel_id=1, source_target_pairs={{0,8},{8,0},{1,9},{9,1},{2,10},{10,2},{3,11},{11,3},{4,12},{12,4},... | collective-permute-start | bytes 1228808 | tf_op jit(solution)/shard_map/ppermute | solution.py:38
  87.5 28.3 %all-to-all-start.1 = ((bf16[8,24,512]{2,1,0:T(8,128)(2,1)}), bf16[8,24,512]{2,1,0:T(8,128)(2,1)S(1)}, u32[]{:S(2)}, u32[]{:S(2)}) async-start(bf16[8,24,512]{2,1,0:T(8,128)(2,1)} %tally.1), calls=%async_computation.1 | async-start | bytes 393216 | tf_op jit(solution)/shard_map/all_to_all | solution.py:56
  115.9 3.3 %collective-permute-start.11 = (bf16[192,512]{1,0:T(8,128)(2,1)S(1)}, bf16[192,512]{1,0:T(8,128)(2,1)S(1)}, u32[]{:S(2)}, u32[]{:S(2)}) collective-permute-start(bf16[192,512]{1,0:T(8,128)(2,1)S(1)} %bitcast.29), channel_id=1, source_target_pairs={{0,8},{8,0},{1,9},{9,1},{2,10},{10,2},{3,11},{11,3},{4,12},{12,4},... | collective-permute-start | bytes 589832 | tf_op jit(solution)/shard_map/ppermute | solution.py:38
  119.2 9.7 %collective-permute-start.12 = (bf16[384,512]{1,0:T(8,128)(2,1)S(1)}, bf16[384,512]{1,0:T(8,128)(2,1)S(1)}, u32[]{:S(2)}, u32[]{:S(2)}) collective-permute-start(bf16[384,512]{1,0:T(8,128)(2,1)S(1)} %pad_maximum_fusion.1), channel_id=1, source_target_pairs={{0,240},{8,24},{16,0},{24,40},{32,16},{40,56},{48,32},{56,72},{64,... | collective-permute-start | bytes 1179656 | tf_op jit(solution)/shard_map/ppermute | solution.py:52
  121.2 12.0 %collective-permute-start.13 = (bf16[192,512]{1,0:T(8,128)(2,1)S(1)}, bf16[192,512]{1,0:T(8,128)(2,1)S(1)}, u32[]{:S(2)}, u32[]{:S(2)}) collective-permute-start(bf16[192,512]{1,0:T(8,128)(2,1)S(1)} %maximum_select_fusion.1), channel_id=1, source_target_pairs={{0,224},{8,40},{16,240},{24,56},{32,0},{40,72},{48,16},{56,88},{64... | collective-permute-start | bytes 589832 | tf_op jit(solution)/shard_map/ppermute | solution.py:52
  124.4 12.4 %collective-permute-start.6 = (bf16[256,512]{1,0:T(8,128)(2,1)S(1)}, bf16[256,512]{1,0:T(8,128)(2,1)}, u32[]{:S(2)}, u32[]{:S(2)}) collective-permute-start(bf16[256,512]{1,0:T(8,128)(2,1)S(1)} %maximum_select_fusion), channel_id=1, source_target_pairs={{0,16},{16,32},{32,48},{48,64},{64,80},{80,96},{96,112},{112,128},... | collective-permute-start | bytes 786440 | tf_op jit(solution)/shard_map/ppermute | solution.py:43
  133.2 34.3 %collective-permute-start.14 = (bf16[576,512]{1,0:T(8,128)(2,1)S(1)}, bf16[576,512]{1,0:T(8,128)(2,1)}, u32[]{:S(2)}, u32[]{:S(2)}) collective-permute-start(bf16[576,512]{1,0:T(8,128)(2,1)S(1)} %constant_dynamic-update-slice_fusion.a_ref), channel_id=1, source_target_pairs={{0,8},{8,0},{1,9},{9,1},{2,10},{10,2},{3,11},{11,3},{4,12},{12,4},... | collective-permute-start | bytes 1769480 | tf_op jit(solution)/shard_map/ppermute | solution.py:38
  136.8 13.8 %collective-permute-start.7 = (bf16[256,512]{1,0:T(8,128)(2,1)}, bf16[256,512]{1,0:T(8,128)(2,1)}, u32[]{:S(2)}, u32[]{:S(2)}) collective-permute-start(bf16[256,512]{1,0:T(8,128)(2,1)} %collective-permute-done.6.refs_6_), channel_id=1, source_target_pairs={{0,8},{8,0},{1,9},{9,1},{2,10},{10,2},{3,11},{11,3},{4,12},{12,4},... | collective-permute-start | bytes 786440 | tf_op jit(solution)/shard_map/ppermute | solution.py:38
  140.9 9.6 %collective-permute-start = (bf16[192,512]{1,0:T(8,128)(2,1)}, bf16[192,512]{1,0:T(8,128)(2,1)}, u32[]{:S(2)}, u32[]{:S(2)}) collective-permute-start(bf16[192,512]{1,0:T(8,128)(2,1)} %q_ref.3), channel_id=1, source_target_pairs={{256,0},{272,16},{288,32},{257,1},{273,17},{289,33},{258,2},{274,1... | collective-permute-start | bytes 589832 | tf_op jit(solution)/shard_map/ppermute | solution.py:381
  150.5 1.0 copy-start.2
  154.6 11.7 %collective-permute-start.8 = (bf16[192,640]{1,0:T(8,128)(2,1)S(1)}, bf16[192,640]{1,0:T(8,128)(2,1)S(1)}, u32[]{:S(2)}, u32[]{:S(2)}) collective-permute-start(bf16[192,640]{1,0:T(8,128)(2,1)S(1)} %get-tuple-element.13), channel_id=1, source_target_pairs={{0,256},{16,272},{32,288},{1,257},{17,273},{33,289},{2,258},{18,27... | collective-permute-start | bytes 737288 | tf_op jit(solution)/shard_map/ppermute | solution.py:400

commit v4 on v3

--- a/solution.py
+++ b/solution.py
@@ -10,6 +10,7 @@
 
 HEADS = 8
 HD = 512
+FH = 512
 WINDOW = 1024
 NS_STEPS = 2
 TOK = 192
@@ -43,12 +44,12 @@
     return lax.ppermute(x, RING, [(i, (i + 1) % count) for i in range(count)])
 
 
-def around(x, by):
+def around(x, down, up):
     count = lax.axis_size(RING)
     pairs = []
     for i in range(count):
-        pairs.append((2 * i, 2 * ((i - by) % count)))
-        pairs.append((2 * i + 1, 2 * ((i + by) % count) + 1))
+        pairs.append((2 * i, 2 * ((i + down) % count)))
+        pairs.append((2 * i + 1, 2 * ((i + up) % count) + 1))
     return lax.ppermute(x, RING + ("core",), pairs)
 
 
@@ -68,6 +69,10 @@
     return pltpu.with_memory_space_constraint(x, pltpu.MemorySpace.VMEM)
 
 
+def distant(x):
+    return pltpu.with_memory_space_constraint(x, pltpu.MemorySpace.HBM)
+
+
 def near_out(shape, dtype):
     return pltpu.MemorySpace.VMEM(shape, dtype)
 
@@ -77,7 +82,7 @@
 
 
 VMEM = pl.BlockSpec(memory_space=pltpu.VMEM)
-SMEM = pl.BlockSpec(memory_space=pltpu.SMEM)
+HBM = pl.BlockSpec(memory_space=pltpu.MemorySpace.HBM)
 
 
 def in_lanes(dtype, *columns):
@@ -88,6 +93,37 @@
     return out.astype(dtype)
 
 
+def pack_kernel(k_ref, v_ref, rate_ref, out_ref, row_ref, sems):
+    copies = [
+        pltpu.make_async_copy(k_ref, out_ref.at[0:TOK], sems.at[0]),
+        pltpu.make_async_copy(v_ref, out_ref.at[TOK : 2 * TOK], sems.at[1]),
+        pltpu.make_async_copy(rate_ref, row_ref, sems.at[2]),
+    ]
+    for copy in copies:
+        copy.start()
+    copies[2].wait()
+    rate = jnp.broadcast_to(row_ref[...], (16, TOK))
+    high = rate.astype(jnp.bfloat16).astype(jnp.float32)
+    line = lax.broadcasted_iota(jnp.int32, (16, TOK), 0)
+    extra = jnp.where(line == 0, high, jnp.where(line == 1, rate - high, 0.0))
+    out_ref[2 * TOK : 2 * TOK + 16, :] = jnp.zeros((16, HD), jnp.bfloat16)
+    out_ref[2 * TOK : 2 * TOK + 16, 0:TOK] = extra.astype(jnp.bfloat16)
+    copies[0].wait()
+    copies[1].wait()
+
+
+def pack(k, v, rate):
+    return pl.pallas_call(
+        pack_kernel,
+        out_shape=near_out((2 * TOK + 16, HD), jnp.bfloat16),
+        in_specs=[HBM] * 3,
+        out_specs=VMEM,
+        scratch_shapes=[pltpu.VMEM((1, TOK), jnp.float32), pltpu.SemaphoreType.DMA((3,))],
+        compiler_params=pltpu.CompilerParams(vmem_limit_bytes=4 << 20),
+        name="pack",
+    )(*[distant(x) for x in (k, v, rate)])
+
+
 def tally_kernel(pieces_ref, out_ref):
     total = jnp.sum(pieces_ref[...].astype(jnp.float32), axis=0).astype(jnp.bfloat16)
     for i in range(out_ref.shape[0]):
@@ -100,22 +136,23 @@
         out_shape=jax.ShapeDtypeStruct((copies,) + pieces.shape[1:], jnp.bfloat16),
         in_specs=[VMEM],
         out_specs=VMEM,
-        compiler_params=pltpu.CompilerParams(vmem_limit_bytes=8 << 20),
+        compiler_params=pltpu.CompilerParams(vmem_limit_bytes=4 << 20),
         name="tally",
     )(pieces)
 
 
-def grad_kernel(first, ids_ref, pa_ref, pb_ref, w1_ref, w3_ref, w2_ref, *rest):
+def grad_kernel(first, pa_ref, pb_ref, w1_ref, w3_ref, w2_ref, *rest):
     if first:
         (out_ref,) = rest
     else:
-        sofar_ref, out_ref = rest
-    mine = pl.ds(pl.multiple_of(ids_ref[0] * PART, PART), PART)
+        sofar_ref, out_ref, held_ref, sems = rest
+    part = lax.axis_index("xh") * 2 + lax.axis_index("core")
+    mine = pl.ds(pl.multiple_of(part * PART, PART), PART)
     w13 = jnp.concatenate([w1_ref[mine, :], w3_ref[mine, :]], axis=0)
     w2 = w2_ref[mine, :]
     ones = jnp.ones((8, HD), jnp.bfloat16)
     g13 = None
-    g2 = None
+    later = []
     for ref in (pa_ref, pb_ref):
         k = ref[0:TOK, :]
         v = ref[TOK : 2 * TOK, :]
@@ -130,75 +167,103 @@
         s = sigmoid(a)
         u = a * s
         dh = nt(w2, v) * rate
-        hid = (u * b * rate).astype(jnp.bfloat16)
+        later.append(((u * b * rate).astype(jnp.bfloat16), v))
         d1 = (dh * b * s * (1.0 + a * (1.0 - s)) * scale).astype(jnp.bfloat16)
         d3 = (dh * u * scale).astype(jnp.bfloat16)
         p13 = nn(jnp.concatenate([d1, d3], axis=0), k)
-        p2 = nn(hid, v)
         g13 = p13 if g13 is None else g13 + p13
-        g2 = p2 if g2 is None else g2 + p2
     if first:
         out_ref[0 : 2 * PART, :] = g13
-        out_ref[2 * PART : ROWS, :] = g2
-    else:
-        out_ref[0 : 2 * PART, :] = (g13 + sofar_ref[0 : 2 * PART, :]).astype(jnp.bfloat16)
-        out_ref[2 * PART : ROWS, :] = (g2 + sofar_ref[2 * PART : ROWS, :]).astype(jnp.bfloat16)
-
-
-def gradients(first, ids, *arrays):
+        out_ref[2 * PART : ROWS, :] = nn(*later[0]) + nn(*later[1])
+        return
+    copies = [
+        pltpu.make_async_copy(held_ref.at[rows], out_ref.at[rows], sems.at[i])
+        for i, rows in enumerate((pl.ds(0, 2 * PART), pl.ds(2 * PART, PART)))
+    ]
+    held_ref[0 : 2 * PART, :] = (g13 + sofar_ref[0 : 2 * PART, :]).astype(jnp.bfloat16)
+    copies[0].start()
+    g2 = nn(*later[0]) + nn(*later[1])
+    held_ref[2 * PART : ROWS, :] = (g2 + sofar_ref[2 * PART : ROWS, :]).astype(jnp.bfloat16)
+    copies[1].start()
+    for copy in copies:
+        copy.wait()
+
+
+def gradients(first, *arrays):
+    extra = [pltpu.VMEM((ROWS, HD), jnp.bfloat16), pltpu.SemaphoreType.DMA((2,))]
     return pl.pallas_call(
         functools.partial(grad_kernel, first),
         out_shape=near_out((ROWS, HD), jnp.float32)
         if first
         else jax.ShapeDtypeStruct((ROWS, HD), jnp.bfloat16),
-        in_specs=[SMEM] + [VMEM] * len(arrays),
-        out_specs=VMEM,
-        compiler_params=pltpu.CompilerParams(vmem_limit_bytes=16 << 20),
+        in_specs=[VMEM] * len(arrays),
+        out_specs=VMEM if first else HBM,
+        scratch_shapes=[] if first else extra,
+        compiler_params=pltpu.CompilerParams(vmem_limit_bytes=6 << 20),
         name="grad_first" if first else "grad_second",
-    )(ids, *[near(x) for x in arrays])
+    )(*[near(x) for x in arrays])
 
 
 def solve_kernel(
-    ids_ref, gain_ref, q_ref, w1_ref, w3_ref, w2_ref, h_ref, hx_ref, a_ref, ax_ref, o_ref, sq_ref, all_ref
+    q_ref, w1_ref, w3_ref, w2_ref, *refs
 ):
-    core = ids_ref[1]
-    place = ids_ref[2]
-
-    def put(ref, row, which, plane, turn):
-        start = (plane * 2 + which) * ROWS + lax.rem(place + turn, 4) * BIT
-        all_ref[pl.ds(pl.multiple_of(start, 32), BIT), :] = ref[row : row + BIT, :]
-
-    for plane in range(2):
-        put(h_ref, plane * BIT, core, plane, 0)
-        put(hx_ref, plane * BIT, 1 - core, plane, 0)
-        put(a_ref, plane * BIT, core, plane, 1 + 2 * core)
-        put(a_ref, (2 + plane) * BIT, 1 - core, plane, 1 + 2 * core)
-        put(ax_ref, plane * BIT, 1 - core, plane, 3 + 2 * core)
-        put(ax_ref, (2 + plane) * BIT, core, plane, 3 + 2 * core)
-    put(a_ref, 4 * BIT, core, core, 2)
-    put(a_ref, 5 * BIT, 1 - core, core, 2)
-    put(ax_ref, 4 * BIT, 1 - core, 1 - core, 2)
-    put(ax_ref, 5 * BIT, core, 1 - core, 2)
+    blocks = refs[:4]
+    scale_ref, o_ref, sq_ref, all_ref, w_ref, query_ref, sems = refs[4:]
+    copies = [
+        pltpu.make_async_copy(src, dst, sems.at[i])
+        for i, (src, dst) in enumerate(
+            (
+                (w1_ref, w_ref.at[0]),
+                (w3_ref, w_ref.at[1]),
+                (w2_ref, w_ref.at[2]),
+                (q_ref, query_ref),
+            )
+        )
+    ]
+    for copy in copies:
+        copy.start()
+    core = lax.axis_index("core")
+    place = lax.rem(lax.axis_index(RING), 4)
+
+    def put(ref, row, which, turn):
+        for plane in range(2):
+            start = (plane * 2 + which) * ROWS + lax.rem(place + turn, 4) * BIT
+            source = row + plane * BIT
+            all_ref[pl.ds(pl.multiple_of(start, 32), BIT), :] = ref[source : source + BIT, :]
+
+    for which, (near_ref, far_ref) in ((core, blocks[:2]), (1 - core, blocks[2:])):
+        put(near_ref, 0, which, 0)
+        for i, turn in enumerate((3, 1, 2)):
+            put(far_ref, 2 * i * BIT, which, turn)
     fresh = []
-    for m, w_ref in enumerate((w1_ref, w3_ref, w2_ref)):
+    for m in range(3):
         g = jnp.concatenate(
             [all_ref[i * ROWS + m * PART : i * ROWS + (m + 1) * PART, :] for i in range(4)], axis=0
         ).astype(jnp.float32)
         norm = jnp.sqrt(jnp.sum(g * g, keepdims=True)) + 1e-07
-        x = (g / norm).astype(jnp.bfloat16)
-        for _ in range(NS_STEPS):
-            gram = nt(x, x).astype(jnp.bfloat16)
-            mixer = (COEF_B * gram.astype(jnp.float32) + COEF_C * nn(gram, gram)).astype(
-                jnp.bfloat16
-            )
-            x = (COEF_A * x.astype(jnp.float32) + nn(mixer, x)).astype(jnp.bfloat16)
-        fresh.append((w_ref[...].astype(jnp.float32) - x.astype(jnp.float32)).astype(jnp.bfloat16))
-    q = q_ref[...].astype(jnp.float32)
+        fresh.append((g * (1.0 / norm)).astype(jnp.bfloat16))
+    for _ in range(NS_STEPS):
+        grams = [nt(x, x).astype(jnp.bfloat16) for x in fresh]
+        mixers = [
+            (COEF_B * gram.astype(jnp.float32) + COEF_C * nn(gram, gram)).astype(jnp.bfloat16)
+            for gram in grams
+        ]
+        fresh = [
+            (COEF_A * x.astype(jnp.float32) + nn(mixer, x)).astype(jnp.bfloat16)
+            for x, mixer in zip(fresh, mixers)
+        ]
+    for copy in copies:
+        copy.wait()
+    fresh = [
+        (w_ref[m].astype(jnp.float32) - x.astype(jnp.float32)).astype(jnp.bfloat16)
+        for m, x in enumerate(fresh)
+    ]
+    q = query_ref[...].astype(jnp.float32)
     qn = (q * lax.rsqrt(jnp.mean(q * q, axis=-1, keepdims=True) + EPSILON)).astype(jnp.bfloat16)
     h1 = nt(qn, fresh[0])
     h3 = nt(qn, fresh[1])
     hidden = (h1 * sigmoid(h1) * h3).astype(jnp.bfloat16)
-    o = nn(hidden, fresh[2]) * gain_ref[0]
+    o = nn(hidden, fresh[2]) * scale_ref[...]
     o_ref[...] = o
     sq_ref[...] = lax.dot_general(
         jnp.ones((8, HD), jnp.float32), o * o, NT,
@@ -206,16 +271,21 @@
     )
 
 
-def solve(ids, gain, *arrays):
+def solve(outside, inside):
     return pl.pallas_call(
         solve_kernel,
         out_shape=(near_out((TOK, HD), jnp.float32), near_out((8, TOK), jnp.float32)),
-        in_specs=[SMEM, SMEM] + [VMEM] * len(arrays),
+        in_specs=[HBM] * len(outside) + [VMEM] * len(inside),
         out_specs=(VMEM, VMEM),
-        scratch_shapes=[pltpu.VMEM((4 * ROWS, HD), jnp.bfloat16)],
-        compiler_params=pltpu.CompilerParams(vmem_limit_bytes=28 << 20),
+        scratch_shapes=[
+            pltpu.VMEM((4 * ROWS, HD), jnp.bfloat16),
+            pltpu.VMEM((3, FH, HD), jnp.bfloat16),
+            pltpu.VMEM((TOK, HD), jnp.bfloat16),
+            pltpu.SemaphoreType.DMA((4,)),
+        ],
+        compiler_params=pltpu.CompilerParams(vmem_limit_bytes=14 << 20),
         name="solve",
-    )(ids, gain, *[near(x) for x in arrays])
+    )(*[distant(x) for x in outside], *[near(x) for x in inside])
 
 
 def attend(q, blocks, core, start, foreign):
@@ -258,12 +328,13 @@
     return o, top, total
 
 
-def window_kernel(info_ref, q_ref, visitor_ref, *refs):
+def window_kernel(q_ref, visitor_ref, *refs):
     blocks = refs[:8]
     o_ref, stat_ref, reply_ref = refs[8:]
-    core = info_ref[0]
-    start = info_ref[1]
-    hosts = info_ref[2] == 1
+    core = lax.axis_index("core")
+    z = lax.axis_index(RING)
+    start = z * 2 + core
+    hosts = (lax.axis_index("xh") == 0) & (z < SPAN)
     o, top, total = attend(q_ref[...], blocks, core, start, False)
     o_ref[...] = o
     stat_ref[...] = in_lanes(jnp.float32, top, total)
@@ -280,7 +351,7 @@
         reply_ref[...] = jnp.zeros_like(reply_ref)
 
 
-def window_attention(info, *arrays):
+def window_attention(*arrays):
     return pl.pallas_call(
         window_kernel,
         out_shape=(
@@ -288,15 +359,15 @@
             near_out((TOK, 128), jnp.float32),
             near_out((TOK, HD + 128), jnp.bfloat16),
         ),
-        in_specs=[SMEM] + [VMEM] * len(arrays),
+        in_specs=[VMEM] * len(arrays),
         out_specs=(VMEM, VMEM, VMEM),
-        compiler_params=pltpu.CompilerParams(vmem_limit_bytes=24 << 20),
+        compiler_params=pltpu.CompilerParams(vmem_limit_bytes=10 << 20),
         name="window",
-    )(info, *[near(x) for x in arrays])
-
-
-def merge_kernel(info_ref, o_ref, stat_ref, reply_ref, out_ref, sq_ref):
-    guest = info_ref[3] == 1
+    )(*[near(x) for x in arrays])
+
+
+def merge_kernel(o_ref, stat_ref, reply_ref, out_ref, sq_ref):
+    guest = (lax.axis_index("xh") == 1) & (lax.axis_index(RING) < SPAN)
     top = stat_ref[:, 0:1]
     total = stat_ref[:, 1:2]
     far_stat = reply_ref[:, HD : HD + 128].astype(jnp.float32)
@@ -314,15 +385,15 @@
     )
 
 
-def merge(info, *arrays):
+def merge(*arrays):
     return pl.pallas_call(
         merge_kernel,
         out_shape=(near_out((TOK, HD), jnp.float32), near_out((8, TOK), jnp.float32)),
-        in_specs=[SMEM] + [VMEM] * len(arrays),
+        in_specs=[VMEM] * len(arrays),
         out_specs=(VMEM, VMEM),
-        compiler_params=pltpu.CompilerParams(vmem_limit_bytes=8 << 20),
+        compiler_params=pltpu.CompilerParams(vmem_limit_bytes=4 << 20),
         name="merge",
-    )(info, *[near(x) for x in arrays])
+    )(*[near(x) for x in arrays])
 
 
 def finish_kernel(sums_ref, a_ref, o_ref, wo_ref, fo_ref):
@@ -346,24 +417,15 @@
         ),
         in_specs=[VMEM] * 3,
         out_specs=(VMEM, VMEM),
-        compiler_params=pltpu.CompilerParams(vmem_limit_bytes=8 << 20),
+        compiler_params=pltpu.CompilerParams(vmem_limit_bytes=4 << 20),
         name="finish",
     )(*[near(x) for x in arrays])
 
 
 def local(queries, key_rows, value_rows, token_rates, fast_one, fast_three, fast_two, head_gain):
-    xh = lax.axis_index("xh")
-    z = lax.axis_index(RING)
     core = lax.axis_index("core")
-    ids = jnp.stack([xh * 2 + core, core, lax.rem(z, 4)]).astype(jnp.int32)
-    edge = (z < SPAN).astype(jnp.int32)
-    info = jnp.stack([core, z * 2 + core, (1 - xh) * edge, xh * edge]).astype(jnp.int32)
-
-    rate = token_rates[:, 0]
-    high = lax.reduce_precision(rate, 8, 7)
-    extra = jnp.stack([high, rate - high]).astype(jnp.bfloat16)
-    extra = jnp.pad(extra, ((0, 14), (0, HD - TOK)))
-    own = jnp.concatenate([key_rows, value_rows, extra], axis=0)
+    gain = jnp.broadcast_to(head_gain.reshape(1, 1), (1, HD))
+    own = pack(key_rows, value_rows, token_rates.T)
 
     deep = lax.axis_size(RING)
     own_x = swapped(own, "core")
@@ -372,10 +434,10 @@
     w1t = fast_one[0].T
     w3t = fast_three[0].T
     w2 = fast_two[0]
-    sofar = gradients(True, ids, own, own_x, w1t, w3t, w2)
+    sofar = gradients(True, own, own_x, w1t, w3t, w2)
     across, sofar = lax.optimization_barrier((across, sofar))
     across_x = swapped(across, "core")
-    partial = gradients(False, ids, across, across_x, w1t, w3t, w2, sofar)
+    partial = gradients(False, across, across_x, w1t, w3t, w2, sofar)
     pieces = exchanged(partial.reshape(16, ROWS // 16, HD), SAME)
 
     visitor = lax.ppermute(queries, CHIPS, [(deep + i, i) for i in range(SPAN)])
@@ -395,26 +457,20 @@
     spread = tally(pieces, 8)
     mine = exchanged(spread, KIN).reshape(2 * BIT, HD)
     seen, stats, answer = window_attention(
-        info, queries, visitor, own, own_x, back1, back1_x, back2, back2_x, back3, back3_x
+        queries, visitor, own, own_x, back1, back1_x, back2, back2_x, back3, back3_x
     )
     reply = lax.ppermute(answer, CHIPS, [(i, deep + i) for i in range(SPAN)])
-    attended, attended_sq = merge(info, seen, stats, reply)
-
+    attended, attended_sq = merge(seen, stats, reply)
+
+    above = around(mine, 1, 1)
+    below = around(mine, -1, -1)
+    beyond = around(mine, -2, 2)
     mine_x = swapped(mine, "core")
-    beside = around(jnp.concatenate([mine, mine_x]), 1)
-    beyond = around(
-        jnp.where(
-            core == 0,
-            jnp.concatenate([mine[:BIT], mine_x[:BIT]]),
-            jnp.concatenate([mine[BIT:], mine_x[BIT:]]),
-        ),
-        2,
-    )
-    held = jnp.concatenate([beside, beyond])
+    held = jnp.concatenate([above, below, beyond])
     held_x = swapped(held, "core")
 
     fast, fast_sq = solve(
-        ids, head_gain, queries, w1t, w3t, w2, mine, mine_x, held, held_x
+        (queries, w1t, w3t, w2), (mine, held, mine_x, held_x, gain)
     )
     sums = jnp.concatenate([attended_sq[0:1], fast_sq[0:1]], axis=0)
     sums = exchanged(jnp.broadcast_to(sums[None], (HEADS,) + sums.shape), "head")

time: 190 us -> 170 us (0.89)
  waiting for transfers between devices: 79.4 us -> 65.5 us
  Pallas kernels: 19.6 us -> 16.1 us
  starting transfers between devices: 70.9 us -> 73.3 us
  local copies, waits for them, and re-layouts: 3.99 us -> 1.73 us
  other arithmetic: 2.14 us -> 0.08 us
    ppermute x3, waiting for transfers between devices: 37.1 us -> 25.6 us  [forwarded(): return lax.ppermute(x, RING, [(i, (i + 1) % count) for i in range(count)])]
    ppermute x2 -> x3, starting transfers between devices: 4.99 us -> 9.29 us  [around(): return lax.ppermute(x, RING + ('core',), pairs)]
    all_to_all x2, waiting for transfers between devices: 14.3 us -> 10.8 us  [exchanged(): return lax.all_to_all(x, axes, 0, 0)]
    ppermute x2 -> x3, waiting for transfers between devices: 4.89 us -> 7.86 us  [around(): return lax.ppermute(x, RING + ('core',), pairs)]
    ppermute x1, waiting for transfers between devices: 9.61 us -> 7.68 us  [local(): reply = lax.ppermute(answer, CHIPS, [(i, deep + i) for i in range(SPAN)])]
  transfers between devices with their start and end apart: 17 -> 18, of which waited for: 11 -> 7; matrix products, arithmetic and copies ran while one was open for 1% -> 0% of each run, Pallas kernels for 4% -> 3%
where the time goes in v4:
time: 170 us; the launch traced here: 169 us
  starting transfers between devices  73.3 us (43%)
  waiting for transfers between devices  65.5 us (39%)
  Pallas kernels  16.1 us (9%)
  blocking collectives  11.1 us (7%)
  local copies, waits for them, and re-layouts  1.73 us (1%)
    all_to_all x2, starting transfers between devices, exchanged(): return lax.all_to_all(x, axes, 0, 0)  26.4 us
    ppermute x3, waiting for transfers between devices, forwarded(): return lax.ppermute(x, RING, [(i, (i + 1) % count) for i in range(count)])  25.6 us
    ppermute x8, starting transfers between devices, swapped(): return lax.ppermute(x, axis, [(0, 1), (1, 0)])  22.5 us
    all_to_all x1, blocking collectives, exchanged(): return lax.all_to_all(x, axes, 0, 0)  11.1 us
    all_to_all x2, waiting for transfers between devices, exchanged(): return lax.all_to_all(x, axes, 0, 0)  10.8 us
    ppermute x3, starting transfers between devices, around(): return lax.ppermute(x, RING + ('core',), pairs)  9.29 us
    ppermute x8, waiting for transfers between devices, swapped(): return lax.ppermute(x, axis, [(0, 1), (1, 0)])  9.29 us
    ppermute x3, starting transfers between devices, forwarded(): return lax.ppermute(x, RING, [(i, (i + 1) % count) for i in range(count)])  8.77 us
  transfers between devices with their start and end apart: 18, of which 7 were waited for; matrix products, arithmetic and copies ran while one was open for 0% of the time, Pallas kernels for 3%

profile of v4, /device:TPU:4, one launch (start us, length us, event | category | flops | bytes accessed | tf_op | source)
XLA Modules:
  0.0 169.5 jit_solution(16151925491030716206)
XLA Ops:
  1.8 2.1 %collective-permute-start.1 = (bf16[400,512]{1,0:T(8,128)(2,1)S(1)}, bf16[400,512]{1,0:T(8,128)(2,1)S(1)}, u32[]{:S(2)}, u32[]{:S(2)}) collective-permute-start(bf16[400,512]{1,0:T(8,128)(2,1)S(1)} %pack.1.refs_0_.pa_ref), channel_id=1, source_target_pairs={{0,8},{8,0},{1,9},{9,1},{2,10},{10,2},{3,11},{11,3},{4,12},{12,4},... | collective-permute-start | bytes 1228808 | tf_op jit(solution)/shard_map/ppermute | solution.py:39
  3.8 7.8 %collective-permute-start.9 = (bf16[400,512]{1,0:T(8,128)(2,1)S(1)}, bf16[400,512]{1,0:T(8,128)(2,1)S(1)}, u32[]{:S(2)}, u32[]{:S(2)}) collective-permute-start(bf16[400,512]{1,0:T(8,128)(2,1)S(1)} %pack.1.refs_0_.pa_ref), channel_id=1, source_target_pairs={{0,256},{256,0},{1,257},{257,1},{2,258},{258,2},{3,259},{259,3},{4... | collective-permute-start | bytes 1228808 | tf_op jit(solution)/shard_map/ppermute | solution.py:39
  14.2 7.6 %collective-permute-done.9.pa_ref = bf16[400,512]{1,0:T(8,128)(2,1)S(1)} collective-permute-done((bf16[400,512]{1,0:T(8,128)(2,1)S(1)}, bf16[400,512]{1,0:T(8,128)(2,1)S(1)}, u32[]{:S(2)}, u32[]{:S(2)}) %collective-permute-start.9) | collective-permute-done | bytes 409632 | tf_op jit(solution)/shard_map/ppermute | solution.py:39
  26.9 12.6 %all-to-all-start = ((bf16[16,24,512]{2,1,0:T(8,128)(2,1)}), bf16[16,24,512]{2,1,0:T(8,128)(2,1)S(1)}, u32[]{:S(2)}, u32[]{:S(2)}) async-start(bf16[16,24,512]{2,1,0:T(8,128)(2,1)} %bitcast.8), calls=%async_computation | async-start | bytes 786432 | tf_op jit(solution)/shard_map/all_to_all | solution.py:57
  39.5 3.8 %collective-permute-start.2 = (bf16[400,512]{1,0:T(8,128)(2,1)S(1)}, bf16[400,512]{1,0:T(8,128)(2,1)S(1)}, u32[]{:S(2)}, u32[]{:S(2)}) collective-permute-start(bf16[400,512]{1,0:T(8,128)(2,1)S(1)} %pack.1.refs_0_.pa_ref), channel_id=1, source_target_pairs={{0,16},{16,32},{32,48},{48,64},{64,80},{80,96},{96,112},{112,128},... | collective-permute-start | bytes 1228808 | tf_op jit(solution)/shard_map/ppermute | solution.py:44
  43.4 25.6 %collective-permute-done.2.refs_2_ = bf16[400,512]{1,0:T(8,128)(2,1)S(1)} collective-permute-done((bf16[400,512]{1,0:T(8,128)(2,1)S(1)}, bf16[400,512]{1,0:T(8,128)(2,1)S(1)}, u32[]{:S(2)}, u32[]{:S(2)}) %collective-permute-start.2) | collective-permute-done | bytes 409632 | tf_op jit(solution)/shard_map/ppermute | solution.py:44
  71.6 13.7 %all-to-all-start.1 = ((bf16[8,24,512]{2,1,0:T(8,128)(2,1)}), bf16[8,24,512]{2,1,0:T(8,128)(2,1)S(1)}, u32[]{:S(2)}, u32[]{:S(2)}) async-start(bf16[8,24,512]{2,1,0:T(8,128)(2,1)} %tally.1), calls=%async_computation.1 | async-start | bytes 393216 | tf_op jit(solution)/shard_map/all_to_all | solution.py:57
  85.3 1.9 %collective-permute-start.3 = (bf16[400,512]{1,0:T(8,128)(2,1)S(1)}, bf16[400,512]{1,0:T(8,128)(2,1)}, u32[]{:S(2)}, u32[]{:S(2)}) collective-permute-start(bf16[400,512]{1,0:T(8,128)(2,1)S(1)} %collective-permute-done.2.refs_2_), channel_id=1, source_target_pairs={{0,8},{8,0},{1,9},{9,1},{2,10},{10,2},{3,11},{11,3},{4,12},{12,4},... | collective-permute-start | bytes 1228808 | tf_op jit(solution)/shard_map/ppermute | solution.py:39
  87.3 2.4 %collective-permute-start.5 = (bf16[400,512]{1,0:T(8,128)(2,1)S(1)}, bf16[400,512]{1,0:T(8,128)(2,1)S(1)}, u32[]{:S(2)}, u32[]{:S(2)}) collective-permute-start(bf16[400,512]{1,0:T(8,128)(2,1)S(1)} %collective-permute-done.4.refs_4_), channel_id=1, source_target_pairs={{0,8},{8,0},{1,9},{9,1},{2,10},{10,2},{3,11},{11,3},{4,12},{12,4},... | collective-permute-start | bytes 1228808 | tf_op jit(solution)/shard_map/ppermute | solution.py:39
  89.7 10.7 %all-to-all-done.1 = bf16[8,24,512]{2,1,0:T(8,128)(2,1)S(1)} async-done(((bf16[8,24,512]{2,1,0:T(8,128)(2,1)}), bf16[8,24,512]{2,1,0:T(8,128)(2,1)S(1)}, u32[]{:S(2)}, u32[]{:S(2)}) %all-to-all-start.1) | async-done | bytes 196640 | tf_op jit(solution)/shard_map/all_to_all | solution.py:57
  100.5 4.2 %collective-permute-start.11 = (bf16[192,512]{1,0:T(8,128)(2,1)S(1)}, bf16[192,512]{1,0:T(8,128)(2,1)S(1)}, u32[]{:S(2)}, u32[]{:S(2)}) collective-permute-start(bf16[192,512]{1,0:T(8,128)(2,1)S(1)} %bitcast.21), channel_id=1, source_target_pairs={{0,16},{8,24},{16,32},{24,40},{32,48},{40,56},{48,64},{56,72},{64,... | collective-permute-start | bytes 589832 | tf_op jit(solution)/shard_map/ppermute | solution.py:53
  104.7 2.8 %collective-permute-start.12 = (bf16[192,512]{1,0:T(8,128)(2,1)S(1)}, bf16[192,512]{1,0:T(8,128)(2,1)S(1)}, u32[]{:S(2)}, u32[]{:S(2)}) collective-permute-start(bf16[192,512]{1,0:T(8,128)(2,1)S(1)} %bitcast.22), channel_id=1, source_target_pairs={{0,240},{8,248},{16,0},{24,8},{32,16},{40,24},{48,32},{56,40},{64,... | collective-permute-start | bytes 589832 | tf_op jit(solution)/shard_map/ppermute | solution.py:53
  107.6 3.0 %collective-permute-start.6 = (bf16[256,512]{1,0:T(8,128)(2,1)S(1)}, bf16[256,512]{1,0:T(8,128)(2,1)S(1)}, u32[]{:S(2)}, u32[]{:S(2)}) collective-permute-start(bf16[256,512]{1,0:T(8,128)(2,1)S(1)} %maximum_select_fusion), channel_id=1, source_target_pairs={{0,16},{16,32},{32,48},{48,64},{64,80},{80,96},{96,112},{112,128},... | collective-permute-start | bytes 786440 | tf_op jit(solution)/shard_map/ppermute | solution.py:44
  110.7 2.2 %collective-permute-start.13 = (bf16[192,512]{1,0:T(8,128)(2,1)S(1)}, bf16[192,512]{1,0:T(8,128)(2,1)S(1)}, u32[]{:S(2)}, u32[]{:S(2)}) collective-permute-start(bf16[192,512]{1,0:T(8,128)(2,1)S(1)} %bitcast.23), channel_id=1, source_target_pairs={{0,224},{8,40},{16,240},{24,56},{32,0},{40,72},{48,16},{56,88},{64... | collective-permute-start | bytes 589832 | tf_op jit(solution)/shard_map/ppermute | solution.py:53
  113.0 7.9 %collective-permute-done.13 = bf16[192,512]{1,0:T(8,128)(2,1)S(1)} collective-permute-done((bf16[192,512]{1,0:T(8,128)(2,1)S(1)}, bf16[192,512]{1,0:T(8,128)(2,1)S(1)}, u32[]{:S(2)}, u32[]{:S(2)}) %collective-permute-start.13) | collective-permute-done | bytes 196640 | tf_op jit(solution)/shard_map/ppermute | solution.py:53
  120.9 1.9 %collective-permute-start.15 = (bf16[576,512]{1,0:T(8,128)(2,1)S(1)}, bf16[576,512]{1,0:T(8,128)(2,1)S(1)}, u32[]{:S(2)}, u32[]{:S(2)}) collective-permute-start(bf16[576,512]{1,0:T(8,128)(2,1)S(1)} %constant_dynamic-update-slice_fusion.refs_1_), channel_id=1, source_target_pairs={{0,8},{8,0},{1,9},{9,1},{2,10},{10,2},{3,11},{11,3},{4,12},{12,4},... | collective-permute-start | bytes 1769480 | tf_op jit(solution)/shard_map/ppermute | solution.py:39
  122.8 2.4 %collective-permute-start.7 = (bf16[256,512]{1,0:T(8,128)(2,1)S(1)}, bf16[256,512]{1,0:T(8,128)(2,1)S(1)}, u32[]{:S(2)}, u32[]{:S(2)}) collective-permute-start(bf16[256,512]{1,0:T(8,128)(2,1)S(1)} %collective-permute-done.6.refs_6_), channel_id=1, source_target_pairs={{0,8},{8,0},{1,9},{9,1},{2,10},{10,2},{3,11},{11,3},{4,12},{12,4},... | collective-permute-start | bytes 786440 | tf_op jit(solution)/shard_map/ppermute | solution.py:39
  125.3 5.1 %collective-permute-start = (bf16[192,512]{1,0:T(8,128)(2,1)S(1)}, bf16[192,512]{1,0:T(8,128)(2,1)S(1)}, u32[]{:S(2)}, u32[]{:S(2)}) collective-permute-start(bf16[192,512]{1,0:T(8,128)(2,1)S(1)} %copy-done.3), channel_id=1, source_target_pairs={{256,0},{272,16},{288,32},{257,1},{273,17},{289,33},{258,2},{274,1... | collective-permute-start | bytes 589832 | tf_op jit(solution)/shard_map/ppermute | solution.py:443
  130.4 4.3 %collective-permute-done.visitor_ref = bf16[192,512]{1,0:T(8,128)(2,1)S(1)} collective-permute-done((bf16[192,512]{1,0:T(8,128)(2,1)S(1)}, bf16[192,512]{1,0:T(8,128)(2,1)S(1)}, u32[]{:S(2)}, u32[]{:S(2)}) %collective-permute-start) | collective-permute-done | bytes 196640 | tf_op jit(solution)/shard_map/ppermute | solution.py:443
  134.7 2.5 %window.1 = (f32[192,512]{1,0:T(8,128)S(1)}, f32[192,128]{1,0:T(8,128)S(1)}, bf16[192,640]{1,0:T(8,128)(2,1)S(1)}) custom-call(bf16[192,512]{1,0:T(8,128)(2,1)S(1)} %copy-done.3, bf16[192,512]{1,0:T(8,128)(2,1)S(1)} %collective-permute-done.visitor_ref, bf16[400,512]{1,0:T(8,128)(2,1)S(1)} %pack.1.refs_0_.pa_ref, ...), custom_call_target="tpu_custom_call" | custom-call | tf_op jit(solution)/shard_map/window/pallas_call | solution.py:355
  138.5 2.1 %collective-permute-start.14 = (bf16[192,512]{1,0:T(8,128)(2,1)S(1)}, bf16[192,512]{1,0:T(8,128)(2,1)S(1)}, u32[]{:S(2)}, u32[]{:S(2)}) collective-permute-start(bf16[192,512]{1,0:T(8,128)(2,1)S(1)} %bitcast.24), channel_id=1, source_target_pairs={{0,8},{8,0},{1,9},{9,1},{2,10},{10,2},{3,11},{11,3},{4,12},{12,4},... | collective-permute-start | bytes 589832 | tf_op jit(solution)/shard_map/ppermute | solution.py:39
  141.3 7.7 %collective-permute-done.8.reply_ref = bf16[192,640]{1,0:T(8,128)(2,1)S(1)} collective-permute-done((bf16[192,640]{1,0:T(8,128)(2,1)S(1)}, bf16[192,640]{1,0:T(8,128)(2,1)S(1)}, u32[]{:S(2)}, u32[]{:S(2)}) %collective-permute-start.8) | collective-permute-done | bytes 245792 | tf_op jit(solution)/shard_map/ppermute | solution.py:462
  149.6 7.4 %solve.1 = (f32[192,512]{1,0:T(8,128)S(1)}, f32[8,192]{1,0:T(8,128)S(1)}) custom-call(bf16[192,512]{1,0:T(8,128)(2,1)} %q_ref.3, bf16[512,512]{1,0:T(8,128)(2,1)} %bitcast.14, bf16[512,512]{1,0:T(8,128)(2,1)} %bitcast.17, bf16[512,512]{1,0:T(8,128)(2,1)} %bitcast.18, bf16[192,512]{1,0:T(8,128)(2,1)S(1)} %bitcast.25, ...), custom_call_target="tpu_custom_call" | custom-call | tf_op jit(solution)/shard_map/solve/pallas_call | solution.py:275
  157.1 11.1 %all_to_all.15.sums_ref = f32[8,2,192]{2,1,0:T(2,128)S(1)} all-to-all(f32[8,2,192]{2,1,0:T(2,128)S(1)} %broadcast_in_dim.15), channel_id=1, replica_groups=mesh['xh'=2,'zq'=4,'zm'=2,'zl'=2,'core'=2,'head'=8] {'head'}, dimensions={0} | all-to-all | bytes 24576 | tf_op jit(solution)/shard_map/all_to_all | solution.py:57
  (47 shorter events, 14.8 us)
Async XLA Ops:
  0.6 11.0 %copy-start.4 = (bf16[1,512,512]{2,1,0:T(8,128)(2,1)S(1)}, bf16[1,512,512]{2,1,0:T(8,128)(2,1)}, u32[]{:S(2)}) copy-start(bf16[1,512,512]{2,1,0:T(8,128)(2,1)} %param.12) | copy-start | bytes 1572868
  1.8 10.1 %copy-start.5 = (bf16[1,512,512]{2,1,0:T(8,128)(2,1)S(1)}, bf16[1,512,512]{2,1,0:T(8,128)(2,1)}, u32[]{:S(2)}) copy-start(bf16[1,512,512]{2,1,0:T(8,128)(2,1)} %param.13) | copy-start | bytes 1572868
  1.8 10.3 %collective-permute-start.1 = (bf16[400,512]{1,0:T(8,128)(2,1)S(1)}, bf16[400,512]{1,0:T(8,128)(2,1)S(1)}, u32[]{:S(2)}, u32[]{:S(2)}) collective-permute-start(bf16[400,512]{1,0:T(8,128)(2,1)S(1)} %pack.1.refs_0_.pa_ref), channel_id=1, source_target_pairs={{0,8},{8,0},{1,9},{9,1},{2,10},{10,2},{3,11},{11,3},{4,12},{12,4},... | collective-permute-start | bytes 1228808 | tf_op jit(solution)/shard_map/ppermute | solution.py:39
  3.8 17.9 %collective-permute-start.9 = (bf16[400,512]{1,0:T(8,128)(2,1)S(1)}, bf16[400,512]{1,0:T(8,128)(2,1)S(1)}, u32[]{:S(2)}, u32[]{:S(2)}) collective-permute-start(bf16[400,512]{1,0:T(8,128)(2,1)S(1)} %pack.1.refs_0_.pa_ref), channel_id=1, source_target_pairs={{0,256},{256,0},{1,257},{257,1},{2,258},{258,2},{3,259},{259,3},{4... | collective-permute-start | bytes 1228808 | tf_op jit(solution)/shard_map/ppermute | solution.py:39
  11.8 13.5 %copy-start = (bf16[1,512,512]{1,2,0:T(8,128)(2,1)}, bf16[1,512,512]{1,2,0:T(8,128)(2,1)S(1)}, u32[]{:S(2)}) copy-start(bf16[1,512,512]{1,2,0:T(8,128)(2,1)S(1)} %copy.10) | copy-start | bytes 1572868
  11.8 1.4 copy-start.2
  12.1 13.3 %copy-start.1 = (bf16[1,512,512]{1,2,0:T(8,128)(2,1)}, bf16[1,512,512]{1,2,0:T(8,128)(2,1)S(1)}, u32[]{:S(2)}) copy-start(bf16[1,512,512]{1,2,0:T(8,128)(2,1)S(1)} %copy.11) | copy-start | bytes 1572868
  21.7 3.6 %collective-permute-start.10 = (bf16[400,512]{1,0:T(8,128)(2,1)S(1)}, bf16[400,512]{1,0:T(8,128)(2,1)S(1)}, u32[]{:S(2)}, u32[]{:S(2)}) collective-permute-start(bf16[400,512]{1,0:T(8,128)(2,1)S(1)} %collective-permute-done.9.pa_ref), channel_id=1, source_target_pairs={{0,8},{8,0},{1,9},{9,1},{2,10},{10,2},{3,11},{11,3},{4,12},{12,4},... | collective-permute-start | bytes 1228808 | tf_op jit(solution)/shard_map/ppermute | solution.py:39
  26.9 43.9 %all-to-all-start = ((bf16[16,24,512]{2,1,0:T(8,128)(2,1)}), bf16[16,24,512]{2,1,0:T(8,128)(2,1)S(1)}, u32[]{:S(2)}, u32[]{:S(2)}) async-start(bf16[16,24,512]{2,1,0:T(8,128)(2,1)} %bitcast.8), calls=%async_computation | async-start | bytes 786432 | tf_op jit(solution)/shard_map/all_to_all | solution.py:57
  39.5 29.4 %collective-permute-start.2 = (bf16[400,512]{1,0:T(8,128)(2,1)S(1)}, bf16[400,512]{1,0:T(8,128)(2,1)S(1)}, u32[]{:S(2)}, u32[]{:S(2)}) collective-permute-start(bf16[400,512]{1,0:T(8,128)(2,1)S(1)} %pack.1.refs_0_.pa_ref), channel_id=1, source_target_pairs={{0,16},{16,32},{32,48},{48,64},{64,80},{80,96},{96,112},{112,128},... | collective-permute-start | bytes 1228808 | tf_op jit(solution)/shard_map/ppermute | solution.py:44
  68.9 18.3 %collective-permute-start.4 = (bf16[400,512]{1,0:T(8,128)(2,1)S(1)}, bf16[400,512]{1,0:T(8,128)(2,1)S(1)}, u32[]{:S(2)}, u32[]{:S(2)}) collective-permute-start(bf16[400,512]{1,0:T(8,128)(2,1)S(1)} %collective-permute-done.2.refs_2_), channel_id=1, source_target_pairs={{0,16},{16,32},{32,48},{48,64},{64,80},{80,96},{96,112},{112,128},... | collective-permute-start | bytes 1228808 | tf_op jit(solution)/shard_map/ppermute | solution.py:44
  71.6 28.9 %all-to-all-start.1 = ((bf16[8,24,512]{2,1,0:T(8,128)(2,1)}), bf16[8,24,512]{2,1,0:T(8,128)(2,1)S(1)}, u32[]{:S(2)}, u32[]{:S(2)}) async-start(bf16[8,24,512]{2,1,0:T(8,128)(2,1)} %tally.1), calls=%async_computation.1 | async-start | bytes 393216 | tf_op jit(solution)/shard_map/all_to_all | solution.py:57
  85.3 49.4 %collective-permute-start.3 = (bf16[400,512]{1,0:T(8,128)(2,1)S(1)}, bf16[400,512]{1,0:T(8,128)(2,1)}, u32[]{:S(2)}, u32[]{:S(2)}) collective-permute-start(bf16[400,512]{1,0:T(8,128)(2,1)S(1)} %collective-permute-done.2.refs_2_), channel_id=1, source_target_pairs={{0,8},{8,0},{1,9},{9,1},{2,10},{10,2},{3,11},{11,3},{4,12},{12,4},... | collective-permute-start | bytes 1228808 | tf_op jit(solution)/shard_map/ppermute | solution.py:39
  87.3 17.5 %collective-permute-start.5 = (bf16[400,512]{1,0:T(8,128)(2,1)S(1)}, bf16[400,512]{1,0:T(8,128)(2,1)S(1)}, u32[]{:S(2)}, u32[]{:S(2)}) collective-permute-start(bf16[400,512]{1,0:T(8,128)(2,1)S(1)} %collective-permute-done.4.refs_4_), channel_id=1, source_target_pairs={{0,8},{8,0},{1,9},{9,1},{2,10},{10,2},{3,11},{11,3},{4,12},{12,4},... | collective-permute-start | bytes 1228808 | tf_op jit(solution)/shard_map/ppermute | solution.py:39
  100.5 12.5 %collective-permute-start.11 = (bf16[192,512]{1,0:T(8,128)(2,1)S(1)}, bf16[192,512]{1,0:T(8,128)(2,1)S(1)}, u32[]{:S(2)}, u32[]{:S(2)}) collective-permute-start(bf16[192,512]{1,0:T(8,128)(2,1)S(1)} %bitcast.21), channel_id=1, source_target_pairs={{0,16},{8,24},{16,32},{24,40},{32,48},{40,56},{48,64},{56,72},{64,... | collective-permute-start | bytes 589832 | tf_op jit(solution)/shard_map/ppermute | solution.py:53
  104.7 8.2 %collective-permute-start.12 = (bf16[192,512]{1,0:T(8,128)(2,1)S(1)}, bf16[192,512]{1,0:T(8,128)(2,1)S(1)}, u32[]{:S(2)}, u32[]{:S(2)}) collective-permute-start(bf16[192,512]{1,0:T(8,128)(2,1)S(1)} %bitcast.22), channel_id=1, source_target_pairs={{0,240},{8,248},{16,0},{24,8},{32,16},{40,24},{48,32},{56,40},{64,... | collective-permute-start | bytes 589832 | tf_op jit(solution)/shard_map/ppermute | solution.py:53
  107.6 15.2 %collective-permute-start.6 = (bf16[256,512]{1,0:T(8,128)(2,1)S(1)}, bf16[256,512]{1,0:T(8,128)(2,1)S(1)}, u32[]{:S(2)}, u32[]{:S(2)}) collective-permute-start(bf16[256,512]{1,0:T(8,128)(2,1)S(1)} %maximum_select_fusion), channel_id=1, source_target_pairs={{0,16},{16,32},{32,48},{48,64},{64,80},{80,96},{96,112},{112,128},... | collective-permute-start | bytes 786440 | tf_op jit(solution)/shard_map/ppermute | solution.py:44
  110.7 10.2 %collective-permute-start.13 = (bf16[192,512]{1,0:T(8,128)(2,1)S(1)}, bf16[192,512]{1,0:T(8,128)(2,1)S(1)}, u32[]{:S(2)}, u32[]{:S(2)}) collective-permute-start(bf16[192,512]{1,0:T(8,128)(2,1)S(1)} %bitcast.23), channel_id=1, source_target_pairs={{0,224},{8,40},{16,240},{24,56},{32,0},{40,72},{48,16},{56,88},{64... | collective-permute-start | bytes 589832 | tf_op jit(solution)/shard_map/ppermute | solution.py:53
  113.0 12.2 %copy-start.3 = (bf16[192,512]{1,0:T(8,128)(2,1)S(1)}, bf16[192,512]{1,0:T(8,128)(2,1)}, u32[]{:S(2)}) copy-start(bf16[192,512]{1,0:T(8,128)(2,1)} %q_ref.3) | copy-start | bytes 589828
  120.9 28.7 %collective-permute-start.15 = (bf16[576,512]{1,0:T(8,128)(2,1)S(1)}, bf16[576,512]{1,0:T(8,128)(2,1)S(1)}, u32[]{:S(2)}, u32[]{:S(2)}) collective-permute-start(bf16[576,512]{1,0:T(8,128)(2,1)S(1)} %constant_dynamic-update-slice_fusion.refs_1_), channel_id=1, source_target_pairs={{0,8},{8,0},{1,9},{9,1},{2,10},{10,2},{3,11},{11,3},{4,12},{12,4},... | collective-permute-start | bytes 1769480 | tf_op jit(solution)/shard_map/ppermute | solution.py:39
  122.8 11.9 %collective-permute-start.7 = (bf16[256,512]{1,0:T(8,128)(2,1)S(1)}, bf16[256,512]{1,0:T(8,128)(2,1)S(1)}, u32[]{:S(2)}, u32[]{:S(2)}) collective-permute-start(bf16[256,512]{1,0:T(8,128)(2,1)S(1)} %collective-permute-done.6.refs_6_), channel_id=1, source_target_pairs={{0,8},{8,0},{1,9},{9,1},{2,10},{10,2},{3,11},{11,3},{4,12},{12,4},... | collective-permute-start | bytes 786440 | tf_op jit(solution)/shard_map/ppermute | solution.py:39
  125.3 9.4 %collective-permute-start = (bf16[192,512]{1,0:T(8,128)(2,1)S(1)}, bf16[192,512]{1,0:T(8,128)(2,1)S(1)}, u32[]{:S(2)}, u32[]{:S(2)}) collective-permute-start(bf16[192,512]{1,0:T(8,128)(2,1)S(1)} %copy-done.3), channel_id=1, source_target_pairs={{256,0},{272,16},{288,32},{257,1},{273,17},{289,33},{258,2},{274,1... | collective-permute-start | bytes 589832 | tf_op jit(solution)/shard_map/ppermute | solution.py:443
  137.2 11.7 %collective-permute-start.8 = (bf16[192,640]{1,0:T(8,128)(2,1)S(1)}, bf16[192,640]{1,0:T(8,128)(2,1)S(1)}, u32[]{:S(2)}, u32[]{:S(2)}) collective-permute-start(bf16[192,640]{1,0:T(8,128)(2,1)S(1)} %get-tuple-element.13), channel_id=1, source_target_pairs={{0,256},{16,272},{32,288},{1,257},{17,273},{33,289},{2,258},{18,27... | collective-permute-start | bytes 737288 | tf_op jit(solution)/shard_map/ppermute | solution.py:462
  138.5 11.1 %collective-permute-start.14 = (bf16[192,512]{1,0:T(8,128)(2,1)S(1)}, bf16[192,512]{1,0:T(8,128)(2,1)S(1)}, u32[]{:S(2)}, u32[]{:S(2)}) collective-permute-start(bf16[192,512]{1,0:T(8,128)(2,1)S(1)} %bitcast.24), channel_id=1, source_target_pairs={{0,8},{8,0},{1,9},{9,1},{2,10},{10,2},{3,11},{11,3},{4,12},{12,4},... | collective-permute-start | bytes 589832 | tf_op jit(solution)/shard_map/ppermute | solution.py:39

commit v5 on v4

--- a/solution.py
+++ b/solution.py
@@ -233,7 +233,7 @@
 
     for which, (near_ref, far_ref) in ((core, blocks[:2]), (1 - core, blocks[2:])):
         put(near_ref, 0, which, 0)
-        for i, turn in enumerate((3, 1, 2)):
+        for i, turn in enumerate((1 + 2 * which, 3 + 2 * which, 2)):
             put(far_ref, 2 * i * BIT, which, turn)
     fresh = []
     for m in range(3):
@@ -462,8 +462,8 @@
     reply = lax.ppermute(answer, CHIPS, [(i, deep + i) for i in range(SPAN)])
     attended, attended_sq = merge(seen, stats, reply)
 
-    above = around(mine, 1, 1)
-    below = around(mine, -1, -1)
+    above = around(mine, -1, 1)
+    below = around(mine, 1, -1)
     beyond = around(mine, -2, 2)
     mine_x = swapped(mine, "core")
     held = jnp.concatenate([above, below, beyond])

time: 170 us -> 170 us (level)
  transfers between devices with their start and end apart: 18 -> 18, of which waited for: 7 -> 8; matrix products, arithmetic and copies ran while one was open for 0% -> 0% of each run, Pallas kernels for 3% -> 3%
where the time goes in v5:
time: 170 us
  starting transfers between devices  73.3 us (43%)
  waiting for transfers between devices  65.5 us (39%)
  Pallas kernels  16.1 us (9%)
  blocking collectives  11.1 us (7%)
  local copies, waits for them, and re-layouts  1.73 us (1%)
    all_to_all x2, starting transfers between devices, exchanged(): return lax.all_to_all(x, axes, 0, 0)  26.4 us
    ppermute x3, waiting for transfers between devices, forwarded(): return lax.ppermute(x, RING, [(i, (i + 1) % count) for i in range(count)])  25.6 us
    ppermute x8, starting transfers between devices, swapped(): return lax.ppermute(x, axis, [(0, 1), (1, 0)])  22.5 us
    all_to_all x1, blocking collectives, exchanged(): return lax.all_to_all(x, axes, 0, 0)  11.1 us
    all_to_all x2, waiting for transfers between devices, exchanged(): return lax.all_to_all(x, axes, 0, 0)  10.8 us
    ppermute x3, starting transfers between devices, forwarded(): return lax.ppermute(x, RING, [(i, (i + 1) % count) for i in range(count)])  9.65 us
    ppermute x8, waiting for transfers between devices, swapped(): return lax.ppermute(x, axis, [(0, 1), (1, 0)])  9.29 us
    ppermute x3, starting transfers between devices, around(): return lax.ppermute(x, RING + ('core',), pairs)  8.41 us
  transfers between devices with their start and end apart: 18, of which 8 were waited for; matrix products, arithmetic and copies ran while one was open for 0% of the time, Pallas kernels for 3%

profile of v5, /device:TPU:4, one launch (start us, length us, event | category | flops | bytes accessed | tf_op | source)
XLA Modules:
  0.0 169.5 jit_solution(5963191349881249980)
XLA Ops:
  1.8 2.1 %collective-permute-start.1 = (bf16[400,512]{1,0:T(8,128)(2,1)S(1)}, bf16[400,512]{1,0:T(8,128)(2,1)S(1)}, u32[]{:S(2)}, u32[]{:S(2)}) collective-permute-start(bf16[400,512]{1,0:T(8,128)(2,1)S(1)} %pack.1.refs_0_.pa_ref), channel_id=1, source_target_pairs={{0,8},{8,0},{1,9},{9,1},{2,10},{10,2},{3,11},{11,3},{4,12},{12,4},... | collective-permute-start | bytes 1228808 | tf_op jit(solution)/shard_map/ppermute | solution.py:39
  3.8 7.8 %collective-permute-start.9 = (bf16[400,512]{1,0:T(8,128)(2,1)S(1)}, bf16[400,512]{1,0:T(8,128)(2,1)S(1)}, u32[]{:S(2)}, u32[]{:S(2)}) collective-permute-start(bf16[400,512]{1,0:T(8,128)(2,1)S(1)} %pack.1.refs_0_.pa_ref), channel_id=1, source_target_pairs={{0,256},{256,0},{1,257},{257,1},{2,258},{258,2},{3,259},{259,3},{4... | collective-permute-start | bytes 1228808 | tf_op jit(solution)/shard_map/ppermute | solution.py:39
  14.2 7.6 %collective-permute-done.9.pa_ref = bf16[400,512]{1,0:T(8,128)(2,1)S(1)} collective-permute-done((bf16[400,512]{1,0:T(8,128)(2,1)S(1)}, bf16[400,512]{1,0:T(8,128)(2,1)S(1)}, u32[]{:S(2)}, u32[]{:S(2)}) %collective-permute-start.9) | collective-permute-done | bytes 409632 | tf_op jit(solution)/shard_map/ppermute | solution.py:39
  21.7 1.9 %collective-permute-start.10 = (bf16[400,512]{1,0:T(8,128)(2,1)S(1)}, bf16[400,512]{1,0:T(8,128)(2,1)S(1)}, u32[]{:S(2)}, u32[]{:S(2)}) collective-permute-start(bf16[400,512]{1,0:T(8,128)(2,1)S(1)} %collective-permute-done.9.pa_ref), channel_id=1, source_target_pairs={{0,8},{8,0},{1,9},{9,1},{2,10},{10,2},{3,11},{11,3},{4,12},{12,4},... | collective-permute-start | bytes 1228808 | tf_op jit(solution)/shard_map/ppermute | solution.py:39
  26.9 12.6 %all-to-all-start = ((bf16[16,24,512]{2,1,0:T(8,128)(2,1)}), bf16[16,24,512]{2,1,0:T(8,128)(2,1)S(1)}, u32[]{:S(2)}, u32[]{:S(2)}) async-start(bf16[16,24,512]{2,1,0:T(8,128)(2,1)} %bitcast.8), calls=%async_computation | async-start | bytes 786432 | tf_op jit(solution)/shard_map/all_to_all | solution.py:57
  39.5 3.8 %collective-permute-start.2 = (bf16[400,512]{1,0:T(8,128)(2,1)S(1)}, bf16[400,512]{1,0:T(8,128)(2,1)S(1)}, u32[]{:S(2)}, u32[]{:S(2)}) collective-permute-start(bf16[400,512]{1,0:T(8,128)(2,1)S(1)} %pack.1.refs_0_.pa_ref), channel_id=1, source_target_pairs={{0,16},{16,32},{32,48},{48,64},{64,80},{80,96},{96,112},{112,128},... | collective-permute-start | bytes 1228808 | tf_op jit(solution)/shard_map/ppermute | solution.py:44
  43.4 25.6 %collective-permute-done.2.refs_2_ = bf16[400,512]{1,0:T(8,128)(2,1)S(1)} collective-permute-done((bf16[400,512]{1,0:T(8,128)(2,1)S(1)}, bf16[400,512]{1,0:T(8,128)(2,1)S(1)}, u32[]{:S(2)}, u32[]{:S(2)}) %collective-permute-start.2) | collective-permute-done | bytes 409632 | tf_op jit(solution)/shard_map/ppermute | solution.py:44
  71.6 13.7 %all-to-all-start.1 = ((bf16[8,24,512]{2,1,0:T(8,128)(2,1)}), bf16[8,24,512]{2,1,0:T(8,128)(2,1)S(1)}, u32[]{:S(2)}, u32[]{:S(2)}) async-start(bf16[8,24,512]{2,1,0:T(8,128)(2,1)} %tally.1), calls=%async_computation.1 | async-start | bytes 393216 | tf_op jit(solution)/shard_map/all_to_all | solution.py:57
  85.3 1.9 %collective-permute-start.3 = (bf16[400,512]{1,0:T(8,128)(2,1)S(1)}, bf16[400,512]{1,0:T(8,128)(2,1)}, u32[]{:S(2)}, u32[]{:S(2)}) collective-permute-start(bf16[400,512]{1,0:T(8,128)(2,1)S(1)} %collective-permute-done.2.refs_2_), channel_id=1, source_target_pairs={{0,8},{8,0},{1,9},{9,1},{2,10},{10,2},{3,11},{11,3},{4,12},{12,4},... | collective-permute-start | bytes 1228808 | tf_op jit(solution)/shard_map/ppermute | solution.py:39
  87.3 2.4 %collective-permute-start.5 = (bf16[400,512]{1,0:T(8,128)(2,1)S(1)}, bf16[400,512]{1,0:T(8,128)(2,1)S(1)}, u32[]{:S(2)}, u32[]{:S(2)}) collective-permute-start(bf16[400,512]{1,0:T(8,128)(2,1)S(1)} %collective-permute-done.4.refs_4_), channel_id=1, source_target_pairs={{0,8},{8,0},{1,9},{9,1},{2,10},{10,2},{3,11},{11,3},{4,12},{12,4},... | collective-permute-start | bytes 1228808 | tf_op jit(solution)/shard_map/ppermute | solution.py:39
  89.7 10.7 %all-to-all-done.1 = bf16[8,24,512]{2,1,0:T(8,128)(2,1)S(1)} async-done(((bf16[8,24,512]{2,1,0:T(8,128)(2,1)}), bf16[8,24,512]{2,1,0:T(8,128)(2,1)S(1)}, u32[]{:S(2)}, u32[]{:S(2)}) %all-to-all-start.1) | async-done | bytes 196640 | tf_op jit(solution)/shard_map/all_to_all | solution.py:57
  102.4 4.3 %collective-permute-start.12 = (bf16[192,512]{1,0:T(8,128)(2,1)S(1)}, bf16[192,512]{1,0:T(8,128)(2,1)S(1)}, u32[]{:S(2)}, u32[]{:S(2)}) collective-permute-start(bf16[192,512]{1,0:T(8,128)(2,1)S(1)} %bitcast.22), channel_id=1, source_target_pairs={{0,16},{8,248},{16,32},{24,8},{32,48},{40,24},{48,64},{56,40},{64,... | collective-permute-start | bytes 589832 | tf_op jit(solution)/shard_map/ppermute | solution.py:53
  106.8 3.9 %collective-permute-start.6 = (bf16[256,512]{1,0:T(8,128)(2,1)S(1)}, bf16[256,512]{1,0:T(8,128)(2,1)S(1)}, u32[]{:S(2)}, u32[]{:S(2)}) collective-permute-start(bf16[256,512]{1,0:T(8,128)(2,1)S(1)} %maximum_select_fusion), channel_id=1, source_target_pairs={{0,16},{16,32},{32,48},{48,64},{64,80},{80,96},{96,112},{112,128},... | collective-permute-start | bytes 786440 | tf_op jit(solution)/shard_map/ppermute | solution.py:44
  110.7 2.2 %collective-permute-start.13 = (bf16[192,512]{1,0:T(8,128)(2,1)S(1)}, bf16[192,512]{1,0:T(8,128)(2,1)S(1)}, u32[]{:S(2)}, u32[]{:S(2)}) collective-permute-start(bf16[192,512]{1,0:T(8,128)(2,1)S(1)} %bitcast.23), channel_id=1, source_target_pairs={{0,224},{8,40},{16,240},{24,56},{32,0},{40,72},{48,16},{56,88},{64... | collective-permute-start | bytes 589832 | tf_op jit(solution)/shard_map/ppermute | solution.py:53
  114.0 6.9 %collective-permute-done.13 = bf16[192,512]{1,0:T(8,128)(2,1)S(1)} collective-permute-done((bf16[192,512]{1,0:T(8,128)(2,1)S(1)}, bf16[192,512]{1,0:T(8,128)(2,1)S(1)}, u32[]{:S(2)}, u32[]{:S(2)}) %collective-permute-start.13) | collective-permute-done | bytes 196640 | tf_op jit(solution)/shard_map/ppermute | solution.py:53
  120.9 1.9 %collective-permute-start.15 = (bf16[576,512]{1,0:T(8,128)(2,1)S(1)}, bf16[576,512]{1,0:T(8,128)(2,1)S(1)}, u32[]{:S(2)}, u32[]{:S(2)}) collective-permute-start(bf16[576,512]{1,0:T(8,128)(2,1)S(1)} %constant_dynamic-update-slice_fusion.refs_1_), channel_id=1, source_target_pairs={{0,8},{8,0},{1,9},{9,1},{2,10},{10,2},{3,11},{11,3},{4,12},{12,4},... | collective-permute-start | bytes 1769480 | tf_op jit(solution)/shard_map/ppermute | solution.py:39
  122.8 2.4 %collective-permute-start.7 = (bf16[256,512]{1,0:T(8,128)(2,1)S(1)}, bf16[256,512]{1,0:T(8,128)(2,1)S(1)}, u32[]{:S(2)}, u32[]{:S(2)}) collective-permute-start(bf16[256,512]{1,0:T(8,128)(2,1)S(1)} %collective-permute-done.6.refs_6_), channel_id=1, source_target_pairs={{0,8},{8,0},{1,9},{9,1},{2,10},{10,2},{3,11},{11,3},{4,12},{12,4},... | collective-permute-start | bytes 786440 | tf_op jit(solution)/shard_map/ppermute | solution.py:39
  125.3 5.2 %collective-permute-start = (bf16[192,512]{1,0:T(8,128)(2,1)S(1)}, bf16[192,512]{1,0:T(8,128)(2,1)S(1)}, u32[]{:S(2)}, u32[]{:S(2)}) collective-permute-start(bf16[192,512]{1,0:T(8,128)(2,1)S(1)} %copy-done.3), channel_id=1, source_target_pairs={{256,0},{272,16},{288,32},{257,1},{273,17},{289,33},{258,2},{274,1... | collective-permute-start | bytes 589832 | tf_op jit(solution)/shard_map/ppermute | solution.py:443
  130.4 4.3 %collective-permute-done.visitor_ref = bf16[192,512]{1,0:T(8,128)(2,1)S(1)} collective-permute-done((bf16[192,512]{1,0:T(8,128)(2,1)S(1)}, bf16[192,512]{1,0:T(8,128)(2,1)S(1)}, u32[]{:S(2)}, u32[]{:S(2)}) %collective-permute-start) | collective-permute-done | bytes 196640 | tf_op jit(solution)/shard_map/ppermute | solution.py:443
  134.7 2.5 %window.1 = (f32[192,512]{1,0:T(8,128)S(1)}, f32[192,128]{1,0:T(8,128)S(1)}, bf16[192,640]{1,0:T(8,128)(2,1)S(1)}) custom-call(bf16[192,512]{1,0:T(8,128)(2,1)S(1)} %copy-done.3, bf16[192,512]{1,0:T(8,128)(2,1)S(1)} %collective-permute-done.visitor_ref, bf16[400,512]{1,0:T(8,128)(2,1)S(1)} %pack.1.refs_0_.pa_ref, ...), custom_call_target="tpu_custom_call" | custom-call | tf_op jit(solution)/shard_map/window/pallas_call | solution.py:355
  138.6 2.1 %collective-permute-start.14 = (bf16[192,512]{1,0:T(8,128)(2,1)S(1)}, bf16[192,512]{1,0:T(8,128)(2,1)S(1)}, u32[]{:S(2)}, u32[]{:S(2)}) collective-permute-start(bf16[192,512]{1,0:T(8,128)(2,1)S(1)} %bitcast.24), channel_id=1, source_target_pairs={{0,8},{8,0},{1,9},{9,1},{2,10},{10,2},{3,11},{11,3},{4,12},{12,4},... | collective-permute-start | bytes 589832 | tf_op jit(solution)/shard_map/ppermute | solution.py:39
  141.3 7.7 %collective-permute-done.8.reply_ref = bf16[192,640]{1,0:T(8,128)(2,1)S(1)} collective-permute-done((bf16[192,640]{1,0:T(8,128)(2,1)S(1)}, bf16[192,640]{1,0:T(8,128)(2,1)S(1)}, u32[]{:S(2)}, u32[]{:S(2)}) %collective-permute-start.8) | collective-permute-done | bytes 245792 | tf_op jit(solution)/shard_map/ppermute | solution.py:462
  149.7 7.4 %solve.1 = (f32[192,512]{1,0:T(8,128)S(1)}, f32[8,192]{1,0:T(8,128)S(1)}) custom-call(bf16[192,512]{1,0:T(8,128)(2,1)} %q_ref.3, bf16[512,512]{1,0:T(8,128)(2,1)} %bitcast.14, bf16[512,512]{1,0:T(8,128)(2,1)} %bitcast.17, bf16[512,512]{1,0:T(8,128)(2,1)} %bitcast.18, bf16[192,512]{1,0:T(8,128)(2,1)S(1)} %bitcast.25, ...), custom_call_target="tpu_custom_call" | custom-call | tf_op jit(solution)/shard_map/solve/pallas_call | solution.py:275
  157.2 11.1 %all_to_all.15.sums_ref = f32[8,2,192]{2,1,0:T(2,128)S(1)} all-to-all(f32[8,2,192]{2,1,0:T(2,128)S(1)} %broadcast_in_dim.15), channel_id=1, replica_groups=mesh['xh'=2,'zq'=4,'zm'=2,'zl'=2,'core'=2,'head'=8] {'head'}, dimensions={0} | all-to-all | bytes 24576 | tf_op jit(solution)/shard_map/all_to_all | solution.py:57
  (47 shorter events, 15.8 us)
Async XLA Ops:
  0.6 11.0 %copy-start.4 = (bf16[1,512,512]{2,1,0:T(8,128)(2,1)S(1)}, bf16[1,512,512]{2,1,0:T(8,128)(2,1)}, u32[]{:S(2)}) copy-start(bf16[1,512,512]{2,1,0:T(8,128)(2,1)} %param.12) | copy-start | bytes 1572868
  1.8 10.1 %copy-start.5 = (bf16[1,512,512]{2,1,0:T(8,128)(2,1)S(1)}, bf16[1,512,512]{2,1,0:T(8,128)(2,1)}, u32[]{:S(2)}) copy-start(bf16[1,512,512]{2,1,0:T(8,128)(2,1)} %param.13) | copy-start | bytes 1572868
  1.8 10.3 %collective-permute-start.1 = (bf16[400,512]{1,0:T(8,128)(2,1)S(1)}, bf16[400,512]{1,0:T(8,128)(2,1)S(1)}, u32[]{:S(2)}, u32[]{:S(2)}) collective-permute-start(bf16[400,512]{1,0:T(8,128)(2,1)S(1)} %pack.1.refs_0_.pa_ref), channel_id=1, source_target_pairs={{0,8},{8,0},{1,9},{9,1},{2,10},{10,2},{3,11},{11,3},{4,12},{12,4},... | collective-permute-start | bytes 1228808 | tf_op jit(solution)/shard_map/ppermute | solution.py:39
  3.8 17.9 %collective-permute-start.9 = (bf16[400,512]{1,0:T(8,128)(2,1)S(1)}, bf16[400,512]{1,0:T(8,128)(2,1)S(1)}, u32[]{:S(2)}, u32[]{:S(2)}) collective-permute-start(bf16[400,512]{1,0:T(8,128)(2,1)S(1)} %pack.1.refs_0_.pa_ref), channel_id=1, source_target_pairs={{0,256},{256,0},{1,257},{257,1},{2,258},{258,2},{3,259},{259,3},{4... | collective-permute-start | bytes 1228808 | tf_op jit(solution)/shard_map/ppermute | solution.py:39
  11.8 13.5 %copy-start = (bf16[1,512,512]{1,2,0:T(8,128)(2,1)}, bf16[1,512,512]{1,2,0:T(8,128)(2,1)S(1)}, u32[]{:S(2)}) copy-start(bf16[1,512,512]{1,2,0:T(8,128)(2,1)S(1)} %copy.10) | copy-start | bytes 1572868
  11.8 1.4 copy-start.2
  12.1 13.3 %copy-start.1 = (bf16[1,512,512]{1,2,0:T(8,128)(2,1)}, bf16[1,512,512]{1,2,0:T(8,128)(2,1)S(1)}, u32[]{:S(2)}) copy-start(bf16[1,512,512]{1,2,0:T(8,128)(2,1)S(1)} %copy.11) | copy-start | bytes 1572868
  21.7 3.6 %collective-permute-start.10 = (bf16[400,512]{1,0:T(8,128)(2,1)S(1)}, bf16[400,512]{1,0:T(8,128)(2,1)S(1)}, u32[]{:S(2)}, u32[]{:S(2)}) collective-permute-start(bf16[400,512]{1,0:T(8,128)(2,1)S(1)} %collective-permute-done.9.pa_ref), channel_id=1, source_target_pairs={{0,8},{8,0},{1,9},{9,1},{2,10},{10,2},{3,11},{11,3},{4,12},{12,4},... | collective-permute-start | bytes 1228808 | tf_op jit(solution)/shard_map/ppermute | solution.py:39
  26.9 43.9 %all-to-all-start = ((bf16[16,24,512]{2,1,0:T(8,128)(2,1)}), bf16[16,24,512]{2,1,0:T(8,128)(2,1)S(1)}, u32[]{:S(2)}, u32[]{:S(2)}) async-start(bf16[16,24,512]{2,1,0:T(8,128)(2,1)} %bitcast.8), calls=%async_computation | async-start | bytes 786432 | tf_op jit(solution)/shard_map/all_to_all | solution.py:57
  39.5 29.4 %collective-permute-start.2 = (bf16[400,512]{1,0:T(8,128)(2,1)S(1)}, bf16[400,512]{1,0:T(8,128)(2,1)S(1)}, u32[]{:S(2)}, u32[]{:S(2)}) collective-permute-start(bf16[400,512]{1,0:T(8,128)(2,1)S(1)} %pack.1.refs_0_.pa_ref), channel_id=1, source_target_pairs={{0,16},{16,32},{32,48},{48,64},{64,80},{80,96},{96,112},{112,128},... | collective-permute-start | bytes 1228808 | tf_op jit(solution)/shard_map/ppermute | solution.py:44
  68.9 18.3 %collective-permute-start.4 = (bf16[400,512]{1,0:T(8,128)(2,1)S(1)}, bf16[400,512]{1,0:T(8,128)(2,1)S(1)}, u32[]{:S(2)}, u32[]{:S(2)}) collective-permute-start(bf16[400,512]{1,0:T(8,128)(2,1)S(1)} %collective-permute-done.2.refs_2_), channel_id=1, source_target_pairs={{0,16},{16,32},{32,48},{48,64},{64,80},{80,96},{96,112},{112,128},... | collective-permute-start | bytes 1228808 | tf_op jit(solution)/shard_map/ppermute | solution.py:44
  71.6 28.9 %all-to-all-start.1 = ((bf16[8,24,512]{2,1,0:T(8,128)(2,1)}), bf16[8,24,512]{2,1,0:T(8,128)(2,1)S(1)}, u32[]{:S(2)}, u32[]{:S(2)}) async-start(bf16[8,24,512]{2,1,0:T(8,128)(2,1)} %tally.1), calls=%async_computation.1 | async-start | bytes 393216 | tf_op jit(solution)/shard_map/all_to_all | solution.py:57
  85.3 49.4 %collective-permute-start.3 = (bf16[400,512]{1,0:T(8,128)(2,1)S(1)}, bf16[400,512]{1,0:T(8,128)(2,1)}, u32[]{:S(2)}, u32[]{:S(2)}) collective-permute-start(bf16[400,512]{1,0:T(8,128)(2,1)S(1)} %collective-permute-done.2.refs_2_), channel_id=1, source_target_pairs={{0,8},{8,0},{1,9},{9,1},{2,10},{10,2},{3,11},{11,3},{4,12},{12,4},... | collective-permute-start | bytes 1228808 | tf_op jit(solution)/shard_map/ppermute | solution.py:39
  87.3 15.1 %collective-permute-start.5 = (bf16[400,512]{1,0:T(8,128)(2,1)S(1)}, bf16[400,512]{1,0:T(8,128)(2,1)S(1)}, u32[]{:S(2)}, u32[]{:S(2)}) collective-permute-start(bf16[400,512]{1,0:T(8,128)(2,1)S(1)} %collective-permute-done.4.refs_4_), channel_id=1, source_target_pairs={{0,8},{8,0},{1,9},{9,1},{2,10},{10,2},{3,11},{11,3},{4,12},{12,4},... | collective-permute-start | bytes 1228808 | tf_op jit(solution)/shard_map/ppermute | solution.py:39
  100.5 12.5 %collective-permute-start.11 = (bf16[192,512]{1,0:T(8,128)(2,1)S(1)}, bf16[192,512]{1,0:T(8,128)(2,1)S(1)}, u32[]{:S(2)}, u32[]{:S(2)}) collective-permute-start(bf16[192,512]{1,0:T(8,128)(2,1)S(1)} %bitcast.21), channel_id=1, source_target_pairs={{0,240},{8,24},{16,0},{24,40},{32,16},{40,56},{48,32},{56,72},{64,... | collective-permute-start | bytes 589832 | tf_op jit(solution)/shard_map/ppermute | solution.py:53
  102.4 11.6 %collective-permute-start.12 = (bf16[192,512]{1,0:T(8,128)(2,1)S(1)}, bf16[192,512]{1,0:T(8,128)(2,1)S(1)}, u32[]{:S(2)}, u32[]{:S(2)}) collective-permute-start(bf16[192,512]{1,0:T(8,128)(2,1)S(1)} %bitcast.22), channel_id=1, source_target_pairs={{0,16},{8,248},{16,32},{24,8},{32,48},{40,24},{48,64},{56,40},{64,... | collective-permute-start | bytes 589832 | tf_op jit(solution)/shard_map/ppermute | solution.py:53
  106.8 16.1 %collective-permute-start.6 = (bf16[256,512]{1,0:T(8,128)(2,1)S(1)}, bf16[256,512]{1,0:T(8,128)(2,1)S(1)}, u32[]{:S(2)}, u32[]{:S(2)}) collective-permute-start(bf16[256,512]{1,0:T(8,128)(2,1)S(1)} %maximum_select_fusion), channel_id=1, source_target_pairs={{0,16},{16,32},{32,48},{48,64},{64,80},{80,96},{96,112},{112,128},... | collective-permute-start | bytes 786440 | tf_op jit(solution)/shard_map/ppermute | solution.py:44
  110.7 10.2 %collective-permute-start.13 = (bf16[192,512]{1,0:T(8,128)(2,1)S(1)}, bf16[192,512]{1,0:T(8,128)(2,1)S(1)}, u32[]{:S(2)}, u32[]{:S(2)}) collective-permute-start(bf16[192,512]{1,0:T(8,128)(2,1)S(1)} %bitcast.23), channel_id=1, source_target_pairs={{0,224},{8,40},{16,240},{24,56},{32,0},{40,72},{48,16},{56,88},{64... | collective-permute-start | bytes 589832 | tf_op jit(solution)/shard_map/ppermute | solution.py:53
  114.0 11.3 %copy-start.3 = (bf16[192,512]{1,0:T(8,128)(2,1)S(1)}, bf16[192,512]{1,0:T(8,128)(2,1)}, u32[]{:S(2)}) copy-start(bf16[192,512]{1,0:T(8,128)(2,1)} %q_ref.3) | copy-start | bytes 589828
  120.9 28.8 %collective-permute-start.15 = (bf16[576,512]{1,0:T(8,128)(2,1)S(1)}, bf16[576,512]{1,0:T(8,128)(2,1)S(1)}, u32[]{:S(2)}, u32[]{:S(2)}) collective-permute-start(bf16[576,512]{1,0:T(8,128)(2,1)S(1)} %constant_dynamic-update-slice_fusion.refs_1_), channel_id=1, source_target_pairs={{0,8},{8,0},{1,9},{9,1},{2,10},{10,2},{3,11},{11,3},{4,12},{12,4},... | collective-permute-start | bytes 1769480 | tf_op jit(solution)/shard_map/ppermute | solution.py:39
  122.8 11.9 %collective-permute-start.7 = (bf16[256,512]{1,0:T(8,128)(2,1)S(1)}, bf16[256,512]{1,0:T(8,128)(2,1)S(1)}, u32[]{:S(2)}, u32[]{:S(2)}) collective-permute-start(bf16[256,512]{1,0:T(8,128)(2,1)S(1)} %collective-permute-done.6.refs_6_), channel_id=1, source_target_pairs={{0,8},{8,0},{1,9},{9,1},{2,10},{10,2},{3,11},{11,3},{4,12},{12,4},... | collective-permute-start | bytes 786440 | tf_op jit(solution)/shard_map/ppermute | solution.py:39
  125.3 9.5 %collective-permute-start = (bf16[192,512]{1,0:T(8,128)(2,1)S(1)}, bf16[192,512]{1,0:T(8,128)(2,1)S(1)}, u32[]{:S(2)}, u32[]{:S(2)}) collective-permute-start(bf16[192,512]{1,0:T(8,128)(2,1)S(1)} %copy-done.3), channel_id=1, source_target_pairs={{256,0},{272,16},{288,32},{257,1},{273,17},{289,33},{258,2},{274,1... | collective-permute-start | bytes 589832 | tf_op jit(solution)/shard_map/ppermute | solution.py:443
  137.3 11.7 %collective-permute-start.8 = (bf16[192,640]{1,0:T(8,128)(2,1)S(1)}, bf16[192,640]{1,0:T(8,128)(2,1)S(1)}, u32[]{:S(2)}, u32[]{:S(2)}) collective-permute-start(bf16[192,640]{1,0:T(8,128)(2,1)S(1)} %get-tuple-element.13), channel_id=1, source_target_pairs={{0,256},{16,272},{32,288},{1,257},{17,273},{33,289},{2,258},{18,27... | collective-permute-start | bytes 737288 | tf_op jit(solution)/shard_map/ppermute | solution.py:462
  138.6 11.1 %collective-permute-start.14 = (bf16[192,512]{1,0:T(8,128)(2,1)S(1)}, bf16[192,512]{1,0:T(8,128)(2,1)S(1)}, u32[]{:S(2)}, u32[]{:S(2)}) collective-permute-start(bf16[192,512]{1,0:T(8,128)(2,1)S(1)} %bitcast.24), channel_id=1, source_target_pairs={{0,8},{8,0},{1,9},{9,1},{2,10},{10,2},{3,11},{11,3},{4,12},{12,4},... | collective-permute-start | bytes 589832 | tf_op jit(solution)/shard_map/ppermute | solution.py:39
